TPU v7x, 32 devices: a whole 2x2x4 slice. The times are simulated.
32 devices in a mesh: groups: 2 (over y), blk: 4 (over z), heads: 4 (over x, core).
Axes of the slice: x: 2, y: 2, z: 4, core: 2. Of those that a mesh axis runs over, the one named last changes fastest.
Arguments:
- cand_feat: bfloat16 [256, 2048], P(('groups', 'blk')), parts along dimension 0, may hold values from -6 to 6
- cand_counts: int32 [4], P('groups'), parts along dimension 0, may hold values from 1 to 102, 128 in all
- proj_weight: bfloat16 [2, 2048, 2048], P(None, None, 'heads'), may hold values from -0.125 to 0.125
- norm_gain: bfloat16 [2048], P('heads'), may hold values from 0.25 to 1.75
- hist_kv: bfloat16 [2, 16384, 2048], P(None, ('groups', 'blk'), 'heads'), parts along dimension 1, may hold values from -6 to 6
- hist_lens: int32 [4], P('groups'), parts along dimension 0, may hold values from 1 to 6144, 8192 in all
- hist_mask: int32 [16384], P(('groups', 'blk')), parts along dimension 0, may hold values 0 or 1
- out_cot: bfloat16 [256, 2048], P(('groups', 'blk'), 'heads'), parts along dimension 0, may hold values from -6 to 6
- owner: int32 [256, 1], P(('groups', 'blk')), parts along dimension 0, may hold values from 0 to 3; in each aligned block of 32 rows (0 to 31, 32 to 63, ...) at most 24 rows name the same one
- item_row: int32 [256], P(('groups', 'blk')), parts along dimension 0, may hold values from 0 to 47
Outputs:
- attended: bfloat16 [256, 2048], P(('groups', 'blk'), 'heads'), parts along dimension 0
- item_grad: float32 [384, 2048], P(('groups', 'blk'), 'heads'), parts along dimension 0
There are 2 independent parts, one for each index of `groups`. A program takes and returns all parts, laid end to end along the dimension named above; an argument that names none is the same for every part. Nothing has to cross between parts.
Inputs may be any that keep to these rules, and one draw needn't show every extreme that they name: `cand_counts`: the counts sum to 128; candidates are laid out user after user. `hist_lens`: the lengths sum to 8192; events are laid out user after user. Among the candidates of one device, at most 24 name the same owner.
All inputs are finite; a program needn't handle non-finite values. No bound on the sum of `hist_mask` on one device may be relied on, other than what follows from the above.
Results may differ from a plain program's by a relative error of at most 0.006.
Values may be sent and summed in bfloat16 or wider, within the bound.
No kernel may reach another device: no remote copies, remote signals or barrier semaphores. Data moves between devices by JAX's collectives and lax.ppermute only.
A program may use at most 64 MiB of HBM per device.

v0:
```python
import jax
import jax.numpy as jnp
from jax import lax
from jax.sharding import PartitionSpec as P

HD = 128
ITEMS_DEV = 48


NORM_EPS = 1e-05


def silu_grad(values):
    sigmoid = jax.nn.sigmoid(values)
    return sigmoid * (1.0 + values * (1.0 - sigmoid))


def segment_user(counts, positions):
    segment_ends = jnp.cumsum(counts)
    return jnp.sum((positions[:, None] >= segment_ends[None, :]).astype(jnp.int32), axis=1)


def body(
    cand_feat,
    cand_counts,
    proj_weight,
    norm_gain,
    hist_kv,
    hist_lens,
    hist_mask,
    out_cot,
    owner,
    item_row,
):
    cand_rows = cand_feat.shape[0]
    shard_count = lax.axis_size("blk")
    cand_total = cand_rows * shard_count
    hist_rows = hist_kv.shape[1]
    feat_width = hist_kv.shape[2]
    heads_here = feat_width // HD
    score_scale = HD ** (-0.5)
    block_width = min(512, hist_rows)
    block_count = hist_rows // block_width
    query_pre = jnp.dot(cand_feat, proj_weight[0], preferred_element_type=jnp.float32)
    up_pre = jnp.dot(cand_feat, proj_weight[1], preferred_element_type=jnp.float32)
    queries = jax.nn.silu(query_pre).astype(jnp.bfloat16)
    gate_act = jax.nn.silu(up_pre).reshape(cand_rows, heads_here, HD)
    shard_index = lax.axis_index("blk")
    key_pos = shard_index * hist_rows + jnp.arange(hist_rows, dtype=jnp.int32)
    key_user = segment_user(hist_lens, key_pos).reshape(block_count, block_width)
    key_live = (hist_mask > 0).reshape(block_count, block_width)
    key_blocks = hist_kv[0].reshape(block_count, block_width, heads_here, HD)
    value_blocks = hist_kv[1].reshape(block_count, block_width, heads_here, HD)
    cand_user = segment_user(cand_counts, jnp.arange(cand_total, dtype=jnp.int32))

    def keep_weights(user_rows, user_block, live_block):
        return ((user_rows[:, None] == user_block[None, :]) & live_block[None, :]).astype(
            jnp.float32
        )

    def local_scores(query_rows, key_block):
        return (
            jnp.einsum("chd,khd->hck", query_rows, key_block, preferred_element_type=jnp.float32)
            * score_scale
        )

    gathered_q = lax.all_gather(queries, "blk", axis=0, tiled=True)
    query_rows = gathered_q.reshape(lax.axis_size("blk") * cand_rows, heads_here, HD)
    user_rows = cand_user

    def forward_advance(running, blocks_in):
        key_block, value_block, user_block, live_block = blocks_in
        scores = local_scores(query_rows, key_block)
        attention = (
            jax.nn.silu(scores) * keep_weights(user_rows, user_block, live_block)[None]
        ).astype(jnp.bfloat16)
        return (
            running
            + jnp.einsum(
                "hck,khd->chd", attention, value_block, preferred_element_type=jnp.float32
            ),
            None,
        )

    start_sum = jnp.zeros((lax.axis_size("blk") * cand_rows, heads_here, HD), jnp.float32)
    running = lax.scan(forward_advance, start_sum, (key_blocks, value_blocks, key_user, key_live))[
        0
    ]
    attended_sum = lax.psum_scatter(
        running.reshape(lax.axis_size("blk") * cand_rows, feat_width),
        "blk",
        scatter_dimension=0,
        tiled=True,
    ).reshape(cand_rows, heads_here, HD)
    mean_square = jnp.mean(attended_sum * attended_sum, axis=-1, keepdims=True)
    inv_rms = lax.rsqrt(mean_square + NORM_EPS)
    normed = attended_sum * inv_rms
    gain_heads = norm_gain.astype(jnp.float32).reshape(heads_here, HD)
    attended = (normed * gain_heads * gate_act).reshape(cand_rows, feat_width).astype(jnp.bfloat16)
    cot_heads = out_cot.astype(jnp.float32).reshape(cand_rows, heads_here, HD)
    gate_grad = cot_heads * normed * gain_heads
    up_grad = (gate_grad.reshape(cand_rows, feat_width) * silu_grad(up_pre)).astype(jnp.bfloat16)
    normed_grad = cot_heads * gate_act * gain_heads
    av_grad = (
        inv_rms * (normed_grad - normed * jnp.mean(normed_grad * normed, axis=-1, keepdims=True))
    ).astype(jnp.bfloat16)
    gathered_grad = lax.all_gather(
        av_grad.reshape(cand_rows, feat_width), "blk", axis=0, tiled=True
    )
    row_count = lax.axis_size("blk") * cand_rows
    backward_query_rows = gathered_q.reshape(row_count, heads_here, HD)
    grad_rows = gathered_grad.reshape(row_count, heads_here, HD)

    def backward_advance(running, blocks_in):
        key_block, value_block, user_block, live_block = blocks_in
        scores = local_scores(backward_query_rows, key_block)
        along = jnp.einsum(
            "chd,khd->hck", grad_rows, value_block, preferred_element_type=jnp.float32
        )
        score_grad = (
            silu_grad(scores) * keep_weights(cand_user, user_block, live_block)[None] * along
        ).astype(jnp.bfloat16)
        return (
            running
            + jnp.einsum("hck,khd->chd", score_grad, key_block, preferred_element_type=jnp.float32),
            None,
        )

    start_sum = jnp.zeros((row_count, heads_here, HD), jnp.float32)
    running = lax.scan(backward_advance, start_sum, (key_blocks, value_blocks, key_user, key_live))[
        0
    ]
    query_grad = (
        lax.psum_scatter(
            running.reshape(row_count, feat_width), "blk", scatter_dimension=0, tiled=True
        )
        * score_scale
    )
    query_pre_grad = (query_grad * silu_grad(query_pre)).astype(jnp.bfloat16)
    partial_grad = jnp.einsum(
        "cf,df->cd", query_pre_grad, proj_weight[0], preferred_element_type=jnp.float32
    ) + jnp.einsum("cf,df->cd", up_grad, proj_weight[1], preferred_element_type=jnp.float32)
    feature_grad = lax.psum_scatter(partial_grad, "heads", scatter_dimension=1, tiled=True)
    owner_id = owner[:, 0]
    table_size = ITEMS_DEV * shard_count
    table_row = owner_id * ITEMS_DEV + item_row
    one_hot = (jnp.arange(table_size, dtype=jnp.int32)[:, None] == table_row[None, :]).astype(
        jnp.float32
    )
    table_terms = jnp.dot(one_hot, feature_grad, precision=lax.Precision.HIGHEST)
    item_grad = lax.psum_scatter(table_terms, "blk", scatter_dimension=0, tiled=True)
    return (attended, item_grad)


def solution(mesh):
    return jax.shard_map(
        body,
        mesh=mesh,
        in_specs=(
            P(("groups", "blk"), None),
            P("groups"),
            P(None, None, "heads"),
            P("heads"),
            P(None, ("groups", "blk"), "heads"),
            P("groups"),
            P(("groups", "blk")),
            P(("groups", "blk"), "heads"),
            P(("groups", "blk"), None),
            P(("groups", "blk")),
        ),
        out_specs=(P(("groups", "blk"), "heads"), P(("groups", "blk"), "heads")),
        check_vma=False,
    )
```

profile of v0, /device:TPU:0, one launch (start us, length us, event | category | flops | bytes accessed | tf_op | source)
XLA Modules:
  0.0 187.0 jit_solution(1513407749887231478)
XLA Ops:
  7.2 4.4 %fusion.68 = (bf16[1,2048,512]{2,1,0:T(8,128)(2,1)}, bf16[1,2048,512]{2,1,0:T(8,128)(2,1)}) fusion(bf16[2,2048,512]{2,1,0:T(8,128)(2,1)} %param.18), kind=kLoop, calls=%fused_computation.101 | loop fusion | bytes 8388608 | tf_op jit(solution)/shard_map/slice | solution.py:52
  11.7 2.5 %reshape_squeeze.7 = bf16[4,512,4,128]{3,2,1,0:T(4,128)(2,1)S(1)} reshape(bf16[1,2048,512]{2,1,0:T(8,128)(2,1)} %get-tuple-element.252) | data formatting | bytes 4194304 | tf_op jit(solution)/shard_map/reshape;squeeze | solution.py:52
  15.9 2.5 %reshape_squeeze.6 = bf16[4,512,4,128]{3,2,1,0:T(4,128)(2,1)S(1)} reshape(bf16[1,2048,512]{2,1,0:T(8,128)(2,1)} %get-tuple-element.253) | data formatting | bytes 4194304 | tf_op jit(solution)/shard_map/reshape;squeeze | solution.py:53
  18.5 2.7 %multiply_convert_fusion.3 = (bf16[32,512]{1,0:T(8,128)(2,1)S(1)}, f32[32,512]{1,0:T(8,128)}) fusion(bf16[32,2048]{1,0:T(8,128)(2,1)S(1)} %copy-done, bf16[2,2048,512]{2,1,0:T(8,128)(2,1)} %param.16), kind=kOutput, calls=%fused_computation.81 | convolution fusion | flops 67190784 | bytes 2326528 | tf_op jit(solution)/shard_map/dot_general | solution.py:44
  21.2 15.1 %all_gather.6 = bf16[128,512]{1,0:T(8,128)(2,1)S(1)} all-gather(bf16[32,512]{1,0:T(8,128)(2,1)S(1)} %get-tuple-element.258), channel_id=1, replica_groups=mesh['groups'=2,'blk'=4,'heads'=4] {'blk'}, dimensions={0}, use_global_device_ids=true | all-gather | bytes 163840 | tf_op jit(solution)/shard_map/all_gather | solution.py:67
  37.6 13.1 %while.22 = (s32[]{:T(128)}, f32[128,4,128]{0,2,1:T(8,128)}, bf16[4,512,4,128]{3,2,1,0:T(4,128)(2,1)S(1)}, bf16[4,512,4,128]{3,1,2,0:T(8,128)(2,1)}, bf16[128,4,...) while((s32[]{:T(128)}, f32[128,4,128]{0,2,1:T(8,128)}, ...), condition=%wide.region_5.6_spmd.clone, body=%wide.region_4.5_spmd.clone.sunk | while | flops 136380416 | bytes 4334203 | solution.py:86
  38.3 2.4 %fusion.90 = f32[128,4,128]{0,2,1:T(8,128)} fusion(bf16[128,4,128]{2,0,1:T(8,128)(2,1)} %get-tuple-element.390, bf16[1,512,4,128]{1,3,2,0:T(8,128)(2,1)S(1)} %copy.81, f32[128,512]{0,1:T(8,128)S(1)} %and_convert_fusion.4, bf16[4,512,4,128]{3,1,2,0:T(8,128)(2,1)} %get-tuple-element.389, s32[]{:T(128)} %get-tuple-element.376, ...), kind=kOutput, calls=%fused_computation.3.clone.1 | convolution fusion | flops 136183808 | bytes 1966593 | tf_op jit(solution)/shard_map/while/body/eval_jaxpr/hck,khd->chd/dot_general | solution.py:79
  41.5 2.5 %fusion.90 = f32[128,4,128]{0,2,1:T(8,128)} fusion(bf16[128,4,128]{2,0,1:T(8,128)(2,1)} %get-tuple-element.390, bf16[1,512,4,128]{1,3,2,0:T(8,128)(2,1)S(1)} %copy.81, f32[128,512]{0,1:T(8,128)S(1)} %and_convert_fusion.4, bf16[4,512,4,128]{3,1,2,0:T(8,128)(2,1)} %get-tuple-element.389, s32[]{:T(128)} %get-tuple-element.376, ...), kind=kOutput, calls=%fused_computation.3.clone.1 | convolution fusion | flops 136183808 | bytes 1966593 | tf_op jit(solution)/shard_map/while/body/eval_jaxpr/hck,khd->chd/dot_general | solution.py:79
  44.8 2.5 %fusion.90 = f32[128,4,128]{0,2,1:T(8,128)} fusion(bf16[128,4,128]{2,0,1:T(8,128)(2,1)} %get-tuple-element.390, bf16[1,512,4,128]{1,3,2,0:T(8,128)(2,1)S(1)} %copy.81, f32[128,512]{0,1:T(8,128)S(1)} %and_convert_fusion.4, bf16[4,512,4,128]{3,1,2,0:T(8,128)(2,1)} %get-tuple-element.389, s32[]{:T(128)} %get-tuple-element.376, ...), kind=kOutput, calls=%fused_computation.3.clone.1 | convolution fusion | flops 136183808 | bytes 1966593 | tf_op jit(solution)/shard_map/while/body/eval_jaxpr/hck,khd->chd/dot_general | solution.py:79
  48.1 2.5 %fusion.90 = f32[128,4,128]{0,2,1:T(8,128)} fusion(bf16[128,4,128]{2,0,1:T(8,128)(2,1)} %get-tuple-element.390, bf16[1,512,4,128]{1,3,2,0:T(8,128)(2,1)S(1)} %copy.81, f32[128,512]{0,1:T(8,128)S(1)} %and_convert_fusion.4, bf16[4,512,4,128]{3,1,2,0:T(8,128)(2,1)} %get-tuple-element.389, s32[]{:T(128)} %get-tuple-element.376, ...), kind=kOutput, calls=%fused_computation.3.clone.1 | convolution fusion | flops 136183808 | bytes 1966593 | tf_op jit(solution)/shard_map/while/body/eval_jaxpr/hck,khd->chd/dot_general | solution.py:79
  52.5 2.1 %convert_multiply_fusion.1 = (f32[32,512]{1,0:T(8,128)S(1)}, f32[32,512]{1,0:T(8,128)S(1)}) fusion(bf16[32,512]{1,0:T(8,128)(2,1)} %param.21, bf16[32,2048]{1,0:T(8,128)(2,1)S(1)} %copy-done, bf16[2,2048,512]{2,1,0:T(8,128)(2,1)} %param.16), kind=kOutput, calls=%fused_computation.66 | convolution fusion | flops 67207168 | bytes 2392064 | tf_op jit(solution)/shard_map/dot_general | solution.py:45
  54.7 19.3 %reduce-scatter.5.cloned.1.call-done = f32[32,512]{1,0:T(8,128)} async-done(((f32[128,512]{1,0:T(8,128)}), f32[32,512]{1,0:T(8,128)}) %reduce-scatter.5.cloned.1.call-update) | async-done | bytes 65552 | tf_op jit(solution)/shard_map/reduce_scatter | solution.py:89
  77.5 13.3 %all_gather.7 = bf16[128,512]{1,0:T(8,128)(2,1)S(1)} all-gather(bf16[32,512]{1,0:T(8,128)(2,1)S(1)} %get-tuple-element.254), channel_id=1, replica_groups=mesh['groups'=2,'blk'=4,'heads'=4] {'blk'}, dimensions={0}, use_global_device_ids=true | all-gather | bytes 163840 | tf_op jit(solution)/shard_map/all_gather | solution.py:107
  91.5 21.3 %while.23 = (s32[]{:T(128)}, f32[128,4,128]{0,2,1:T(8,128)}, bf16[4,512,4,128]{3,1,2,0:T(8,128)(2,1)}, bf16[128,4,128]{2,0,1:T(8,128)(2,1)}, s32[128]{0:T(128)S(...) while((s32[]{:T(128)}, f32[128,4,128]{0,2,1:T(8,128)}, ...), condition=%wide.region_10.11_spmd.clone, body=%wide.region_9.10_spmd.clone.sunk | while | flops 204537856 | bytes 6038659 | solution.py:130
  94.1 2.7 %fusion.96 = f32[128,4,128]{0,2,1:T(8,128)} fusion(bf16[128,4,128]{2,0,1:T(8,128)(2,1)} %get-tuple-element.426, f32[4,128,512]{1,2,0:T(8,128)S(1)} %fusion.95, bf16[1,512,4,128]{3,2,1,0:T(4,128)(2,1)} %constant_dynamic-slice_fusion.10, f32[128,512]{0,1:T(8,128)S(1)} %and_convert_fusion.5, bf16[4,512,4,128]{3,1,2,0:T(8,128)(2,1)} %get-tuple-element.420, ...), kind=kOutput, calls=%fused_computation.25.clone.1 | convolution fusion | flops 136970240 | bytes 3015169 | tf_op jit(solution)/shard_map/while/body/eval_jaxpr/hck,khd->chd/dot_general | solution.py:125
  99.4 2.8 %fusion.96 = f32[128,4,128]{0,2,1:T(8,128)} fusion(bf16[128,4,128]{2,0,1:T(8,128)(2,1)} %get-tuple-element.426, f32[4,128,512]{1,2,0:T(8,128)S(1)} %fusion.95, bf16[1,512,4,128]{3,2,1,0:T(4,128)(2,1)} %constant_dynamic-slice_fusion.10, f32[128,512]{0,1:T(8,128)S(1)} %and_convert_fusion.5, bf16[4,512,4,128]{3,1,2,0:T(8,128)(2,1)} %get-tuple-element.420, ...), kind=kOutput, calls=%fused_computation.25.clone.1 | convolution fusion | flops 136970240 | bytes 3015169 | tf_op jit(solution)/shard_map/while/body/eval_jaxpr/hck,khd->chd/dot_general | solution.py:125
  104.7 2.8 %fusion.96 = f32[128,4,128]{0,2,1:T(8,128)} fusion(bf16[128,4,128]{2,0,1:T(8,128)(2,1)} %get-tuple-element.426, f32[4,128,512]{1,2,0:T(8,128)S(1)} %fusion.95, bf16[1,512,4,128]{3,2,1,0:T(4,128)(2,1)} %constant_dynamic-slice_fusion.10, f32[128,512]{0,1:T(8,128)S(1)} %and_convert_fusion.5, bf16[4,512,4,128]{3,1,2,0:T(8,128)(2,1)} %get-tuple-element.420, ...), kind=kOutput, calls=%fused_computation.25.clone.1 | convolution fusion | flops 136970240 | bytes 3015169 | tf_op jit(solution)/shard_map/while/body/eval_jaxpr/hck,khd->chd/dot_general | solution.py:125
  110.0 2.8 %fusion.96 = f32[128,4,128]{0,2,1:T(8,128)} fusion(bf16[128,4,128]{2,0,1:T(8,128)(2,1)} %get-tuple-element.426, f32[4,128,512]{1,2,0:T(8,128)S(1)} %fusion.95, bf16[1,512,4,128]{3,2,1,0:T(4,128)(2,1)} %constant_dynamic-slice_fusion.10, f32[128,512]{0,1:T(8,128)S(1)} %and_convert_fusion.5, bf16[4,512,4,128]{3,1,2,0:T(8,128)(2,1)} %get-tuple-element.420, ...), kind=kOutput, calls=%fused_computation.25.clone.1 | convolution fusion | flops 136970240 | bytes 3015169 | tf_op jit(solution)/shard_map/while/body/eval_jaxpr/hck,khd->chd/dot_general | solution.py:125
  114.7 18.4 %reduce-scatter.7.cloned.1.call-done = f32[32,512]{1,0:T(8,128)} async-done(((f32[128,512]{1,0:T(8,128)}), f32[32,512]{1,0:T(8,128)}) %reduce-scatter.7.cloned.1.call-update) | async-done | bytes 65552 | tf_op jit(solution)/shard_map/reduce_scatter | solution.py:134
  133.1 2.4 %fusion.41 = f32[32,2048]{1,0:T(8,128)S(1)} fusion(bf16[2,2048,512]{2,1,0:T(8,128)(2,1)} %param.16, f32[32,512]{1,0:T(8,128)} %get-tuple-element.259, f32[32,512]{1,0:T(8,128)} %reduce-scatter.7.cloned.1.call-done), kind=kOutput, calls=%fused_computation.53 | convolution fusion | flops 67272704 | bytes 2490368 | tf_op jit(solution)/shard_map/cf,df->cd/dot_general | solution.py:140
  135.5 3.0 %convolution_add_fusion = f32[32,2048]{1,0:T(8,128)} fusion(f32[32,2048]{1,0:T(8,128)S(1)} %fusion.41, bf16[2,2048,512]{2,1,0:T(8,128)(2,1)} %param.16, bf16[32,512]{1,0:T(8,128)(2,1)S(1)} %copy-done.6, f32[32,512]{1,0:T(8,128)S(1)} %copy-done.5, f32[512]{0:T(512)S(1)} %copy-done.8, f32[32,512]{1,0:T(8,128)S(1)} %copy-done.3, f32[4,8,4,128]{3,2,1,0:T(4,128)S(1)} %bitcast.137), kind=kOutput, calls=%fused_computation.49 | convolution fusion | flops 67387392 | bytes 2852864 | tf_op jit(solution)/shard_map/cf,df->cd/dot_general | solution.py:142
  138.6 18.3 %reduce-scatter.9.cloned.1.call-done = f32[32,512]{1,0:T(8,128)} async-done(((f32[32,2048]{1,0:T(8,128)}), f32[32,512]{1,0:T(8,128)}) %reduce-scatter.9.cloned.1.call-update) | async-done | bytes 65552 | tf_op jit(solution)/shard_map/reduce_scatter | solution.py:143
  157.0 1.9 %fusion.49 = f32[192,512]{1,0:T(8,128)} fusion(f32[32,512]{1,0:T(8,128)} %reduce-scatter.9.cloned.1.call-done, s32[32]{0:T(128)S(1)} %bitcast_add_fusion), kind=kOutput, calls=%fused_computation.64 | convolution fusion | flops 37754880 | bytes 458880 | tf_op jit(solution)/shard_map/dot_general | solution.py:150
  158.9 21.6 %reduce-scatter.11.cloned.1.call-done = f32[48,512]{1,0:T(8,128)} async-done(((f32[192,512]{1,0:T(8,128)}), f32[48,512]{1,0:T(8,128)}) %reduce-scatter.11.cloned.1.call-update) | async-done | bytes 98320 | tf_op jit(solution)/shard_map/reduce_scatter | solution.py:151
  (104 shorter events, 24.4 us)
Async XLA Ops:
  7.2 11.3 %copy-start = (bf16[32,2048]{1,0:T(8,128)(2,1)S(1)}, bf16[32,2048]{1,0:T(8,128)(2,1)}, u32[]{:S(2)}) copy-start(bf16[32,2048]{1,0:T(8,128)(2,1)} %param.14) | copy-start | bytes 393220
  7.2 66.8 %reduce-scatter.5.cloned.1.call-start = ((), (), s32[]{:S(2)}) async-start(), calls=%async_computation.4 | async-start | bytes 327680 | tf_op jit(solution)/shard_map/reduce_scatter | solution.py:89
  18.5 18.5 %copy-start.11 = (s32[2]{0:T(128)S(1)}, s32[2]{0:T(128)}, u32[]{:S(2)}) copy-start(s32[2]{0:T(128)} %param.19) | copy-start | bytes 28
  18.5 18.8 %copy-start.9 = (s32[2048]{0:T(1024)S(1)}, s32[2048]{0:T(1024)}, u32[]{:S(2)}) copy-start(s32[2048]{0:T(1024)} %param.20) | copy-start | bytes 24580
  18.5 18.8 %copy-start.12 = (s32[2]{0:T(128)S(1)}, s32[2]{0:T(128)}, u32[]{:S(2)}) copy-start(s32[2]{0:T(128)} %param.15) | copy-start | bytes 28
  50.6 4.0 %copy-start.10 = (bf16[512]{0:T(512)(128)(2,1)S(1)}, bf16[512]{0:T(512)(128)(2,1)}, u32[]{:S(2)}) copy-start(bf16[512]{0:T(512)(128)(2,1)} %param.17) | copy-start | bytes 3076
  52.5 80.6 %reduce-scatter.7.cloned.1.call-start = ((), (), s32[]{:S(2)}) async-start(), calls=%async_computation.5 | async-start | bytes 327680 | tf_op jit(solution)/shard_map/reduce_scatter | solution.py:134
  54.6 36.9 %copy-start.4 = (f32[32,512]{1,0:T(8,128)}, f32[32,512]{1,0:T(8,128)S(1)}, u32[]{:S(2)}) copy-start(f32[32,512]{1,0:T(8,128)S(1)} %get-tuple-element.261) | copy-start | bytes 196612
  54.7 36.8 %copy-start.7 = (f32[512]{0:T(512)}, f32[512]{0:T(512)S(1)}, u32[]{:S(2)}) copy-start(f32[512]{0:T(512)S(1)} %get-tuple-element.257) | copy-start | bytes 6148
  75.4 0.6 copy-start.1
  112.8 22.7 %copy-start.2 = (f32[32,4,128]{2,1,0:T(4,128)S(1)}, f32[32,4,128]{2,1,0:T(4,128)}, u32[]{:S(2)}) copy-start(f32[32,4,128]{2,1,0:T(4,128)} %copy-done.1) | copy-start | bytes 196612
  112.8 22.7 %copy-start.3 = (f32[32,512]{1,0:T(8,128)S(1)}, f32[32,512]{1,0:T(8,128)}, u32[]{:S(2)}) copy-start(f32[32,512]{1,0:T(8,128)} %reduce-scatter.5.cloned.1.call-done) | copy-start | bytes 196612
  112.8 22.7 %copy-start.5 = (f32[32,512]{1,0:T(8,128)S(1)}, f32[32,512]{1,0:T(8,128)}, u32[]{:S(2)}) copy-start(f32[32,512]{1,0:T(8,128)} %copy-done.4) | copy-start | bytes 196612
  112.8 22.7 %copy-start.6 = (bf16[32,512]{1,0:T(8,128)(2,1)S(1)}, bf16[32,512]{1,0:T(8,128)(2,1)}, u32[]{:S(2)}) copy-start(bf16[32,512]{1,0:T(8,128)(2,1)} %param.21) | copy-start | bytes 98308
  112.8 22.7 %copy-start.8 = (f32[512]{0:T(512)S(1)}, f32[512]{0:T(512)}, u32[]{:S(2)}) copy-start(f32[512]{0:T(512)} %copy-done.7) | copy-start | bytes 6148
  114.7 42.3 %reduce-scatter.9.cloned.1.call-start = ((), (), s32[]{:S(2)}) async-start(), calls=%async_computation.6 | async-start | bytes 327680 | tf_op jit(solution)/shard_map/reduce_scatter | solution.py:143
  135.5 3.1 %copy-start.13 = (s32[32]{0:T(128)S(1)}, s32[32]{0:T(128)}, u32[]{:S(2)}) copy-start(s32[32]{0:T(128)} %param.23) | copy-start | bytes 388
  135.5 3.1 %copy-start.14 = (s32[32,1]{0,1:T(1,128)S(1)}, s32[32,1]{0,1:T(1,128)}, u32[]{:S(2)}) copy-start(s32[32,1]{0,1:T(1,128)} %param.22) | copy-start | bytes 388
  138.6 41.9 %reduce-scatter.11.cloned.1.call-start = ((), (), s32[]{:S(2)}) async-start(), calls=%async_computation.7 | async-start | bytes 491520 | tf_op jit(solution)/shard_map/reduce_scatter | solution.py:151
Sparse Core Ops, SparseCore 0:
  52.6 21.3 reduce-scatter.4
  114.8 18.2 reduce-scatter.6
  138.7 18.2 reduce-scatter.8
  159.7 20.7 reduce-scatter.10
where the time goes:
time: 188 us; the launch traced here: 187 us
  waiting for transfers between devices  77.6 us (41%)
  matrix products  38.4 us (20%)
  blocking collectives  28.4 us (15%)
  local copies, waits for them, and re-layouts  24.2 us (13%)
  between operations  14.1 us (8%)
  other arithmetic  3.97 us (2%)
    reduce_scatter x1, waiting for transfers between devices, body(): lax.psum_scatter(table_terms, 'blk', scatter_dimension=0, tiled=True)  21.6 us
    reduce_scatter x1, waiting for transfers between devices, body(): lax.psum_scatter(running.reshape(lax.axis_size('blk') * cand_rows, feat_w...  19.3 us
    reduce_scatter x1, waiting for transfers between devices, body(): lax.psum_scatter(running.reshape(row_count, feat_width), 'blk', scatter_d...  18.4 us
    reduce_scatter x1, waiting for transfers between devices, body(): lax.psum_scatter(partial_grad, 'heads', scatter_dimension=1, tiled=True)  18.3 us
    all_gather x1, blocking collectives, body(): gathered_q = lax.all_gather(queries, 'blk', axis=0, tiled=True)  15.1 us
    all_gather x1, blocking collectives, body(): lax.all_gather(av_grad.reshape(cand_rows, feat_width), 'blk', axis=0, til...  13.3 us
    dot_general x4, matrix products, backward_advance(): jnp.einsum('hck,khd->chd', score_grad, key_block, preferred_element_type=...  10.9 us
    dot_general x4, matrix products, forward_advance(): jnp.einsum('hck,khd->chd', attention, value_block, preferred_element_type...  9.99 us
  transfers between devices with their start and end apart: 4, of which 4 were waited for; matrix products, arithmetic and copies ran while one was open for 1% of the time, Pallas kernels for 0%

commit v1 on v0

v1 whole, which is shorter than its diff:
```python
import functools

import jax
import jax.numpy as jnp
from jax import lax
from jax.experimental import pallas as pl
from jax.experimental.pallas import tpu as pltpu
from jax.sharding import PartitionSpec as P

HD = 128
ITEMS_DEV = 48
NORM_EPS = 1e-05
SCALE = HD ** (-0.5)
IDX_LANES = 128
DIRECT = 4

BF = jnp.bfloat16
F32 = jnp.float32
VMEM = pltpu.MemorySpace.VMEM
SMEM = pltpu.MemorySpace.SMEM


def silu(v):
    half = v * 0.5
    return half * jnp.tanh(half) + half


def silu_grad(v):
    half = v * 0.5
    t = jnp.tanh(half)
    return 0.5 * (1.0 + t + half * (1.0 - t * t))


def dot_nt(a, b):
    return lax.dot_general(a, b, (((1,), (1,)), ((), ())), preferred_element_type=F32)


def dot_nn(a, b):
    return lax.dot_general(a, b, (((1,), (0,)), ((), ())), preferred_element_type=F32)


def dot_tn(a, b):
    return lax.dot_general(a, b, (((0,), (0,)), ((), ())), preferred_element_type=F32)


def vmem_full(shape):
    return pl.BlockSpec(shape, lambda *_: (0,) * len(shape))


def smem_spec():
    return pl.BlockSpec(memory_space=SMEM)


def slot_order(axis):
    return lax.axis_index(axis) ^ jnp.arange(lax.axis_size(axis), dtype=jnp.int32)


def send(x, axis, m):
    return lax.ppermute(x, axis, [(j, j ^ m) for j in range(lax.axis_size(axis))])


def gather_slots(x, axis):
    n = lax.axis_size(axis)
    if n <= DIRECT:
        return [x] + [send(x, axis, m) for m in range(1, n)]
    whole = lax.all_gather(x, axis)[slot_order(axis)]
    return [whole[m] for m in range(n)]


def scatter_slots(tiles, axis):
    n = lax.axis_size(axis)
    if n <= DIRECT:
        return [tiles[0]] + [send(tiles[m], axis, m) for m in range(1, n)]
    stacked = jnp.stack([t.astype(F32) for t in tiles])[slot_order(axis)]
    return [lax.psum_scatter(stacked, axis, scatter_dimension=0, tiled=False)]


def proj_query_kernel(x_ref, w_ref, out_ref, acc_ref):
    k = pl.program_id(0)

    @pl.when(k == 0)
    def _():
        acc_ref[...] = jnp.zeros_like(acc_ref)

    acc_ref[...] += dot_nn(x_ref[...], w_ref[0])

    @pl.when(k == pl.num_programs(0) - 1)
    def _():
        out_ref[...] = acc_ref[...].astype(BF)


def proj_up_kernel(x_ref, w_ref, cot_ref, owner_ref, row_ref, pack_ref, up_ref):
    k = pl.program_id(0)
    cols = up_ref.shape[1]

    @pl.when(k == 0)
    def _():
        up_ref[...] = jnp.zeros_like(up_ref)

    up_ref[...] += dot_nn(x_ref[...], w_ref[0])

    @pl.when(k == pl.num_programs(0) - 1)
    def _():
        rows = up_ref.shape[0]
        pack_ref[:, :cols] = cot_ref[...]
        pack_ref[:, cols : 2 * cols] = up_ref[...].astype(BF)
        lane = lax.broadcasted_iota(jnp.int32, (rows, IDX_LANES), 1)
        idx = jnp.where(lane == 0, owner_ref[...], row_ref[...]).astype(F32)
        pack_ref[:, 2 * cols :] = idx.astype(BF)


def user_of(pos, counts_ref):
    user = jnp.zeros_like(pos)
    end = jnp.int32(0)
    for u in range(counts_ref.shape[0]):
        end = end + counts_ref[u]
        user = user + (pos >= end).astype(jnp.int32)
    return user


def keep_mask(slots, rows, width, first_key, me, counts_ref, lens_ref, live):
    cand = jnp.concatenate(
        [
            lax.broadcasted_iota(jnp.int32, (rows, 1), 0) + (me ^ m) * rows
            for m in range(slots)
        ],
        axis=0,
    )
    key = lax.broadcasted_iota(jnp.int32, (1, width), 1) + first_key
    key_user = jnp.where(live > 0, user_of(key, lens_ref), -1)
    return user_of(cand, counts_ref) == key_user


def forward_kernel(slots, me_ref, counts_ref, lens_ref, live_ref, *refs):
    pre_refs = refs[:slots]
    key_ref, value_ref, sum_ref, low_ref, query_ref = refs[slots:]
    k = pl.program_id(0)
    rows = pre_refs[0].shape[0]
    cols = sum_ref.shape[1]
    width = key_ref.shape[1]
    me = me_ref[0]

    @pl.when(k == 0)
    def _():
        sum_ref[...] = jnp.zeros_like(sum_ref)
        for m in range(slots):
            query_ref[m * rows : (m + 1) * rows, :] = silu(pre_refs[m][...].astype(F32)).astype(BF)

    first = (me * pl.num_programs(0) + k) * width
    keep = keep_mask(slots, rows, width, first, me, counts_ref, lens_ref, live_ref[...])
    for h in range(cols // HD):
        at = slice(h * HD, (h + 1) * HD)
        half = dot_nt(query_ref[:, at], key_ref[0, :, at]) * (0.5 * SCALE)
        att = jnp.where(keep, half * jnp.tanh(half) + half, 0.0).astype(BF)
        sum_ref[:, at] += dot_nn(att, value_ref[0, :, at])

    @pl.when(k == pl.num_programs(0) - 1)
    def _():
        low_ref[...] = sum_ref[...].astype(BF)


def slope_kernel(slots, rows, me_ref, counts_ref, lens_ref, live_ref, query_ref, key_ref, out_ref):
    k = pl.program_id(0)
    width = key_ref.shape[1]
    me = me_ref[0]
    first = (me * pl.num_programs(0) + k) * width
    keep = keep_mask(slots, rows, width, first, me, counts_ref, lens_ref, live_ref[...])
    for h in range(query_ref.shape[1] // HD):
        at = slice(h * HD, (h + 1) * HD)
        half = dot_nt(query_ref[:, at], key_ref[0, :, at]) * (0.5 * SCALE)
        t = jnp.tanh(half)
        slope = 1.0 + t + half * (1.0 - t * t)
        out_ref[h] = jnp.where(keep, slope, 0.0).astype(BF)


def backward_kernel(slots, *refs):
    me_ref, gain_ref, up_ref, sum_ref = refs[:4]
    refs = refs[4:]
    got = refs[: len(refs) - 9 - 3 * slots]
    refs = refs[len(got) :]
    pre_refs, pack_refs = refs[:slots], refs[slots : 2 * slots]
    refs = refs[2 * slots :]
    slope_ref, key_ref, value_ref, att_ref, upt_ref = refs[:5]
    tile_refs = refs[5 : 5 + slots]
    acc_ref, grad_ref, ug_ref, tot_ref = refs[5 + slots :]
    k = pl.program_id(0)
    rows, cols = up_ref.shape
    heads = cols // HD
    me = me_ref[0]

    @pl.when(k == 0)
    def _():
        acc_ref[...] = jnp.zeros_like(acc_ref)
        for s in range(slots):
            block = slice(s * rows, (s + 1) * rows)
            total = sum_ref[block, :]
            for m in range(1, len(got) + 1):
                other = s ^ m
                total = total + got[m - 1][other * rows : (other + 1) * rows, :].astype(F32)
            for h in range(heads):
                at = slice(h * HD, (h + 1) * HD)
                part = total[:, at]
                inv = lax.rsqrt(jnp.mean(part * part, axis=-1, keepdims=True) + NORM_EPS)
                normed = part * inv
                gain = gain_ref[:, at].astype(F32)
                if s == 0:
                    up = up_ref[:, at]
                else:
                    up = pack_refs[s][:, cols + h * HD : cols + (h + 1) * HD].astype(F32)
                cot = pack_refs[s][:, at].astype(F32)
                gate = silu(up)
                if s == 0:
                    att_ref[:, at] = (normed * gain * gate).astype(BF)
                ug_ref[block, at] = (cot * normed * gain * silu_grad(up)).astype(BF)
                ngr = cot * gate * gain
                mean = jnp.mean(ngr * normed, axis=-1, keepdims=True)
                grad_ref[block, at] = (inv * (ngr - normed * mean)).astype(BF)

    for h in range(heads):
        at = slice(h * HD, (h + 1) * HD)
        along = dot_nt(grad_ref[:, at], value_ref[0, :, at])
        score_grad = (slope_ref[h].astype(F32) * along).astype(BF)
        acc_ref[:, at] += dot_nn(score_grad, key_ref[0, :, at])

    @pl.when(k == pl.num_programs(0) - 1)
    def _():
        for s in range(slots):
            block = slice(s * rows, (s + 1) * rows)
            slope = silu_grad(pre_refs[s][...].astype(F32))
            grad_ref[block, :] = (acc_ref[block, :] * (0.5 * SCALE) * slope).astype(BF)
        own = jnp.concatenate([r[:, 2 * cols : 2 * cols + 1] for r in pack_refs], axis=0).astype(F32)
        row = jnp.concatenate([r[:, 2 * cols + 1 : 2 * cols + 2] for r in pack_refs], axis=0).astype(F32)
        at_row = lax.broadcasted_iota(jnp.int32, (slots * rows, ITEMS_DEV), 1).astype(F32)
        here = row == at_row
        for m in range(slots):
            mine = own == (me ^ m).astype(F32)
            pick = jnp.where(here & mine, 1.0, 0.0).astype(BF)
            tile_refs[m][...] = dot_tn(pick, grad_ref[...]).astype(tile_refs[m].dtype)
            if m == 0:
                upt_ref[...] = dot_tn(pick, ug_ref[...]).astype(BF)


def weight_kernel(slots, terms, me_ref, upt_ref, *refs):
    term_refs, w_ref = refs[:terms], refs[terms]
    out_refs = refs[terms + 1 : terms + 1 + slots]
    sum_ref = refs[terms + 1 + slots]
    k = pl.program_id(0)

    @pl.when(k == 0)
    def _():
        total = term_refs[0][...]
        for r in term_refs[1:]:
            total = total + r[...].astype(F32)
        sum_ref[...] = total.astype(BF)

    part = dot_nt(sum_ref[...], w_ref[0]) + dot_nt(upt_ref[...], w_ref[1])
    for m in range(slots):

        @pl.when(k == m)
        def _():
            out_refs[m][...] = part.astype(out_refs[m].dtype)


def body(
    cand_feat,
    cand_counts,
    proj_weight,
    norm_gain,
    hist_kv,
    hist_lens,
    hist_mask,
    out_cot,
    owner,
    item_row,
):
    rows, depth = cand_feat.shape
    slots = lax.axis_size("blk")
    wide = lax.axis_size("heads")
    cols = proj_weight.shape[2]
    heads = cols // HD
    cands = rows * slots
    keys = hist_kv.shape[1]
    me = lax.axis_index("blk").astype(jnp.int32).reshape(1)
    head_me = lax.axis_index("heads").astype(jnp.int32).reshape(1)
    live = hist_mask.reshape(1, keys)
    kstep = min(512, depth)
    width = min(512, keys)
    chunks = keys // width
    sds = jax.ShapeDtypeStruct

    x_spec = pl.BlockSpec((rows, kstep), lambda k: (0, k))
    pre = pl.pallas_call(
        proj_query_kernel,
        grid=(depth // kstep,),
        in_specs=[x_spec, pl.BlockSpec((1, kstep, cols), lambda k: (0, k, 0))],
        out_specs=vmem_full((rows, cols)),
        out_shape=sds((rows, cols), BF),
        scratch_shapes=[pltpu.VMEM((rows, cols), F32)],
        name="proj_query",
    )(cand_feat, proj_weight)
    pre_slots = gather_slots(pre, "blk")

    pack_cols = 2 * cols + IDX_LANES
    pack, up = pl.pallas_call(
        proj_up_kernel,
        grid=(depth // kstep,),
        in_specs=[
            x_spec,
            pl.BlockSpec((1, kstep, cols), lambda k: (1, k, 0)),
            vmem_full((rows, cols)),
            vmem_full((rows, 1)),
            vmem_full((rows, 1)),
        ],
        out_specs=[vmem_full((rows, pack_cols)), vmem_full((rows, cols))],
        out_shape=[sds((rows, pack_cols), BF), sds((rows, cols), F32)],
        name="proj_up",
    )(cand_feat, proj_weight, out_cot, owner, item_row.reshape(rows, 1))
    pack_slots = gather_slots(pack, "blk")

    key_spec = pl.BlockSpec((1, width, cols), lambda k: (0, k, 0))
    value_spec = pl.BlockSpec((1, width, cols), lambda k: (1, k, 0))
    live_spec = pl.BlockSpec((1, width), lambda k: (0, k))
    block = vmem_full((rows, cols))
    every = vmem_full((cands, cols))
    sums, low, queries = pl.pallas_call(
        functools.partial(forward_kernel, slots),
        grid=(chunks,),
        in_specs=[smem_spec()] * 3 + [live_spec] + [block] * slots + [key_spec, value_spec],
        out_specs=[every, every, every],
        out_shape=[sds((cands, cols), F32), sds((cands, cols), BF), sds((cands, cols), BF)],
        name="attend",
    )(me, cand_counts, hist_lens, live, *pre_slots, hist_kv, hist_kv)

    if slots <= DIRECT:
        got = [send(low, "blk", m) for m in range(1, slots)]
    else:
        order = slot_order("blk")
        whole = lax.psum(sums.reshape(slots, rows, cols)[order], "blk")
        sums, got = whole[order].reshape(cands, cols), []

    slope = pl.pallas_call(
        functools.partial(slope_kernel, slots, rows),
        grid=(chunks,),
        in_specs=[smem_spec()] * 3 + [live_spec, every, key_spec],
        out_specs=pl.BlockSpec((heads, cands, width), lambda k: (0, 0, k)),
        out_shape=sds((heads, cands, keys), BF),
        name="slope",
    )(me, cand_counts, hist_lens, live, queries, hist_kv)

    tile = vmem_full((ITEMS_DEV, cols))
    outs = pl.pallas_call(
        functools.partial(backward_kernel, slots),
        grid=(chunks,),
        in_specs=[smem_spec(), vmem_full((1, cols)), block, every]
        + [every] * len(got)
        + [block] * slots
        + [vmem_full((rows, pack_cols))] * slots
        + [pl.BlockSpec((heads, cands, width), lambda k: (0, 0, k)), key_spec, value_spec],
        out_specs=[block, tile] + [tile] * slots,
        out_shape=[sds((rows, cols), BF), sds((ITEMS_DEV, cols), BF), sds((ITEMS_DEV, cols), F32)]
        + [sds((ITEMS_DEV, cols), BF)] * (slots - 1),
        scratch_shapes=[
            pltpu.VMEM((cands, cols), F32),
            pltpu.VMEM((cands, cols), BF),
            pltpu.VMEM((cands, cols), BF),
            pltpu.VMEM((8, 128), F32),
        ],
        name="attend_grad",
    )(
        me,
        norm_gain.reshape(1, cols),
        up,
        sums,
        *got,
        *pre_slots,
        *pack_slots,
        slope,
        hist_kv,
        hist_kv,
    )
    attended, up_table = outs[0], outs[1]
    terms = scatter_slots(list(outs[2:]), "blk")

    out_cols = depth // wide
    parts = pl.pallas_call(
        functools.partial(weight_kernel, wide, len(terms)),
        grid_spec=pltpu.PrefetchScalarGridSpec(
            num_scalar_prefetch=1,
            grid=(wide,),
            in_specs=[tile] * (1 + len(terms))
            + [pl.BlockSpec((2, out_cols, cols), lambda k, at: (0, at[0] ^ k, 0))],
            out_specs=[vmem_full((ITEMS_DEV, out_cols))] * wide,
            scratch_shapes=[pltpu.VMEM((ITEMS_DEV, cols), BF)],
        ),
        out_shape=[sds((ITEMS_DEV, out_cols), F32)]
        + [sds((ITEMS_DEV, out_cols), BF)] * (wide - 1),
        name="weight_grad",
    )(head_me, up_table, *terms, proj_weight)
    ends = scatter_slots(list(parts), "heads")
    item_grad = ends[0]
    for e in ends[1:]:
        item_grad = item_grad + e.astype(F32)
    return (attended, item_grad)


def solution(mesh):
    return jax.shard_map(
        body,
        mesh=mesh,
        in_specs=(
            P(("groups", "blk"), None),
            P("groups"),
            P(None, None, "heads"),
            P("heads"),
            P(None, ("groups", "blk"), "heads"),
            P("groups"),
            P(("groups", "blk")),
            P(("groups", "blk"), "heads"),
            P(("groups", "blk"), None),
            P(("groups", "blk")),
        ),
        out_specs=(P(("groups", "blk"), "heads"), P(("groups", "blk"), "heads")),
        check_vma=False,
    )
```

time: 188 us -> 69.6 us (0.37)
  waiting for transfers between devices: 77.6 us -> 11.9 us
  matrix products: 38.4 us -> 0 us
  Pallas kernels: 0 us -> 30.1 us
  blocking collectives: 28.4 us -> 0 us
  starting transfers between devices: 0.16 us -> 20.8 us
  local copies, waits for them, and re-layouts: 24.2 us -> 3.94 us
  between operations: 14.1 us -> 0.77 us
  other arithmetic: 3.97 us -> 1.56 us
    reduce_scatter x4 -> x0, waiting for transfers between devices: 77.6 us -> none  [the longest x1 21.6 us: body(): lax.psum_scatter(table_terms, 'blk', scatter_dimension=0, tiled=True)]
    dot_general x17 -> x0, matrix products: 38.4 us -> none  [the longest x4 10.9 us: backward_advance(): jnp.einsum('hck,khd->chd', score_grad, key_block, preferred_element_type=...]
    pallas_call x0 -> x6, Pallas kernels: none -> 30.1 us  [the longest x1 7.43 us: body(): pl.pallas_call(functools.partial(backward_kernel, slots), grid=(chunks,),...]
    all_gather x2 -> x0, blocking collectives: 28.4 us -> none  [the longest x1 15.1 us: body(): gathered_q = lax.all_gather(queries, 'blk', axis=0, tiled=True)]
    ppermute x0 -> x15, starting transfers between devices: none -> 20.8 us  [send(): lax.ppermute(x, axis, [(j, j ^ m) for j in range(lax.axis_size(axis))])]
    ppermute x0 -> x15, waiting for transfers between devices: none -> 11.9 us  [send(): lax.ppermute(x, axis, [(j, j ^ m) for j in range(lax.axis_size(axis))])]
    dynamic_slice x28 -> x0, local copies, waits for them, and re-layouts: 6.23 us -> none  [body(): lax.scan(forward_advance, start_sum, (key_blocks, value_blocks, key_user,...]
    another operation x2 -> x0, local copies, waits for them, and re-layouts: 5.09 us -> none  [the longest x1 2.54 us: body(): key_blocks = hist_kv[0].reshape(block_count, block_width, heads_here, HD)]
  transfers between devices with their start and end apart: 4 -> 15, of which waited for: 4 -> 5; matrix products, arithmetic and copies ran while one was open for 1% -> 3% of each run, Pallas kernels for 0% -> 21%
where the time goes in v1:
time: 69.6 us; the launch traced here: 69.1 us
  Pallas kernels  30.1 us (43%)
  starting transfers between devices  20.8 us (30%)
  waiting for transfers between devices  11.9 us (17%)
  local copies, waits for them, and re-layouts  3.94 us (6%)
  other arithmetic  1.56 us (2%)
  between operations  0.77 us (1%)
    ppermute x15, starting transfers between devices, send(): lax.ppermute(x, axis, [(j, j ^ m) for j in range(lax.axis_size(axis))])  20.8 us
    ppermute x15, waiting for transfers between devices, send(): lax.ppermute(x, axis, [(j, j ^ m) for j in range(lax.axis_size(axis))])  11.9 us
    pallas_call x1, Pallas kernels, body(): pl.pallas_call(functools.partial(backward_kernel, slots), grid=(chunks,),...  7.43 us
    pallas_call x1, Pallas kernels, body(): pl.pallas_call(functools.partial(forward_kernel, slots), grid=(chunks,),...  6.32 us
    pallas_call x1, Pallas kernels, body(): pl.pallas_call(functools.partial(slope_kernel, slots, rows), grid=(chunks...  4.93 us
    pallas_call x1, Pallas kernels, body(): pl.pallas_call(functools.partial(weight_kernel, wide, len(terms)), grid_s...  4.56 us
    pallas_call x1, Pallas kernels, body(): pl.pallas_call(proj_up_kernel, grid=(depth // kstep,), in_specs=[x_spec,...  3.45 us
    pallas_call x1, Pallas kernels, body(): pl.pallas_call(proj_query_kernel, grid=(depth // kstep,), in_specs=[x_spe...  3.4 us
  transfers between devices with their start and end apart: 15, of which 5 were waited for; matrix products, arithmetic and copies ran while one was open for 3% of the time, Pallas kernels for 21%

profile of v1, /device:TPU:0, one launch (start us, length us, event | category | flops | bytes accessed | tf_op | source)
XLA Modules:
  0.0 69.1 jit_solution(11782337865069345355)
XLA Ops:
  0.6 3.4 %proj_query.1.refs_0_.refs_7_ = bf16[32,512]{1,0:T(8,128)(2,1)} custom-call(bf16[32,2048]{1,0:T(8,128)(2,1)} %x_ref.3, bf16[2,2048,512]{2,1,0:T(8,128)(2,1)} %refs_4_.3), custom_call_target="tpu_custom_call" | custom-call | tf_op jit(solution)/shard_map/proj_query/pallas_call | solution.py:292
  4.0 5.1 %collective-permute-start.2 = (bf16[32,512]{1,0:T(8,128)(2,1)}, bf16[32,512]{1,0:T(8,128)(2,1)S(1)}, u32[]{:S(2)}, u32[]{:S(2)}) collective-permute-start(bf16[32,512]{1,0:T(8,128)(2,1)} %proj_query.1.refs_0_.refs_7_), channel_id=1, source_target_pairs={{0,12},{4,8},{8,4},{12,0},{1,13},{5,9},{9,5},{13,1},{2,14},{6,10},... | collective-permute-start | bytes 98312 | tf_op jit(solution)/shard_map/ppermute | solution.py:59
  9.7 0.7 %copy.12.owner_ref = s32[32,1]{1,0:T(8,128)} copy(s32[32,1]{0,1:T(1,128)S(1)} %copy-done.14) | data formatting | bytes 256 | tf_op args[8]
  10.4 0.7 %copy.13.row_ref = s32[32,1]{1,0:T(8,128)} copy(s32[32,1]{0,1:T(1,128)S(1)} %bitcast.6) | data formatting | bytes 256 | tf_op jit(solution)/shard_map/reshape | solution.py:317
  11.1 3.4 %proj_up.1 = (bf16[32,1152]{1,0:T(8,128)(2,1)}, f32[32,512]{1,0:T(8,128)}) custom-call(bf16[32,2048]{1,0:T(8,128)(2,1)} %x_ref.3, bf16[2,2048,512]{2,1,0:T(8,128)(2,1)} %refs_4_.3, bf16[32,512]{1,0:T(8,128)(2,1)} %cot_ref.1, s32[32,1]{1,0:T(8,128)} %copy.12.owner_ref, s32[32,1]{1,0:T(8,128)} %copy.13.row_ref), custom_call_target="tpu_custom_call" | custom-call | tf_op jit(solution)/shard_map/proj_up/pallas_call | solution.py:304
  14.5 3.8 %collective-permute-start.8 = (bf16[32,1152]{1,0:T(8,128)(2,1)}, bf16[32,1152]{1,0:T(8,128)(2,1)S(1)}, u32[]{:S(2)}, u32[]{:S(2)}) collective-permute-start(bf16[32,1152]{1,0:T(8,128)(2,1)} %get-tuple-element.20.refs_11_), channel_id=1, source_target_pairs={{0,12},{4,8},{8,4},{12,0},{1,13},{5,9},{9,5},{13,1},{2,14},{6,10},... | collective-permute-start | bytes 221192 | tf_op jit(solution)/shard_map/ppermute | solution.py:59
  18.4 0.6 copy-done.3
  19.0 6.3 %attend.1 = (f32[128,512]{1,0:T(8,128)}, bf16[128,512]{1,0:T(8,128)(2,1)}, bf16[128,512]{1,0:T(8,128)(2,1)}) custom-call(s32[1]{0:T(128)} %bitcast.me_ref.refs_0_, s32[2]{0:T(128)} %counts_ref.3, s32[2]{0:T(128)} %lens_ref.3, s32[1,2048]{1,0:T(1,128)} %bitcast.4, bf16[32,512]{1,0:T(8,128)(2,1)} %proj_query.1.refs_0_.refs_7_, bf16[32,512]{1,0:T(8,128)(2,1)} %copy-done.5, ...), custom_call_target="tpu_custom_call" | custom-call | tf_op jit(solution)/shard_map/attend/pallas_call | solution.py:325
  25.9 3.8 %collective-permute-start.3 = (bf16[128,512]{1,0:T(8,128)(2,1)}, bf16[128,512]{1,0:T(8,128)(2,1)S(1)}, u32[]{:S(2)}, u32[]{:S(2)}) collective-permute-start(bf16[128,512]{1,0:T(8,128)(2,1)} %get-tuple-element.19), channel_id=1, source_target_pairs={{0,4},{4,0},{8,12},{12,8},{1,5},{5,1},{9,13},{13,9},{2,6},{6,2},{1... | collective-permute-start | bytes 393224 | tf_op jit(solution)/shard_map/ppermute | solution.py:59
  29.7 0.6 collective-permute-start.6
  30.4 0.6 reshape.20.refs_1_
  30.9 4.9 %slope.1.refs_15_ = bf16[4,128,2048]{2,1,0:T(8,128)(2,1)} custom-call(s32[1]{0:T(128)} %bitcast.me_ref.refs_0_, s32[2]{0:T(128)} %counts_ref.3, s32[2]{0:T(128)} %lens_ref.3, s32[1,2048]{1,0:T(1,128)} %bitcast.5, bf16[128,512]{1,0:T(8,128)(2,1)} %get-tuple-element.21.query_ref, bf16[2,2048,512]{2,1,0:T(8,128)(2,1)} %refs_17_.1), custom_call_target="tpu_custom_call" | custom-call | tf_op jit(solution)/shard_map/slope/pallas_call | solution.py:341
  35.9 4.8 %collective-permute-done.7.refs_13_ = bf16[32,1152]{1,0:T(8,128)(2,1)S(1)} collective-permute-done((bf16[32,1152]{1,0:T(8,128)(2,1)S(1)}, bf16[32,1152]{1,0:T(8,128)(2,1)S(1)}, u32[]{:S(2)}, u32[]{:S(2)}) %collective-permute-start.7) | collective-permute-done | bytes 73760 | tf_op jit(solution)/shard_map/ppermute | solution.py:59
  41.4 7.4 %attend_grad.1 = (bf16[32,512]{1,0:T(8,128)(2,1)}, bf16[48,512]{1,0:T(8,128)(2,1)}, f32[48,512]{1,0:T(8,128)}, bf16[48,512]{1,0:T(8,128)(2,1)}, bf16[48,512]{1,0:T(8,128)(2,1)}, /*index=5*/bf16[48,512]{1,0:T(8,128)(2,1)}) custom-call(s32[1]{0:T(128)} %bitcast.me_ref.refs_0_, bf16[1,512]{1,0:T(2,128)(2,1)} %reshape.20.refs_1_, ...), custom_call_target="tpu_custom_call" | custom-call | tf_op jit(solution)/shard_map/attend_grad/pallas_call | solution.py:351
  48.9 1.8 %collective-permute-start.10 = (bf16[48,512]{1,0:T(8,128)(2,1)}, bf16[48,512]{1,0:T(8,128)(2,1)S(1)}, u32[]{:S(2)}, u32[]{:S(2)}) collective-permute-start(bf16[48,512]{1,0:T(8,128)(2,1)} %get-tuple-element.26), channel_id=1, source_target_pairs={{0,8},{4,12},{8,0},{12,4},{1,9},{5,13},{9,1},{13,5},{2,10},{6,14},... | collective-permute-start | bytes 147464 | tf_op jit(solution)/shard_map/ppermute | solution.py:59
  50.8 2.5 %collective-permute-start.11 = (bf16[48,512]{1,0:T(8,128)(2,1)}, bf16[48,512]{1,0:T(8,128)(2,1)S(1)}, u32[]{:S(2)}, u32[]{:S(2)}) collective-permute-start(bf16[48,512]{1,0:T(8,128)(2,1)} %get-tuple-element.27), channel_id=1, source_target_pairs={{0,12},{4,8},{8,4},{12,0},{1,13},{5,9},{9,5},{13,1},{2,14},{6,10},... | collective-permute-start | bytes 147464 | tf_op jit(solution)/shard_map/ppermute | solution.py:59
  53.3 1.4 %collective-permute-done.10.refs_2_ = bf16[48,512]{1,0:T(8,128)(2,1)S(1)} collective-permute-done((bf16[48,512]{1,0:T(8,128)(2,1)}, bf16[48,512]{1,0:T(8,128)(2,1)S(1)}, u32[]{:S(2)}, u32[]{:S(2)}) %collective-permute-start.10) | collective-permute-done | bytes 49184 | tf_op jit(solution)/shard_map/ppermute | solution.py:59
  54.7 2.2 %collective-permute-done.11.refs_3_ = bf16[48,512]{1,0:T(8,128)(2,1)S(1)} collective-permute-done((bf16[48,512]{1,0:T(8,128)(2,1)}, bf16[48,512]{1,0:T(8,128)(2,1)S(1)}, u32[]{:S(2)}, u32[]{:S(2)}) %collective-permute-start.11) | collective-permute-done | bytes 49184 | tf_op jit(solution)/shard_map/ppermute | solution.py:59
  56.9 0.6 copy-done.12
  57.5 4.6 %weight_grad.1 = (f32[48,512]{1,0:T(8,128)}, bf16[48,512]{1,0:T(8,128)(2,1)}, bf16[48,512]{1,0:T(8,128)(2,1)}, bf16[48,512]{1,0:T(8,128)(2,1)}) custom-call(s32[1]{0:T(128)} %bitcast.3.me_ref, bf16[48,512]{1,0:T(8,128)(2,1)} %get-tuple-element.23.upt_ref, f32[48,512]{1,0:T(8,128)} %get-tuple-element.24.refs_0_, bf16[48,512]{1,0:T(8,128)(2,1)} %copy-done.10, ...), custom_call_target="tpu_custom_call" | custom-call | tf_op jit(solution)/shard_map/weight_grad/pallas_call | solution.py:385
  62.1 1.6 %collective-permute-start.13 = (bf16[48,512]{1,0:T(8,128)(2,1)}, bf16[48,512]{1,0:T(8,128)(2,1)S(1)}, u32[]{:S(2)}, u32[]{:S(2)}) collective-permute-start(bf16[48,512]{1,0:T(8,128)(2,1)} %get-tuple-element.30), channel_id=1, source_target_pairs={{0,2},{1,3},{2,0},{3,1},{4,6},{5,7},{6,4},{7,5},{8,10},{9,11},{10,... | collective-permute-start | bytes 147464 | tf_op jit(solution)/shard_map/ppermute | solution.py:59
  63.9 2.5 %collective-permute-done.13 = bf16[48,512]{1,0:T(8,128)(2,1)S(1)} collective-permute-done((bf16[48,512]{1,0:T(8,128)(2,1)}, bf16[48,512]{1,0:T(8,128)(2,1)S(1)}, u32[]{:S(2)}, u32[]{:S(2)}) %collective-permute-start.13) | collective-permute-done | bytes 49184 | tf_op jit(solution)/shard_map/ppermute | solution.py:59
  66.4 1.1 %collective-permute-done.14 = bf16[48,512]{1,0:T(8,128)(2,1)S(1)} collective-permute-done((bf16[48,512]{1,0:T(8,128)(2,1)}, bf16[48,512]{1,0:T(8,128)(2,1)S(1)}, u32[]{:S(2)}, u32[]{:S(2)}) %collective-permute-start.14) | collective-permute-done | bytes 49184 | tf_op jit(solution)/shard_map/ppermute | solution.py:59
  67.5 1.6 %convert_add_fusion = f32[48,512]{1,0:T(8,128)} fusion(bf16[48,512]{1,0:T(8,128)(2,1)S(1)} %collective-permute-done.14, bf16[48,512]{1,0:T(8,128)(2,1)S(1)} %collective-permute-done.13, f32[48,512]{1,0:T(8,128)} %get-tuple-element.28, bf16[48,512]{1,0:T(8,128)(2,1)S(1)} %collective-permute-done.12), kind=kLoop, calls=%fused_computation | loop fusion | flops 147456 | bytes 344064 | tf_op jit(solution)/shard_map/add | solution.py:402
  (48 shorter events, 2.3 us)
Async XLA Ops:
  0.6 9.1 %copy-start.14 = (s32[32,1]{0,1:T(1,128)S(1)}, s32[32,1]{0,1:T(1,128)}, u32[]{:S(2)}) copy-start(s32[32,1]{0,1:T(1,128)} %param.18) | copy-start | bytes 388
  0.6 9.7 %copy-start.15 = (s32[32]{0:T(128)S(1)}, s32[32]{0:T(128)}, u32[]{:S(2)}) copy-start(s32[32]{0:T(128)} %param.19) | copy-start | bytes 388
  4.0 14.3 %collective-permute-start.2 = (bf16[32,512]{1,0:T(8,128)(2,1)}, bf16[32,512]{1,0:T(8,128)(2,1)S(1)}, u32[]{:S(2)}, u32[]{:S(2)}) collective-permute-start(bf16[32,512]{1,0:T(8,128)(2,1)} %proj_query.1.refs_0_.refs_7_), channel_id=1, source_target_pairs={{0,12},{4,8},{8,4},{12,0},{1,13},{5,9},{9,5},{13,1},{2,14},{6,10},... | collective-permute-start | bytes 98312 | tf_op jit(solution)/shard_map/ppermute | solution.py:59
  9.1 9.2 %collective-permute-start.1 = (bf16[32,512]{1,0:T(8,128)(2,1)}, bf16[32,512]{1,0:T(8,128)(2,1)S(1)}, u32[]{:S(2)}, u32[]{:S(2)}) collective-permute-start(bf16[32,512]{1,0:T(8,128)(2,1)} %proj_query.1.refs_0_.refs_7_), channel_id=1, source_target_pairs={{0,8},{4,12},{8,0},{12,4},{1,9},{5,13},{9,1},{13,5},{2,10},{6,14},... | collective-permute-start | bytes 98312 | tf_op jit(solution)/shard_map/ppermute | solution.py:59
  9.1 9.2 %collective-permute-start = (bf16[32,512]{1,0:T(8,128)(2,1)}, bf16[32,512]{1,0:T(8,128)(2,1)S(1)}, u32[]{:S(2)}, u32[]{:S(2)}) collective-permute-start(bf16[32,512]{1,0:T(8,128)(2,1)} %proj_query.1.refs_0_.refs_7_), channel_id=1, source_target_pairs={{0,4},{4,0},{8,12},{12,8},{1,5},{5,1},{9,13},{13,9},{2,6},{6,2},{1... | collective-permute-start | bytes 98312 | tf_op jit(solution)/shard_map/ppermute | solution.py:59
  14.5 15.2 %collective-permute-start.8 = (bf16[32,1152]{1,0:T(8,128)(2,1)}, bf16[32,1152]{1,0:T(8,128)(2,1)S(1)}, u32[]{:S(2)}, u32[]{:S(2)}) collective-permute-start(bf16[32,1152]{1,0:T(8,128)(2,1)} %get-tuple-element.20.refs_11_), channel_id=1, source_target_pairs={{0,12},{4,8},{8,4},{12,0},{1,13},{5,9},{9,5},{13,1},{2,14},{6,10},... | collective-permute-start | bytes 221192 | tf_op jit(solution)/shard_map/ppermute | solution.py:59
  19.0 10.7 %copy-start.6 = (bf16[32,1152]{1,0:T(8,128)(2,1)S(1)}, bf16[32,1152]{1,0:T(8,128)(2,1)}, u32[]{:S(2)}) copy-start(bf16[32,1152]{1,0:T(8,128)(2,1)} %get-tuple-element.20.refs_11_) | copy-start | bytes 221188
  19.0 11.4 %copy-start.13 = (bf16[512]{0:T(512)(128)(2,1)S(1)}, bf16[512]{0:T(512)(128)(2,1)}, u32[]{:S(2)}) copy-start(bf16[512]{0:T(512)(128)(2,1)} %param.13) | copy-start | bytes 3076
  25.3 15.3 %collective-permute-start.5 = (bf16[128,512]{1,0:T(8,128)(2,1)}, bf16[128,512]{1,0:T(8,128)(2,1)S(1)}, u32[]{:S(2)}, u32[]{:S(2)}) collective-permute-start(bf16[128,512]{1,0:T(8,128)(2,1)} %get-tuple-element.19), channel_id=1, source_target_pairs={{0,12},{4,8},{8,4},{12,0},{1,13},{5,9},{9,5},{13,1},{2,14},{6,10},... | collective-permute-start | bytes 393224 | tf_op jit(solution)/shard_map/ppermute | solution.py:59
  25.3 15.3 %collective-permute-start.4 = (bf16[128,512]{1,0:T(8,128)(2,1)}, bf16[128,512]{1,0:T(8,128)(2,1)S(1)}, u32[]{:S(2)}, u32[]{:S(2)}) collective-permute-start(bf16[128,512]{1,0:T(8,128)(2,1)} %get-tuple-element.19), channel_id=1, source_target_pairs={{0,8},{4,12},{8,0},{12,4},{1,9},{5,13},{9,1},{13,5},{2,10},{6,14},... | collective-permute-start | bytes 393224 | tf_op jit(solution)/shard_map/ppermute | solution.py:59
  25.9 14.8 %collective-permute-start.3 = (bf16[128,512]{1,0:T(8,128)(2,1)}, bf16[128,512]{1,0:T(8,128)(2,1)S(1)}, u32[]{:S(2)}, u32[]{:S(2)}) collective-permute-start(bf16[128,512]{1,0:T(8,128)(2,1)} %get-tuple-element.19), channel_id=1, source_target_pairs={{0,4},{4,0},{8,12},{12,8},{1,5},{5,1},{9,13},{13,9},{2,6},{6,2},{1... | collective-permute-start | bytes 393224 | tf_op jit(solution)/shard_map/ppermute | solution.py:59
  29.7 10.9 %collective-permute-start.7 = (bf16[32,1152]{1,0:T(8,128)(2,1)S(1)}, bf16[32,1152]{1,0:T(8,128)(2,1)S(1)}, u32[]{:S(2)}, u32[]{:S(2)}) collective-permute-start(bf16[32,1152]{1,0:T(8,128)(2,1)S(1)} %copy-done.6), channel_id=1, source_target_pairs={{0,8},{4,12},{8,0},{12,4},{1,9},{5,13},{9,1},{13,5},{2,10},{6,14},... | collective-permute-start | bytes 221192 | tf_op jit(solution)/shard_map/ppermute | solution.py:59
  29.7 11.0 %copy-start.7 = (bf16[32,1152]{1,0:T(8,128)(2,1)}, bf16[32,1152]{1,0:T(8,128)(2,1)S(1)}, u32[]{:S(2)}) copy-start(bf16[32,1152]{1,0:T(8,128)(2,1)S(1)} %collective-permute-done.8.refs_14_) | copy-start | bytes 221188
  29.7 10.9 %collective-permute-start.6 = (bf16[32,1152]{1,0:T(8,128)(2,1)S(1)}, bf16[32,1152]{1,0:T(8,128)(2,1)S(1)}, u32[]{:S(2)}, u32[]{:S(2)}) collective-permute-start(bf16[32,1152]{1,0:T(8,128)(2,1)S(1)} %copy-done.6), channel_id=1, source_target_pairs={{0,4},{4,0},{8,12},{12,8},{1,5},{5,1},{9,13},{13,9},{2,6},{6,2},{1... | collective-permute-start | bytes 221192 | tf_op jit(solution)/shard_map/ppermute | solution.py:59
  40.7 0.7 %copy-start.1 = (bf16[128,512]{1,0:T(8,128)(2,1)}, bf16[128,512]{1,0:T(8,128)(2,1)S(1)}, u32[]{:S(2)}) copy-start(bf16[128,512]{1,0:T(8,128)(2,1)S(1)} %collective-permute-done.4.refs_5_) | copy-start | bytes 393220
  40.7 0.8 %copy-start.2 = (bf16[128,512]{1,0:T(8,128)(2,1)}, bf16[128,512]{1,0:T(8,128)(2,1)S(1)}, u32[]{:S(2)}) copy-start(bf16[128,512]{1,0:T(8,128)(2,1)S(1)} %collective-permute-done.3.refs_4_) | copy-start | bytes 393220
  48.9 4.5 %collective-permute-start.9 = (bf16[48,512]{1,0:T(8,128)(2,1)}, bf16[48,512]{1,0:T(8,128)(2,1)S(1)}, u32[]{:S(2)}, u32[]{:S(2)}) collective-permute-start(bf16[48,512]{1,0:T(8,128)(2,1)} %get-tuple-element.25), channel_id=1, source_target_pairs={{0,4},{4,0},{8,12},{12,8},{1,5},{5,1},{9,13},{13,9},{2,6},{6,2},{1... | collective-permute-start | bytes 147464 | tf_op jit(solution)/shard_map/ppermute | solution.py:59
  48.9 5.7 %collective-permute-start.10 = (bf16[48,512]{1,0:T(8,128)(2,1)}, bf16[48,512]{1,0:T(8,128)(2,1)S(1)}, u32[]{:S(2)}, u32[]{:S(2)}) collective-permute-start(bf16[48,512]{1,0:T(8,128)(2,1)} %get-tuple-element.26), channel_id=1, source_target_pairs={{0,8},{4,12},{8,0},{12,4},{1,9},{5,13},{9,1},{13,5},{2,10},{6,14},... | collective-permute-start | bytes 147464 | tf_op jit(solution)/shard_map/ppermute | solution.py:59
  50.8 6.1 %collective-permute-start.11 = (bf16[48,512]{1,0:T(8,128)(2,1)}, bf16[48,512]{1,0:T(8,128)(2,1)S(1)}, u32[]{:S(2)}, u32[]{:S(2)}) collective-permute-start(bf16[48,512]{1,0:T(8,128)(2,1)} %get-tuple-element.27), channel_id=1, source_target_pairs={{0,12},{4,8},{8,4},{12,0},{1,13},{5,9},{9,5},{13,1},{2,14},{6,10},... | collective-permute-start | bytes 147464 | tf_op jit(solution)/shard_map/ppermute | solution.py:59
  53.3 3.6 %copy-start.10 = (bf16[48,512]{1,0:T(8,128)(2,1)}, bf16[48,512]{1,0:T(8,128)(2,1)S(1)}, u32[]{:S(2)}) copy-start(bf16[48,512]{1,0:T(8,128)(2,1)S(1)} %collective-permute-done.9.refs_1_) | copy-start | bytes 147460
  54.7 2.2 %copy-start.11 = (bf16[48,512]{1,0:T(8,128)(2,1)}, bf16[48,512]{1,0:T(8,128)(2,1)S(1)}, u32[]{:S(2)}) copy-start(bf16[48,512]{1,0:T(8,128)(2,1)S(1)} %collective-permute-done.10.refs_2_) | copy-start | bytes 147460
  62.0 1.9 %collective-permute-start.12 = (bf16[48,512]{1,0:T(8,128)(2,1)}, bf16[48,512]{1,0:T(8,128)(2,1)S(1)}, u32[]{:S(2)}, u32[]{:S(2)}) collective-permute-start(bf16[48,512]{1,0:T(8,128)(2,1)} %get-tuple-element.29), channel_id=1, source_target_pairs={{0,1},{1,0},{2,3},{3,2},{4,5},{5,4},{6,7},{7,6},{8,9},{9,8},{10,11... | collective-permute-start | bytes 147464 | tf_op jit(solution)/shard_map/ppermute | solution.py:59
  62.1 4.4 %collective-permute-start.13 = (bf16[48,512]{1,0:T(8,128)(2,1)}, bf16[48,512]{1,0:T(8,128)(2,1)S(1)}, u32[]{:S(2)}, u32[]{:S(2)}) collective-permute-start(bf16[48,512]{1,0:T(8,128)(2,1)} %get-tuple-element.30), channel_id=1, source_target_pairs={{0,2},{1,3},{2,0},{3,1},{4,6},{5,7},{6,4},{7,5},{8,10},{9,11},{10,... | collective-permute-start | bytes 147464 | tf_op jit(solution)/shard_map/ppermute | solution.py:59
  63.6 3.9 %collective-permute-start.14 = (bf16[48,512]{1,0:T(8,128)(2,1)}, bf16[48,512]{1,0:T(8,128)(2,1)S(1)}, u32[]{:S(2)}, u32[]{:S(2)}) collective-permute-start(bf16[48,512]{1,0:T(8,128)(2,1)} %get-tuple-element.31), channel_id=1, source_target_pairs={{0,3},{1,2},{2,1},{3,0},{4,7},{5,6},{6,5},{7,4},{8,11},{9,10},{10,... | collective-permute-start | bytes 147464 | tf_op jit(solution)/shard_map/ppermute | solution.py:59
  (7 other events, 4.4 us)

commit v2 on v1

v2 whole, which is shorter than its diff:
```python
import functools

import jax
import jax.numpy as jnp
from jax import lax
from jax.experimental import pallas as pl
from jax.experimental.pallas import tpu as pltpu
from jax.sharding import PartitionSpec as P

HD = 128
ITEMS_DEV = 48
NORM_EPS = 1e-05
SCALE = HD ** (-0.5)
IDX_LANES = 128
DIRECT = 4

BF = jnp.bfloat16
F32 = jnp.float32
VMEM = pltpu.MemorySpace.VMEM
SMEM = pltpu.MemorySpace.SMEM


def silu(v):
    half = v * 0.5
    return half * jnp.tanh(half) + half


def silu_grad(v):
    half = v * 0.5
    t = jnp.tanh(half)
    return 0.5 * (1.0 + t + half * (1.0 - t * t))


def dot_nt(a, b):
    return lax.dot_general(a, b, (((1,), (1,)), ((), ())), preferred_element_type=F32)


def dot_nn(a, b):
    return lax.dot_general(a, b, (((1,), (0,)), ((), ())), preferred_element_type=F32)


def dot_tn(a, b):
    return lax.dot_general(a, b, (((0,), (0,)), ((), ())), preferred_element_type=F32)


def vmem_full(shape):
    return pl.BlockSpec(shape, lambda *_: (0,) * len(shape))


def smem_spec():
    return pl.BlockSpec(memory_space=SMEM)


def slot_order(axis):
    return lax.axis_index(axis) ^ jnp.arange(lax.axis_size(axis), dtype=jnp.int32)


def send(x, axis, m):
    return lax.ppermute(x, axis, [(j, j ^ m) for j in range(lax.axis_size(axis))])


def gather_slots(x, axis):
    n = lax.axis_size(axis)
    if n <= DIRECT:
        return [x] + [send(x, axis, m) for m in range(1, n)]
    whole = lax.all_gather(x, axis)[slot_order(axis)]
    return [whole[m] for m in range(n)]


def scatter_slots(tiles, axis):
    n = lax.axis_size(axis)
    if n <= DIRECT:
        return [tiles[0]] + [send(tiles[m], axis, m) for m in range(1, n)]
    stacked = jnp.stack([t.astype(F32) for t in tiles])[slot_order(axis)]
    return [lax.psum_scatter(stacked, axis, scatter_dimension=0, tiled=False)]


def proj_query_kernel(x_ref, w_ref, query_ref, pre_ref):
    k = pl.program_id(0)

    @pl.when(k == 0)
    def _():
        pre_ref[...] = jnp.zeros_like(pre_ref)

    pre_ref[...] += dot_nn(x_ref[...], w_ref[0])

    @pl.when(k == pl.num_programs(0) - 1)
    def _():
        query_ref[...] = silu(pre_ref[...]).astype(BF)


def proj_up_kernel(x_ref, w_ref, up_ref):
    k = pl.program_id(0)

    @pl.when(k == 0)
    def _():
        up_ref[...] = jnp.zeros_like(up_ref)

    up_ref[...] += dot_nn(x_ref[...], w_ref[0])


def user_of(pos, counts_ref):
    user = jnp.zeros_like(pos)
    end = jnp.int32(0)
    for u in range(counts_ref.shape[0]):
        end = end + counts_ref[u]
        user = user + (pos >= end).astype(jnp.int32)
    return user


def keep_mask(slots, rows, width, first_key, me, counts_ref, lens_ref, live):
    cand = jnp.concatenate(
        [
            lax.broadcasted_iota(jnp.int32, (rows, 1), 0) + (me ^ m) * rows
            for m in range(slots)
        ],
        axis=0,
    )
    key = lax.broadcasted_iota(jnp.int32, (1, width), 1) + first_key
    key_user = jnp.where(live > 0, user_of(key, lens_ref), -1)
    return user_of(cand, counts_ref) == key_user


def forward_kernel(slots, me_ref, counts_ref, lens_ref, live_ref, pre_ref, idx_ref, *refs):
    got_refs = refs[:slots]
    key_ref, value_ref, pack_ref, query_ref = refs[slots : slots + 4]
    tile_refs = refs[slots + 4 : 2 * slots + 4]
    sum_ref = refs[2 * slots + 4]
    k = pl.program_id(0)
    rows, cols = pre_ref.shape
    width = key_ref.shape[1]
    me = me_ref[0]

    @pl.when(k == 0)
    def _():
        sum_ref[...] = jnp.zeros_like(sum_ref)
        pack_ref[:, :cols] = silu_grad(pre_ref[...]).astype(BF)
        pack_ref[:, cols:] = idx_ref[...]
        for m in range(slots):
            query_ref[m * rows : (m + 1) * rows, :] = got_refs[m][...]

    first = (me * pl.num_programs(0) + k) * width
    keep = keep_mask(slots, rows, width, first, me, counts_ref, lens_ref, live_ref[...])
    for h in range(cols // HD):
        at = slice(h * HD, (h + 1) * HD)
        half = dot_nt(query_ref[:, at], key_ref[0, :, at]) * (0.5 * SCALE)
        att = jnp.where(keep, half * jnp.tanh(half) + half, 0.0).astype(BF)
        sum_ref[:, at] += dot_nn(att, value_ref[0, :, at])

    @pl.when(k == pl.num_programs(0) - 1)
    def _():
        for m in range(slots):
            tile_refs[m][...] = sum_ref[m * rows : (m + 1) * rows, :].astype(tile_refs[m].dtype)


def norm_kernel(terms, *refs):
    term_refs = refs[:terms]
    up_ref, cot_ref, gain_ref, att_ref, out_ref = refs[terms:]
    cols = up_ref.shape[1]
    for h in range(cols // HD):
        at = slice(h * HD, (h + 1) * HD)
        total = term_refs[0][:, at]
        for r in term_refs[1:]:
            total = total + r[:, at].astype(F32)
        inv = lax.rsqrt(jnp.mean(total * total, axis=-1, keepdims=True) + NORM_EPS)
        normed = total * inv
        gain = gain_ref[:, at].astype(F32)
        up = up_ref[:, at]
        cot = cot_ref[:, at].astype(F32)
        gate = silu(up)
        att_ref[:, at] = (normed * gain * gate).astype(BF)
        ngr = cot * gate * gain
        mean = jnp.mean(ngr * normed, axis=-1, keepdims=True)
        out_ref[:, at] = (inv * (ngr - normed * mean)).astype(BF)
        out_ref[:, cols + h * HD : cols + (h + 1) * HD] = (
            cot * normed * gain * silu_grad(up)
        ).astype(BF)


def slope_kernel(slots, rows, me_ref, counts_ref, lens_ref, live_ref, query_ref, key_ref, out_ref):
    k = pl.program_id(0)
    width = key_ref.shape[1]
    me = me_ref[0]
    first = (me * pl.num_programs(0) + k) * width
    keep = keep_mask(slots, rows, width, first, me, counts_ref, lens_ref, live_ref[...])
    for h in range(query_ref.shape[1] // HD):
        at = slice(h * HD, (h + 1) * HD)
        half = dot_nt(query_ref[:, at], key_ref[0, :, at]) * (0.5 * SCALE)
        t = jnp.tanh(half)
        slope = 1.0 + t + half * (1.0 - t * t)
        out_ref[h] = jnp.where(keep, slope, 0.0).astype(BF)


def split(v):
    high = v.astype(BF)
    return high, (v - high.astype(F32)).astype(BF)


def backward_kernel(slots, me_ref, *refs):
    grad_refs, pack_refs = refs[:slots], refs[slots : 2 * slots]
    refs = refs[2 * slots :]
    slope_ref, key_ref, value_ref, upt_ref = refs[:4]
    tile_refs = refs[4 : 4 + slots]
    acc_ref, grad_ref = refs[4 + slots :]
    k = pl.program_id(0)
    cands, cols = acc_ref.shape
    rows = cands // slots
    me = me_ref[0]

    @pl.when(k == 0)
    def _():
        acc_ref[...] = jnp.zeros_like(acc_ref)
        for m in range(slots):
            grad_ref[m * rows : (m + 1) * rows, :] = grad_refs[m][:, :cols]

    for h in range(cols // HD):
        at = slice(h * HD, (h + 1) * HD)
        along = dot_nt(grad_ref[:, at], value_ref[0, :, at])
        score_grad = (slope_ref[h].astype(F32) * along).astype(BF)
        acc_ref[:, at] += dot_nn(score_grad, key_ref[0, :, at])

    @pl.when(k == pl.num_programs(0) - 1)
    def _():
        pre_slope = jnp.concatenate([r[:, :cols] for r in pack_refs], axis=0).astype(F32)
        high, low = split(acc_ref[...] * (0.5 * SCALE) * pre_slope)
        up_grad = jnp.concatenate([r[:, cols:] for r in grad_refs], axis=0)
        own = jnp.concatenate([r[:, cols : cols + 1] for r in pack_refs], axis=0).astype(F32)
        row = jnp.concatenate([r[:, cols + 1 : cols + 2] for r in pack_refs], axis=0).astype(F32)
        at_row = lax.broadcasted_iota(jnp.int32, (cands, ITEMS_DEV), 1).astype(F32)
        here = row == at_row
        for m in range(slots):
            mine = own == (me ^ m).astype(F32)
            pick = jnp.where(here & mine, 1.0, 0.0).astype(BF)
            tile_refs[m][...] = (dot_tn(pick, high) + dot_tn(pick, low)).astype(tile_refs[m].dtype)
            if m == 0:
                upt_ref[...] = dot_tn(pick, up_grad)


def weight_kernel(slots, terms, me_ref, upt_ref, *refs):
    term_refs, w_ref = refs[:terms], refs[terms]
    out_refs = refs[terms + 1 : terms + 1 + slots]
    sum_ref, up_ref = refs[terms + 1 + slots :]
    k = pl.program_id(0)
    items = upt_ref.shape[0]

    @pl.when(k == 0)
    def _():
        total = term_refs[0][...]
        for r in term_refs[1:]:
            total = total + r[...].astype(F32)
        sum_ref[:items, :], sum_ref[items:, :] = split(total)
        up_ref[:items, :], up_ref[items:, :] = split(upt_ref[...])

    part = dot_nt(sum_ref[...], w_ref[0]) + dot_nt(up_ref[...], w_ref[1])
    part = part[:items, :] + part[items:, :]
    for m in range(slots):

        @pl.when(k == m)
        def _():
            out_refs[m][...] = part.astype(out_refs[m].dtype)


def body(
    cand_feat,
    cand_counts,
    proj_weight,
    norm_gain,
    hist_kv,
    hist_lens,
    hist_mask,
    out_cot,
    owner,
    item_row,
):
    rows, depth = cand_feat.shape
    slots = lax.axis_size("blk")
    wide = lax.axis_size("heads")
    cols = proj_weight.shape[2]
    heads = cols // HD
    cands = rows * slots
    keys = hist_kv.shape[1]
    me = lax.axis_index("blk").astype(jnp.int32).reshape(1)
    head_me = lax.axis_index("heads").astype(jnp.int32).reshape(1)
    live = hist_mask.reshape(1, keys)
    kstep = min(512, depth)
    width = min(512, keys)
    chunks = keys // width
    sds = jax.ShapeDtypeStruct

    x_spec = pl.BlockSpec((rows, kstep), lambda k: (0, k))
    block = vmem_full((rows, cols))
    every = vmem_full((cands, cols))
    query, pre = pl.pallas_call(
        proj_query_kernel,
        grid=(depth // kstep,),
        in_specs=[x_spec, pl.BlockSpec((1, kstep, cols), lambda k: (0, k, 0))],
        out_specs=[block, block],
        out_shape=[sds((rows, cols), BF), sds((rows, cols), F32)],
        name="proj_query",
    )(cand_feat, proj_weight)
    query_slots = gather_slots(query, "blk")

    up = pl.pallas_call(
        proj_up_kernel,
        grid=(depth // kstep,),
        in_specs=[x_spec, pl.BlockSpec((1, kstep, cols), lambda k: (1, k, 0))],
        out_specs=block,
        out_shape=sds((rows, cols), F32),
        name="proj_up",
    )(cand_feat, proj_weight)
    lane = lax.broadcasted_iota(jnp.int32, (rows, IDX_LANES), 1)
    idx = jnp.where(lane == 0, owner, item_row[:, None]).astype(BF)

    key_spec = pl.BlockSpec((1, width, cols), lambda k: (0, k, 0))
    value_spec = pl.BlockSpec((1, width, cols), lambda k: (1, k, 0))
    live_spec = pl.BlockSpec((1, width), lambda k: (0, k))
    pack_shape = (rows, cols + IDX_LANES)
    outs = pl.pallas_call(
        functools.partial(forward_kernel, slots),
        grid=(chunks,),
        in_specs=[smem_spec()] * 3
        + [live_spec, block, vmem_full((rows, IDX_LANES))]
        + [block] * slots
        + [key_spec, value_spec],
        out_specs=[vmem_full(pack_shape), every] + [block] * slots,
        out_shape=[sds(pack_shape, BF), sds((cands, cols), BF), sds((rows, cols), F32)]
        + [sds((rows, cols), BF)] * (slots - 1),
        scratch_shapes=[pltpu.VMEM((cands, cols), F32)],
        name="attend",
    )(me, cand_counts, hist_lens, live, pre, idx, *query_slots, hist_kv, hist_kv)
    pack, queries = outs[:2]
    terms = scatter_slots(list(outs[2:]), "blk")
    pack_slots = gather_slots(pack, "blk")

    attended, grads = pl.pallas_call(
        functools.partial(norm_kernel, len(terms)),
        out_shape=[sds((rows, cols), BF), sds((rows, 2 * cols), BF)],
        name="norm",
    )(*terms, up, out_cot, norm_gain.reshape(1, cols))
    grad_slots = gather_slots(grads, "blk")

    slope = pl.pallas_call(
        functools.partial(slope_kernel, slots, rows),
        grid=(chunks,),
        in_specs=[smem_spec()] * 3 + [live_spec, every, key_spec],
        out_specs=pl.BlockSpec((heads, cands, width), lambda k: (0, 0, k)),
        out_shape=sds((heads, cands, keys), BF),
        name="slope",
    )(me, cand_counts, hist_lens, live, queries, hist_kv)

    tile = vmem_full((ITEMS_DEV, cols))
    outs = pl.pallas_call(
        functools.partial(backward_kernel, slots),
        grid=(chunks,),
        in_specs=[smem_spec()]
        + [vmem_full((rows, 2 * cols))] * slots
        + [vmem_full(pack_shape)] * slots
        + [pl.BlockSpec((heads, cands, width), lambda k: (0, 0, k)), key_spec, value_spec],
        out_specs=[tile] * (1 + slots),
        out_shape=[sds((ITEMS_DEV, cols), F32)] * 2 + [sds((ITEMS_DEV, cols), BF)] * (slots - 1),
        scratch_shapes=[pltpu.VMEM((cands, cols), F32), pltpu.VMEM((cands, cols), BF)],
        name="attend_grad",
    )(me, *grad_slots, *pack_slots, slope, hist_kv, hist_kv)
    up_table = outs[0]
    terms = scatter_slots(list(outs[1:]), "blk")

    out_cols = depth // wide
    parts = pl.pallas_call(
        functools.partial(weight_kernel, wide, len(terms)),
        grid_spec=pltpu.PrefetchScalarGridSpec(
            num_scalar_prefetch=1,
            grid=(wide,),
            in_specs=[tile] * (1 + len(terms))
            + [pl.BlockSpec((2, out_cols, cols), lambda k, at: (0, at[0] ^ k, 0))],
            out_specs=[vmem_full((ITEMS_DEV, out_cols))] * wide,
            scratch_shapes=[pltpu.VMEM((2 * ITEMS_DEV, cols), BF)] * 2,
        ),
        out_shape=[sds((ITEMS_DEV, out_cols), F32)]
        + [sds((ITEMS_DEV, out_cols), BF)] * (wide - 1),
        name="weight_grad",
    )(head_me, up_table, *terms, proj_weight)
    ends = scatter_slots(list(parts), "heads")
    item_grad = ends[0]
    for e in ends[1:]:
        item_grad = item_grad + e.astype(F32)
    return (attended, item_grad)


def solution(mesh):
    return jax.shard_map(
        body,
        mesh=mesh,
        in_specs=(
            P(("groups", "blk"), None),
            P("groups"),
            P(None, None, "heads"),
            P("heads"),
            P(None, ("groups", "blk"), "heads"),
            P("groups"),
            P(("groups", "blk")),
            P(("groups", "blk"), "heads"),
            P(("groups", "blk"), None),
            P(("groups", "blk")),
        ),
        out_specs=(P(("groups", "blk"), "heads"), P(("groups", "blk"), "heads")),
        check_vma=False,
    )
```

time: 69.6 us -> 75 us (1.078)
  starting transfers between devices: 20.8 us -> 25.2 us
  Pallas kernels: 30.1 us -> 31.4 us
    ppermute x15 -> x18, starting transfers between devices: 20.8 us -> 25.2 us  [send(): lax.ppermute(x, axis, [(j, j ^ m) for j in range(lax.axis_size(axis))])]
    pallas_call x0 -> x1, Pallas kernels: none -> 1.76 us  [body(): pl.pallas_call(functools.partial(norm_kernel, len(terms)), out_shape=[sds...]
    ppermute x15 -> x18, waiting for transfers between devices: 11.9 us -> 11.2 us  [send(): lax.ppermute(x, axis, [(j, j ^ m) for j in range(lax.axis_size(axis))])]
    unnamed x33 -> x38, local copies, waits for them, and re-layouts: 2.66 us -> 3.09 us
  transfers between devices with their start and end apart: 15 -> 18, of which waited for: 5 -> 6; matrix products, arithmetic and copies ran while one was open for 3% -> 2% of each run, Pallas kernels for 21% -> 14%
where the time goes in v2:
time: 75 us; the launch traced here: 74.4 us
  Pallas kernels  31.4 us (42%)
  starting transfers between devices  25.2 us (34%)
  waiting for transfers between devices  11.2 us (15%)
  local copies, waits for them, and re-layouts  3.67 us (5%)
  other arithmetic  2.23 us (3%)
  between operations  0.8 us (1%)
    ppermute x18, starting transfers between devices, send(): lax.ppermute(x, axis, [(j, j ^ m) for j in range(lax.axis_size(axis))])  25.2 us
    ppermute x18, waiting for transfers between devices, send(): lax.ppermute(x, axis, [(j, j ^ m) for j in range(lax.axis_size(axis))])  11.2 us
    pallas_call x1, Pallas kernels, body(): pl.pallas_call(functools.partial(backward_kernel, slots), grid=(chunks,),...  6.81 us
    pallas_call x1, Pallas kernels, body(): pl.pallas_call(functools.partial(forward_kernel, slots), grid=(chunks,),...  6.32 us
    pallas_call x1, Pallas kernels, body(): pl.pallas_call(functools.partial(slope_kernel, slots, rows), grid=(chunks...  4.94 us
    pallas_call x1, Pallas kernels, body(): pl.pallas_call(functools.partial(weight_kernel, wide, len(terms)), grid_s...  4.71 us
    pallas_call x1, Pallas kernels, body(): pl.pallas_call(proj_query_kernel, grid=(depth // kstep,), in_specs=[x_spe...  3.44 us
    pallas_call x1, Pallas kernels, body(): pl.pallas_call(proj_up_kernel, grid=(depth // kstep,), in_specs=[x_spec,...  3.4 us
  transfers between devices with their start and end apart: 18, of which 6 were waited for; matrix products, arithmetic and copies ran while one was open for 2% of the time, Pallas kernels for 14%

profile of v2, /device:TPU:0, one launch (start us, length us, event | category | flops | bytes accessed | tf_op | source)
XLA Modules:
  0.0 74.4 jit_solution(8314086602423086701)
XLA Ops:
  0.6 3.4 %proj_query.1 = (bf16[32,512]{1,0:T(8,128)(2,1)}, f32[32,512]{1,0:T(8,128)}) custom-call(bf16[32,2048]{1,0:T(8,128)(2,1)} %x_ref.3, bf16[2,2048,512]{2,1,0:T(8,128)(2,1)} %refs_4_.3), custom_call_target="tpu_custom_call" | custom-call | tf_op jit(solution)/shard_map/proj_query/pallas_call | solution.py:293
  4.1 5.1 %collective-permute-start.2 = (bf16[32,512]{1,0:T(8,128)(2,1)}, bf16[32,512]{1,0:T(8,128)(2,1)S(1)}, u32[]{:S(2)}, u32[]{:S(2)}) collective-permute-start(bf16[32,512]{1,0:T(8,128)(2,1)} %get-tuple-element.22.refs_0_), channel_id=1, source_target_pairs={{0,12},{4,8},{8,4},{12,0},{1,13},{5,9},{9,5},{13,1},{2,14},{6,10},... | collective-permute-start | bytes 98312 | tf_op jit(solution)/shard_map/ppermute | solution.py:59
  11.3 2.9 %collective-permute-done.1.refs_2_ = bf16[32,512]{1,0:T(8,128)(2,1)S(1)} collective-permute-done((bf16[32,512]{1,0:T(8,128)(2,1)}, bf16[32,512]{1,0:T(8,128)(2,1)S(1)}, u32[]{:S(2)}, u32[]{:S(2)}) %collective-permute-start.1) | collective-permute-done | bytes 32800 | tf_op jit(solution)/shard_map/ppermute | solution.py:59
  14.8 6.3 %attend.1 = (bf16[32,640]{1,0:T(8,128)(2,1)}, bf16[128,512]{1,0:T(8,128)(2,1)}, f32[32,512]{1,0:T(8,128)}, bf16[32,512]{1,0:T(8,128)(2,1)}, bf16[32,512]{1,0:T(8,128)(2,1)}, /*index=5*/bf16[32,512]{1,0:T(8,128)(2,1)}) custom-call(s32[1]{0:T(128)} %bitcast.me_ref, s32[2]{0:T(128)} %counts_ref.3, s32[2]{0:T(128)} %lens_ref.3, s32[1,2048]{1,0:T(1,128)} %bitcast.4, ...), custom_call_target="tpu_custom_call" | custom-call | tf_op jit(solution)/shard_map/attend/pallas_call | solution.py:318
  21.2 2.1 %collective-permute-start.4 = (bf16[32,512]{1,0:T(8,128)(2,1)}, bf16[32,512]{1,0:T(8,128)(2,1)S(1)}, u32[]{:S(2)}, u32[]{:S(2)}) collective-permute-start(bf16[32,512]{1,0:T(8,128)(2,1)} %get-tuple-element.25), channel_id=1, source_target_pairs={{0,8},{4,12},{8,0},{12,4},{1,9},{5,13},{9,1},{13,5},{2,10},{6,14},... | collective-permute-start | bytes 98312 | tf_op jit(solution)/shard_map/ppermute | solution.py:59
  23.3 2.3 %collective-permute-start.5 = (bf16[32,512]{1,0:T(8,128)(2,1)}, bf16[32,512]{1,0:T(8,128)(2,1)S(1)}, u32[]{:S(2)}, u32[]{:S(2)}) collective-permute-start(bf16[32,512]{1,0:T(8,128)(2,1)} %get-tuple-element.26), channel_id=1, source_target_pairs={{0,12},{4,8},{8,4},{12,0},{1,13},{5,9},{9,5},{13,1},{2,14},{6,10},... | collective-permute-start | bytes 98312 | tf_op jit(solution)/shard_map/ppermute | solution.py:59
  25.6 1.5 %collective-permute-start.11 = (bf16[32,640]{1,0:T(8,128)(2,1)}, bf16[32,640]{1,0:T(8,128)(2,1)S(1)}, u32[]{:S(2)}, u32[]{:S(2)}) collective-permute-start(bf16[32,640]{1,0:T(8,128)(2,1)} %get-tuple-element.29.refs_4_), channel_id=1, source_target_pairs={{0,12},{4,8},{8,4},{12,0},{1,13},{5,9},{9,5},{13,1},{2,14},{6,10},... | collective-permute-start | bytes 122888 | tf_op jit(solution)/shard_map/ppermute | solution.py:59
  27.1 3.4 %proj_up.1.refs_4_ = f32[32,512]{1,0:T(8,128)} custom-call(bf16[32,2048]{1,0:T(8,128)(2,1)} %x_ref.3, bf16[2,2048,512]{2,1,0:T(8,128)(2,1)} %refs_4_.3), custom_call_target="tpu_custom_call" | custom-call | tf_op jit(solution)/shard_map/proj_up/pallas_call | solution.py:303
  31.7 1.8 %norm.1 = (bf16[32,512]{1,0:T(8,128)(2,1)}, bf16[32,1024]{1,0:T(8,128)(2,1)}) custom-call(f32[32,512]{1,0:T(8,128)} %get-tuple-element.23.refs_0_, bf16[32,512]{1,0:T(8,128)(2,1)} %copy-done.13, bf16[32,512]{1,0:T(8,128)(2,1)} %copy-done.14, bf16[32,512]{1,0:T(8,128)(2,1)} %copy-done.15, f32[32,512]{1,0:T(8,128)} %proj_up.1.refs_4_, ...), custom_call_target="tpu_custom_call" | custom-call | tf_op jit(solution)/shard_map/norm/pallas_call | solution.py:335
  33.5 2.3 %collective-permute-start.8 = (bf16[32,1024]{1,0:T(8,128)(2,1)}, bf16[32,1024]{1,0:T(8,128)(2,1)S(1)}, u32[]{:S(2)}, u32[]{:S(2)}) collective-permute-start(bf16[32,1024]{1,0:T(8,128)(2,1)} %get-tuple-element.28.refs_0_), channel_id=1, source_target_pairs={{0,12},{4,8},{8,4},{12,0},{1,13},{5,9},{9,5},{13,1},{2,14},{6,10},... | collective-permute-start | bytes 196616 | tf_op jit(solution)/shard_map/ppermute | solution.py:59
  35.8 2.1 %collective-permute-start.6 = (bf16[32,1024]{1,0:T(8,128)(2,1)}, bf16[32,1024]{1,0:T(8,128)(2,1)S(1)}, u32[]{:S(2)}, u32[]{:S(2)}) collective-permute-start(bf16[32,1024]{1,0:T(8,128)(2,1)} %get-tuple-element.28.refs_0_), channel_id=1, source_target_pairs={{0,4},{4,0},{8,12},{12,8},{1,5},{5,1},{9,13},{13,9},{2,6},{6,2},{1... | collective-permute-start | bytes 196616 | tf_op jit(solution)/shard_map/ppermute | solution.py:59
  37.9 0.9 %collective-permute-start.10 = (bf16[32,640]{1,0:T(8,128)(2,1)S(1)}, bf16[32,640]{1,0:T(8,128)(2,1)S(1)}, u32[]{:S(2)}, u32[]{:S(2)}) collective-permute-start(bf16[32,640]{1,0:T(8,128)(2,1)S(1)} %copy-done.6), channel_id=1, source_target_pairs={{0,8},{4,12},{8,0},{12,4},{1,9},{5,13},{9,1},{13,5},{2,10},{6,14},... | collective-permute-start | bytes 122888 | tf_op jit(solution)/shard_map/ppermute | solution.py:59
  38.8 2.0 %collective-permute-start.9 = (bf16[32,640]{1,0:T(8,128)(2,1)S(1)}, bf16[32,640]{1,0:T(8,128)(2,1)S(1)}, u32[]{:S(2)}, u32[]{:S(2)}) collective-permute-start(bf16[32,640]{1,0:T(8,128)(2,1)S(1)} %copy-done.6), channel_id=1, source_target_pairs={{0,4},{4,0},{8,12},{12,8},{1,5},{5,1},{9,13},{13,9},{2,6},{6,2},{1... | collective-permute-start | bytes 122888 | tf_op jit(solution)/shard_map/ppermute | solution.py:59
  40.8 4.9 %slope.1.refs_8_ = bf16[4,128,2048]{2,1,0:T(8,128)(2,1)} custom-call(s32[1]{0:T(128)} %bitcast.me_ref, s32[2]{0:T(128)} %counts_ref.3, s32[2]{0:T(128)} %lens_ref.3, s32[1,2048]{1,0:T(1,128)} %bitcast.5, bf16[128,512]{1,0:T(8,128)(2,1)} %get-tuple-element.30.query_ref, bf16[2,2048,512]{2,1,0:T(8,128)(2,1)} %refs_10_.1), custom_call_target="tpu_custom_call" | custom-call | tf_op jit(solution)/shard_map/slope/pallas_call | solution.py:342
  47.0 6.8 %attend_grad.1 = (f32[48,512]{1,0:T(8,128)}, f32[48,512]{1,0:T(8,128)}, bf16[48,512]{1,0:T(8,128)(2,1)}, bf16[48,512]{1,0:T(8,128)(2,1)}, bf16[48,512]{1,0:T(8,128)(2,1)}) custom-call(s32[1]{0:T(128)} %bitcast.me_ref, bf16[32,1024]{1,0:T(8,128)(2,1)} %get-tuple-element.28.refs_0_, bf16[32,1024]{1,0:T(8,128)(2,1)} %copy-done.2, bf16[32,1024]{1,0:T(8,128)(2,1)} %copy-done.1, ...), custom_call_target="tpu_custom_call" | custom-call | tf_op jit(solution)/shard_map/attend_grad/pallas_call | solution.py:352
  53.9 2.0 %collective-permute-start.13 = (bf16[48,512]{1,0:T(8,128)(2,1)}, bf16[48,512]{1,0:T(8,128)(2,1)S(1)}, u32[]{:S(2)}, u32[]{:S(2)}) collective-permute-start(bf16[48,512]{1,0:T(8,128)(2,1)} %get-tuple-element.34), channel_id=1, source_target_pairs={{0,8},{4,12},{8,0},{12,4},{1,9},{5,13},{9,1},{13,5},{2,10},{6,14},... | collective-permute-start | bytes 147464 | tf_op jit(solution)/shard_map/ppermute | solution.py:59
  56.0 2.3 %collective-permute-start.14 = (bf16[48,512]{1,0:T(8,128)(2,1)}, bf16[48,512]{1,0:T(8,128)(2,1)S(1)}, u32[]{:S(2)}, u32[]{:S(2)}) collective-permute-start(bf16[48,512]{1,0:T(8,128)(2,1)} %get-tuple-element.35), channel_id=1, source_target_pairs={{0,12},{4,8},{8,4},{12,0},{1,13},{5,9},{9,5},{13,1},{2,14},{6,10},... | collective-permute-start | bytes 147464 | tf_op jit(solution)/shard_map/ppermute | solution.py:59
  58.3 0.9 %collective-permute-done.13.refs_2_ = bf16[48,512]{1,0:T(8,128)(2,1)S(1)} collective-permute-done((bf16[48,512]{1,0:T(8,128)(2,1)}, bf16[48,512]{1,0:T(8,128)(2,1)S(1)}, u32[]{:S(2)}, u32[]{:S(2)}) %collective-permute-start.13) | collective-permute-done | bytes 49184 | tf_op jit(solution)/shard_map/ppermute | solution.py:59
  59.2 2.9 %collective-permute-done.14.refs_3_ = bf16[48,512]{1,0:T(8,128)(2,1)S(1)} collective-permute-done((bf16[48,512]{1,0:T(8,128)(2,1)}, bf16[48,512]{1,0:T(8,128)(2,1)S(1)}, u32[]{:S(2)}, u32[]{:S(2)}) %collective-permute-start.14) | collective-permute-done | bytes 49184 | tf_op jit(solution)/shard_map/ppermute | solution.py:59
  62.7 4.7 %weight_grad.1 = (f32[48,512]{1,0:T(8,128)}, bf16[48,512]{1,0:T(8,128)(2,1)}, bf16[48,512]{1,0:T(8,128)(2,1)}, bf16[48,512]{1,0:T(8,128)(2,1)}) custom-call(s32[1]{0:T(128)} %bitcast.3.me_ref, f32[48,512]{1,0:T(8,128)} %get-tuple-element.31.upt_ref, f32[48,512]{1,0:T(8,128)} %get-tuple-element.32.refs_0_, bf16[48,512]{1,0:T(8,128)(2,1)} %copy-done.3, ...), custom_call_target="tpu_custom_call" | custom-call | tf_op jit(solution)/shard_map/weight_grad/pallas_call | solution.py:368
  67.4 1.5 %collective-permute-start.16 = (bf16[48,512]{1,0:T(8,128)(2,1)}, bf16[48,512]{1,0:T(8,128)(2,1)S(1)}, u32[]{:S(2)}, u32[]{:S(2)}) collective-permute-start(bf16[48,512]{1,0:T(8,128)(2,1)} %get-tuple-element.38), channel_id=1, source_target_pairs={{0,2},{1,3},{2,0},{3,1},{4,6},{5,7},{6,4},{7,5},{8,10},{9,11},{10,... | collective-permute-start | bytes 147464 | tf_op jit(solution)/shard_map/ppermute | solution.py:59
  69.3 2.5 %collective-permute-done.16 = bf16[48,512]{1,0:T(8,128)(2,1)S(1)} collective-permute-done((bf16[48,512]{1,0:T(8,128)(2,1)}, bf16[48,512]{1,0:T(8,128)(2,1)S(1)}, u32[]{:S(2)}, u32[]{:S(2)}) %collective-permute-start.16) | collective-permute-done | bytes 49184 | tf_op jit(solution)/shard_map/ppermute | solution.py:59
  71.8 1.1 %collective-permute-done.17 = bf16[48,512]{1,0:T(8,128)(2,1)S(1)} collective-permute-done((bf16[48,512]{1,0:T(8,128)(2,1)}, bf16[48,512]{1,0:T(8,128)(2,1)S(1)}, u32[]{:S(2)}, u32[]{:S(2)}) %collective-permute-start.17) | collective-permute-done | bytes 49184 | tf_op jit(solution)/shard_map/ppermute | solution.py:59
  72.8 1.6 %convert_add_fusion = f32[48,512]{1,0:T(8,128)} fusion(bf16[48,512]{1,0:T(8,128)(2,1)S(1)} %collective-permute-done.17, bf16[48,512]{1,0:T(8,128)(2,1)S(1)} %collective-permute-done.16, f32[48,512]{1,0:T(8,128)} %get-tuple-element.36, bf16[48,512]{1,0:T(8,128)(2,1)S(1)} %collective-permute-done.15), kind=kLoop, calls=%fused_computation | loop fusion | flops 147456 | bytes 344064 | tf_op jit(solution)/shard_map/add | solution.py:385
  (61 shorter events, 6.3 us)
Async XLA Ops:
  0.6 9.1 %copy-start.17 = (s32[32]{0:T(128)S(1)}, s32[32]{0:T(128)}, u32[]{:S(2)}) copy-start(s32[32]{0:T(128)} %param.19) | copy-start | bytes 388
  0.6 9.1 %copy-start.18 = (s32[32,1]{0,1:T(1,128)S(1)}, s32[32,1]{0,1:T(1,128)}, u32[]{:S(2)}) copy-start(s32[32,1]{0,1:T(1,128)} %param.18) | copy-start | bytes 388
  4.1 7.2 %collective-permute-start.2 = (bf16[32,512]{1,0:T(8,128)(2,1)}, bf16[32,512]{1,0:T(8,128)(2,1)S(1)}, u32[]{:S(2)}, u32[]{:S(2)}) collective-permute-start(bf16[32,512]{1,0:T(8,128)(2,1)} %get-tuple-element.22.refs_0_), channel_id=1, source_target_pairs={{0,12},{4,8},{8,4},{12,0},{1,13},{5,9},{9,5},{13,1},{2,14},{6,10},... | collective-permute-start | bytes 98312 | tf_op jit(solution)/shard_map/ppermute | solution.py:59
  9.2 5.0 %collective-permute-start.1 = (bf16[32,512]{1,0:T(8,128)(2,1)}, bf16[32,512]{1,0:T(8,128)(2,1)S(1)}, u32[]{:S(2)}, u32[]{:S(2)}) collective-permute-start(bf16[32,512]{1,0:T(8,128)(2,1)} %get-tuple-element.22.refs_0_), channel_id=1, source_target_pairs={{0,8},{4,12},{8,0},{12,4},{1,9},{5,13},{9,1},{13,5},{2,10},{6,14},... | collective-permute-start | bytes 98312 | tf_op jit(solution)/shard_map/ppermute | solution.py:59
  9.2 5.0 %collective-permute-start = (bf16[32,512]{1,0:T(8,128)(2,1)}, bf16[32,512]{1,0:T(8,128)(2,1)S(1)}, u32[]{:S(2)}, u32[]{:S(2)}) collective-permute-start(bf16[32,512]{1,0:T(8,128)(2,1)} %get-tuple-element.22.refs_0_), channel_id=1, source_target_pairs={{0,4},{4,0},{8,12},{12,8},{1,5},{5,1},{9,13},{13,9},{2,6},{6,2},{1... | collective-permute-start | bytes 98312 | tf_op jit(solution)/shard_map/ppermute | solution.py:59
  21.1 9.4 %copy-start.16 = (bf16[512]{0:T(512)(128)(2,1)S(1)}, bf16[512]{0:T(512)(128)(2,1)}, u32[]{:S(2)}) copy-start(bf16[512]{0:T(512)(128)(2,1)} %param.13) | copy-start | bytes 3076
  21.1 16.7 %copy-start.6 = (bf16[32,640]{1,0:T(8,128)(2,1)S(1)}, bf16[32,640]{1,0:T(8,128)(2,1)}, u32[]{:S(2)}) copy-start(bf16[32,640]{1,0:T(8,128)(2,1)} %get-tuple-element.29.refs_4_) | copy-start | bytes 122884
  21.1 9.9 %collective-permute-start.3 = (bf16[32,512]{1,0:T(8,128)(2,1)}, bf16[32,512]{1,0:T(8,128)(2,1)S(1)}, u32[]{:S(2)}, u32[]{:S(2)}) collective-permute-start(bf16[32,512]{1,0:T(8,128)(2,1)} %get-tuple-element.24), channel_id=1, source_target_pairs={{0,4},{4,0},{8,12},{12,8},{1,5},{5,1},{9,13},{13,9},{2,6},{6,2},{1... | collective-permute-start | bytes 98312 | tf_op jit(solution)/shard_map/ppermute | solution.py:59
  21.2 9.9 %collective-permute-start.4 = (bf16[32,512]{1,0:T(8,128)(2,1)}, bf16[32,512]{1,0:T(8,128)(2,1)S(1)}, u32[]{:S(2)}, u32[]{:S(2)}) collective-permute-start(bf16[32,512]{1,0:T(8,128)(2,1)} %get-tuple-element.25), channel_id=1, source_target_pairs={{0,8},{4,12},{8,0},{12,4},{1,9},{5,13},{9,1},{13,5},{2,10},{6,14},... | collective-permute-start | bytes 98312 | tf_op jit(solution)/shard_map/ppermute | solution.py:59
  23.3 7.8 %collective-permute-start.5 = (bf16[32,512]{1,0:T(8,128)(2,1)}, bf16[32,512]{1,0:T(8,128)(2,1)S(1)}, u32[]{:S(2)}, u32[]{:S(2)}) collective-permute-start(bf16[32,512]{1,0:T(8,128)(2,1)} %get-tuple-element.26), channel_id=1, source_target_pairs={{0,12},{4,8},{8,4},{12,0},{1,13},{5,9},{9,5},{13,1},{2,14},{6,10},... | collective-permute-start | bytes 98312 | tf_op jit(solution)/shard_map/ppermute | solution.py:59
  25.6 13.1 %collective-permute-start.11 = (bf16[32,640]{1,0:T(8,128)(2,1)}, bf16[32,640]{1,0:T(8,128)(2,1)S(1)}, u32[]{:S(2)}, u32[]{:S(2)}) collective-permute-start(bf16[32,640]{1,0:T(8,128)(2,1)} %get-tuple-element.29.refs_4_), channel_id=1, source_target_pairs={{0,12},{4,8},{8,4},{12,0},{1,13},{5,9},{9,5},{13,1},{2,14},{6,10},... | collective-permute-start | bytes 122888 | tf_op jit(solution)/shard_map/ppermute | solution.py:59
  33.5 12.3 %collective-permute-start.8 = (bf16[32,1024]{1,0:T(8,128)(2,1)}, bf16[32,1024]{1,0:T(8,128)(2,1)S(1)}, u32[]{:S(2)}, u32[]{:S(2)}) collective-permute-start(bf16[32,1024]{1,0:T(8,128)(2,1)} %get-tuple-element.28.refs_0_), channel_id=1, source_target_pairs={{0,12},{4,8},{8,4},{12,0},{1,13},{5,9},{9,5},{13,1},{2,14},{6,10},... | collective-permute-start | bytes 196616 | tf_op jit(solution)/shard_map/ppermute | solution.py:59
  35.8 10.0 %collective-permute-start.7 = (bf16[32,1024]{1,0:T(8,128)(2,1)}, bf16[32,1024]{1,0:T(8,128)(2,1)S(1)}, u32[]{:S(2)}, u32[]{:S(2)}) collective-permute-start(bf16[32,1024]{1,0:T(8,128)(2,1)} %get-tuple-element.28.refs_0_), channel_id=1, source_target_pairs={{0,8},{4,12},{8,0},{12,4},{1,9},{5,13},{9,1},{13,5},{2,10},{6,14},... | collective-permute-start | bytes 196616 | tf_op jit(solution)/shard_map/ppermute | solution.py:59
  35.8 10.0 %collective-permute-start.6 = (bf16[32,1024]{1,0:T(8,128)(2,1)}, bf16[32,1024]{1,0:T(8,128)(2,1)S(1)}, u32[]{:S(2)}, u32[]{:S(2)}) collective-permute-start(bf16[32,1024]{1,0:T(8,128)(2,1)} %get-tuple-element.28.refs_0_), channel_id=1, source_target_pairs={{0,4},{4,0},{8,12},{12,8},{1,5},{5,1},{9,13},{13,9},{2,6},{6,2},{1... | collective-permute-start | bytes 196616 | tf_op jit(solution)/shard_map/ppermute | solution.py:59
  37.9 7.8 %collective-permute-start.10 = (bf16[32,640]{1,0:T(8,128)(2,1)S(1)}, bf16[32,640]{1,0:T(8,128)(2,1)S(1)}, u32[]{:S(2)}, u32[]{:S(2)}) collective-permute-start(bf16[32,640]{1,0:T(8,128)(2,1)S(1)} %copy-done.6), channel_id=1, source_target_pairs={{0,8},{4,12},{8,0},{12,4},{1,9},{5,13},{9,1},{13,5},{2,10},{6,14},... | collective-permute-start | bytes 122888 | tf_op jit(solution)/shard_map/ppermute | solution.py:59
  38.8 7.1 %copy-start.7 = (bf16[32,640]{1,0:T(8,128)(2,1)}, bf16[32,640]{1,0:T(8,128)(2,1)S(1)}, u32[]{:S(2)}) copy-start(bf16[32,640]{1,0:T(8,128)(2,1)S(1)} %collective-permute-done.11.refs_7_) | copy-start | bytes 122884
  38.8 7.0 %collective-permute-start.9 = (bf16[32,640]{1,0:T(8,128)(2,1)S(1)}, bf16[32,640]{1,0:T(8,128)(2,1)S(1)}, u32[]{:S(2)}, u32[]{:S(2)}) collective-permute-start(bf16[32,640]{1,0:T(8,128)(2,1)S(1)} %copy-done.6), channel_id=1, source_target_pairs={{0,4},{4,0},{8,12},{12,8},{1,5},{5,1},{9,13},{13,9},{2,6},{6,2},{1... | collective-permute-start | bytes 122888 | tf_op jit(solution)/shard_map/ppermute | solution.py:59
  53.9 4.4 %collective-permute-start.12 = (bf16[48,512]{1,0:T(8,128)(2,1)}, bf16[48,512]{1,0:T(8,128)(2,1)S(1)}, u32[]{:S(2)}, u32[]{:S(2)}) collective-permute-start(bf16[48,512]{1,0:T(8,128)(2,1)} %get-tuple-element.33), channel_id=1, source_target_pairs={{0,4},{4,0},{8,12},{12,8},{1,5},{5,1},{9,13},{13,9},{2,6},{6,2},{1... | collective-permute-start | bytes 147464 | tf_op jit(solution)/shard_map/ppermute | solution.py:59
  53.9 5.3 %collective-permute-start.13 = (bf16[48,512]{1,0:T(8,128)(2,1)}, bf16[48,512]{1,0:T(8,128)(2,1)S(1)}, u32[]{:S(2)}, u32[]{:S(2)}) collective-permute-start(bf16[48,512]{1,0:T(8,128)(2,1)} %get-tuple-element.34), channel_id=1, source_target_pairs={{0,8},{4,12},{8,0},{12,4},{1,9},{5,13},{9,1},{13,5},{2,10},{6,14},... | collective-permute-start | bytes 147464 | tf_op jit(solution)/shard_map/ppermute | solution.py:59
  56.0 6.1 %collective-permute-start.14 = (bf16[48,512]{1,0:T(8,128)(2,1)}, bf16[48,512]{1,0:T(8,128)(2,1)S(1)}, u32[]{:S(2)}, u32[]{:S(2)}) collective-permute-start(bf16[48,512]{1,0:T(8,128)(2,1)} %get-tuple-element.35), channel_id=1, source_target_pairs={{0,12},{4,8},{8,4},{12,0},{1,13},{5,9},{9,5},{13,1},{2,14},{6,10},... | collective-permute-start | bytes 147464 | tf_op jit(solution)/shard_map/ppermute | solution.py:59
  58.3 3.8 %copy-start.3 = (bf16[48,512]{1,0:T(8,128)(2,1)}, bf16[48,512]{1,0:T(8,128)(2,1)S(1)}, u32[]{:S(2)}) copy-start(bf16[48,512]{1,0:T(8,128)(2,1)S(1)} %collective-permute-done.12.refs_1_) | copy-start | bytes 147460
  67.4 1.9 %collective-permute-start.15 = (bf16[48,512]{1,0:T(8,128)(2,1)}, bf16[48,512]{1,0:T(8,128)(2,1)S(1)}, u32[]{:S(2)}, u32[]{:S(2)}) collective-permute-start(bf16[48,512]{1,0:T(8,128)(2,1)} %get-tuple-element.37), channel_id=1, source_target_pairs={{0,1},{1,0},{2,3},{3,2},{4,5},{5,4},{6,7},{7,6},{8,9},{9,8},{10,11... | collective-permute-start | bytes 147464 | tf_op jit(solution)/shard_map/ppermute | solution.py:59
  67.4 4.4 %collective-permute-start.16 = (bf16[48,512]{1,0:T(8,128)(2,1)}, bf16[48,512]{1,0:T(8,128)(2,1)S(1)}, u32[]{:S(2)}, u32[]{:S(2)}) collective-permute-start(bf16[48,512]{1,0:T(8,128)(2,1)} %get-tuple-element.38), channel_id=1, source_target_pairs={{0,2},{1,3},{2,0},{3,1},{4,6},{5,7},{6,4},{7,5},{8,10},{9,11},{10,... | collective-permute-start | bytes 147464 | tf_op jit(solution)/shard_map/ppermute | solution.py:59
  68.9 3.9 %collective-permute-start.17 = (bf16[48,512]{1,0:T(8,128)(2,1)}, bf16[48,512]{1,0:T(8,128)(2,1)S(1)}, u32[]{:S(2)}, u32[]{:S(2)}) collective-permute-start(bf16[48,512]{1,0:T(8,128)(2,1)} %get-tuple-element.39), channel_id=1, source_target_pairs={{0,3},{1,2},{2,1},{3,0},{4,7},{5,6},{6,5},{7,4},{8,11},{9,10},{10,... | collective-permute-start | bytes 147464 | tf_op jit(solution)/shard_map/ppermute | solution.py:59
  (13 other events, 12.6 us)

commit v3 on v0

v3 whole, which is shorter than its diff:
```python
import functools

import jax
import jax.numpy as jnp
from jax import lax
from jax.experimental import pallas as pl
from jax.experimental.pallas import tpu as pltpu
from jax.sharding import PartitionSpec as P


HD = 128
ITEMS_DEV = 48
NORM_EPS = 1e-05
SCALE = HD ** (-0.5)
IDX_LANES = 128
DIRECT = 4
GRANT = 24 << 20

BF = jnp.bfloat16
F32 = jnp.float32
VMEM = pltpu.MemorySpace.VMEM
SMEM = pltpu.MemorySpace.SMEM
HBM = pltpu.MemorySpace.HBM


def silu(v):
    half = v * 0.5
    return half * jnp.tanh(half) + half


def silu_grad(v):
    half = v * 0.5
    t = jnp.tanh(half)
    return 0.5 * (1.0 + t + half * (1.0 - t * t))


def dot_nt(a, b):
    return lax.dot_general(a, b, (((1,), (1,)), ((), ())), preferred_element_type=F32)


def dot_nn(a, b):
    return lax.dot_general(a, b, (((1,), (0,)), ((), ())), preferred_element_type=F32)


def dot_tn(a, b):
    return lax.dot_general(a, b, (((0,), (0,)), ((), ())), preferred_element_type=F32)


def vmem_spec():
    return pl.BlockSpec(memory_space=VMEM)


def smem_spec():
    return pl.BlockSpec(memory_space=SMEM)


def near(x):
    return pltpu.with_memory_space_constraint(x, VMEM)


def far(x):
    return pltpu.with_memory_space_constraint(x, HBM)


LOADS = 4


def load_kernel(src_ref, dst_ref, sems):
    step = src_ref.shape[1] // (LOADS // 2)
    copies = [
        pltpu.make_async_copy(
            src_ref.at[i // 2, pl.ds(i % 2 * step, step)],
            dst_ref.at[i // 2, pl.ds(i % 2 * step, step)],
            sems.at[i],
        )
        for i in range(LOADS)
    ]
    for c in copies:
        c.start()
    for c in copies:
        c.wait()


def load(x):
    return pl.pallas_call(
        load_kernel,
        in_specs=[pl.BlockSpec(memory_space=HBM)],
        out_specs=vmem_spec(),
        out_shape=pltpu.VMEM(x.shape, x.dtype),
        scratch_shapes=[pltpu.SemaphoreType.DMA((LOADS,))],
        compiler_params=pltpu.CompilerParams(vmem_limit_bytes=GRANT),
    )(far(x))


def call(kernel, scalars, arrays, outs, scratch=()):
    return pl.pallas_call(
        kernel,
        in_specs=[smem_spec()] * len(scalars) + [vmem_spec()] * len(arrays),
        out_specs=[vmem_spec()] * len(outs),
        out_shape=[pltpu.VMEM(shape, kind) for shape, kind in outs],
        scratch_shapes=[pltpu.VMEM(shape, kind) for shape, kind in scratch],
        compiler_params=pltpu.CompilerParams(vmem_limit_bytes=GRANT),
    )(*scalars, *[near(x) for x in arrays])


def slot_order(axis):
    return lax.axis_index(axis) ^ jnp.arange(lax.axis_size(axis), dtype=jnp.int32)


def send(x, axis, m):
    return lax.ppermute(x, axis, [(j, j ^ m) for j in range(lax.axis_size(axis))])


def gather_slots(x, axis):
    n = lax.axis_size(axis)
    if n <= DIRECT:
        return [x] + [send(x, axis, m) for m in range(1, n)]
    whole = lax.all_gather(x, axis)[slot_order(axis)]
    return [whole[m] for m in range(n)]


def scatter_slots(tiles, axis):
    n = lax.axis_size(axis)
    if n <= DIRECT:
        return [tiles[0]] + [send(tiles[m], axis, m) for m in range(1, n)]
    stacked = jnp.stack([t.astype(F32) for t in tiles])[slot_order(axis)]
    return [lax.psum_scatter(stacked, axis, scatter_dimension=0, tiled=False)]


def split(v):
    high = v.astype(BF)
    return high, (v - high.astype(F32)).astype(BF)


def project_kernel(owner_ref, row_ref, x_ref, w_ref, cot_ref, query_ref, pack_ref, up_ref, pre_ref):
    k = pl.program_id(0)
    rows, cols = up_ref.shape

    @pl.when(k == 0)
    def _():
        pre_ref[...] = jnp.zeros_like(pre_ref)
        up_ref[...] = jnp.zeros_like(up_ref)
        lane = lax.broadcasted_iota(jnp.int32, (rows, IDX_LANES), 1)
        line = lax.broadcasted_iota(jnp.int32, (rows, IDX_LANES), 0)
        idx = jnp.zeros((rows, IDX_LANES), jnp.int32)
        for r in range(rows):
            idx = jnp.where(line == r, jnp.where(lane == 0, owner_ref[r], row_ref[r]), idx)
        pack_ref[:, 3 * cols :] = idx.astype(F32).astype(BF)
        pack_ref[:, :cols] = cot_ref[...]

    pre_ref[...] += dot_nn(x_ref[...], w_ref[0])
    up_ref[...] += dot_nn(x_ref[...], w_ref[1])

    @pl.when(k == pl.num_programs(0) - 1)
    def _():
        query_ref[...] = silu(pre_ref[...]).astype(BF)
        pack_ref[:, cols : 2 * cols] = up_ref[...].astype(BF)
        pack_ref[:, 2 * cols : 3 * cols] = silu_grad(pre_ref[...]).astype(BF)


def user_of(pos, counts_ref):
    user = jnp.zeros_like(pos)
    end = jnp.int32(0)
    for u in range(counts_ref.shape[0]):
        end = end + counts_ref[u]
        user = user + (pos >= end).astype(jnp.int32)
    return user


def keep_mask(slots, rows, width, first_key, me, counts_ref, lens_ref, live):
    cand = jnp.concatenate(
        [
            lax.broadcasted_iota(jnp.int32, (rows, 1), 0) + (me ^ m) * rows
            for m in range(slots)
        ],
        axis=0,
    )
    key = lax.broadcasted_iota(jnp.int32, (1, width), 1) + first_key
    key_user = jnp.where(live > 0, user_of(key, lens_ref), -1)
    return user_of(cand, counts_ref) == key_user


def diagonal(ref, first, heads):
    parts = [ref[:, (first + h) * HD : (first + h + 1) * HD] for h in range(heads)]
    none = jnp.zeros_like(parts[0])
    return jnp.concatenate(
        [
            jnp.concatenate([parts[h] if h == g else none for g in range(heads)], axis=1)
            for h in range(heads)
        ],
        axis=0,
    )


def chunk_mask(slots, rows, k, width, together, me, counts_ref, lens_ref, live_ref, keys):
    live = live_ref[:, k * width : (k + 1) * width]
    first = me * keys + k * width
    keep = keep_mask(slots, rows, width, first, me, counts_ref, lens_ref, live)
    return jnp.concatenate([keep] * together, axis=0)


def forward_kernel(
    slots, together, width, me_ref, counts_ref, lens_ref, live_ref, kv_ref, *refs
):
    got_refs = refs[:slots]
    sum_ref, low_ref, query_ref = refs[slots:]
    cands, cols = sum_ref.shape
    rows = cands // slots
    keys = kv_ref.shape[1]
    me = me_ref[0]
    for m in range(slots):
        query_ref[m * rows : (m + 1) * rows, :] = got_refs[m][...]
    for p in range(0, cols // HD, together):
        at = slice(p * HD, (p + together) * HD)
        query = diagonal(query_ref, p, together)
        total = jnp.zeros((together * cands, together * HD), F32)
        for k in range(keys // width):
            ks = slice(k * width, (k + 1) * width)
            keep = chunk_mask(
                slots, rows, k, width, together, me, counts_ref, lens_ref, live_ref, keys
            )
            half = dot_nt(query, kv_ref[0, ks, at]) * (0.5 * SCALE)
            att = jnp.where(keep, half * jnp.tanh(half) + half, 0.0).astype(BF)
            total = total + dot_nn(att, kv_ref[1, ks, at])
        for h in range(together):
            part = total[h * cands : (h + 1) * cands, h * HD : (h + 1) * HD]
            hs = slice((p + h) * HD, (p + h + 1) * HD)
            sum_ref[:, hs] = part
            low_ref[:, hs] = part.astype(BF)


def slope_kernel(
    slots, together, width, me_ref, counts_ref, lens_ref, live_ref, kv_ref, query_ref, out_ref
):
    cands, cols = query_ref.shape
    keys = kv_ref.shape[1]
    me = me_ref[0]
    for p in range(0, cols // HD, together):
        at = slice(p * HD, (p + together) * HD)
        query = diagonal(query_ref, p, together)
        for k in range(keys // width):
            ks = slice(k * width, (k + 1) * width)
            keep = chunk_mask(
                slots, cands // slots, k, width, together, me, counts_ref, lens_ref, live_ref, keys
            )
            half = dot_nt(query, kv_ref[0, ks, at]) * (0.5 * SCALE)
            t = jnp.tanh(half)
            slope = 1.0 + t + half * (1.0 - t * t)
            out_ref[p * cands : (p + together) * cands, ks] = jnp.where(keep, slope, 0.0).astype(BF)


def backward_kernel(slots, together, width, me_ref, gain_ref, up_ref, sum_ref, kv_ref, slope_ref, *refs):
    got, pack_refs = refs[: len(refs) - 2 * slots - 5], refs[len(refs) - 2 * slots - 5 :][:slots]
    refs = refs[len(refs) - slots - 5 :]
    att_ref, upt_ref = refs[:2]
    tile_refs = refs[2 : 2 + slots]
    acc_ref, grad_ref, ug_ref = refs[2 + slots :]
    rows, cols = up_ref.shape
    cands = rows * slots
    keys = kv_ref.shape[1]
    me = me_ref[0]

    for s in range(slots):
        block = slice(s * rows, (s + 1) * rows)
        total = sum_ref[block, :]
        for m in range(1, len(got) + 1):
            other = s ^ m
            total = total + got[m - 1][other * rows : (other + 1) * rows, :].astype(F32)
        for h in range(cols // HD):
            at = slice(h * HD, (h + 1) * HD)
            part = total[:, at]
            inv = lax.rsqrt(jnp.mean(part * part, axis=-1, keepdims=True) + NORM_EPS)
            normed = part * inv
            gain = gain_ref[:, at].astype(F32)
            cot = pack_refs[s][:, at].astype(F32)
            if s == 0:
                up = up_ref[:, at]
            else:
                up = pack_refs[s][:, cols + h * HD : cols + (h + 1) * HD].astype(F32)
            gate = silu(up)
            if s == 0:
                att_ref[:, at] = (normed * gain * gate).astype(BF)
            ug_ref[block, at] = (cot * normed * gain * silu_grad(up)).astype(BF)
            ngr = cot * gate * gain
            mean = jnp.mean(ngr * normed, axis=-1, keepdims=True)
            grad_ref[block, at] = (inv * (ngr - normed * mean)).astype(BF)

    for p in range(0, cols // HD, together):
        at = slice(p * HD, (p + together) * HD)
        grad = diagonal(grad_ref, p, together)
        total = jnp.zeros((together * cands, together * HD), F32)
        for k in range(keys // width):
            ks = slice(k * width, (k + 1) * width)
            along = dot_nt(grad, kv_ref[1, ks, at])
            slope = slope_ref[p * cands : (p + together) * cands, ks].astype(F32)
            total = total + dot_nn((slope * along).astype(BF), kv_ref[0, ks, at])
        for h in range(together):
            hs = slice((p + h) * HD, (p + h + 1) * HD)
            acc_ref[:, hs] = total[h * cands : (h + 1) * cands, h * HD : (h + 1) * HD]

    pre_slope = jnp.concatenate([r[:, 2 * cols : 3 * cols] for r in pack_refs], axis=0).astype(F32)
    high, low = split(acc_ref[...] * (0.5 * SCALE) * pre_slope)
    idx = jnp.concatenate([r[:, 3 * cols :] for r in pack_refs], axis=0).astype(F32)
    own, row = idx[:, :1], idx[:, 1:2]
    at_row = lax.broadcasted_iota(jnp.int32, (cands, ITEMS_DEV), 1).astype(F32)
    here = row == at_row
    for m in range(slots):
        mine = own == (me ^ m).astype(F32)
        pick = jnp.where(here & mine, 1.0, 0.0).astype(BF)
        tile_refs[m][...] = (dot_tn(pick, high) + dot_tn(pick, low)).astype(tile_refs[m].dtype)
        if m == 0:
            upt_ref[...] = dot_tn(pick, ug_ref[...])


def weight_kernel(slots, terms, me_ref, w_ref, upt_ref, *refs):
    term_refs, out_refs = refs[:terms], refs[terms:]
    items = upt_ref.shape[0]
    height = out_refs[0].shape[1]
    total = term_refs[0][...]
    for r in term_refs[1:]:
        total = total + r[...].astype(F32)
    table = jnp.concatenate(split(total), axis=0)
    ups = jnp.concatenate(split(upt_ref[...]), axis=0)
    for m in range(slots):
        at = pl.ds(pl.multiple_of((me_ref[0] ^ m) * height, height), height)
        part = dot_nt(table, w_ref[0, at, :]) + dot_nt(ups, w_ref[1, at, :])
        out_refs[m][...] = (part[:items, :] + part[items:, :]).astype(out_refs[m].dtype)


def finish_kernel(*refs):
    total = refs[0][...]
    for r in refs[1:-1]:
        total = total + r[...].astype(F32)
    refs[-1][...] = total


def whole_body(
    cand_feat,
    cand_counts,
    proj_weight,
    norm_gain,
    hist_kv,
    hist_lens,
    hist_mask,
    out_cot,
    owner,
    item_row,
):
    rows, depth = cand_feat.shape
    slots = lax.axis_size("blk")
    wide = lax.axis_size("heads")
    cols = proj_weight.shape[2]
    heads = cols // HD
    cands = rows * slots
    keys = hist_kv.shape[1]
    me = lax.axis_index("blk").astype(jnp.int32).reshape(1)
    head_me = lax.axis_index("heads").astype(jnp.int32).reshape(1)
    live = hist_mask.reshape(1, keys)
    kstep = min(512, depth)
    width = min(512, keys)

    together = 2 if heads % 2 == 0 else 1
    pack_cols = 3 * cols + IDX_LANES
    query, pack, up = pl.pallas_call(
        project_kernel,
        grid=(depth // kstep,),
        in_specs=[
            smem_spec(),
            smem_spec(),
            pl.BlockSpec((rows, kstep), lambda k: (0, k)),
            pl.BlockSpec((2, kstep, cols), lambda k: (0, k, 0)),
            pl.BlockSpec((rows, cols), lambda k: (0, 0)),
        ],
        out_specs=[vmem_spec()] * 3,
        out_shape=[
            pltpu.VMEM((rows, cols), BF),
            pltpu.VMEM((rows, pack_cols), BF),
            pltpu.VMEM((rows, cols), F32),
        ],
        scratch_shapes=[pltpu.VMEM((rows, cols), F32)],
        compiler_params=pltpu.CompilerParams(vmem_limit_bytes=GRANT),
        name="project",
    )(owner.reshape(rows), item_row, far(cand_feat), far(proj_weight), far(out_cot))
    query_slots = gather_slots(query, "blk")
    pack_slots = gather_slots(pack, "blk")

    hist_kv = load(hist_kv)
    weight = load(proj_weight)

    every = (cands, cols)
    ranges = [me, cand_counts, hist_lens]
    sums, low, queries = call(
        functools.partial(forward_kernel, slots, together, width),
        ranges,
        [live, hist_kv, *query_slots],
        [(every, F32), (every, BF), (every, BF)],
    )
    if slots <= DIRECT:
        got = [send(low, "blk", m) for m in range(1, slots)]
    else:
        order = slot_order("blk")
        whole = lax.psum(sums.reshape(slots, rows, cols)[order], "blk")
        sums, got = whole[order].reshape(cands, cols), []

    slope = call(
        functools.partial(slope_kernel, slots, together, width),
        ranges,
        [live, hist_kv, queries],
        [((heads * cands, keys), BF)],
    )[0]

    tile = (ITEMS_DEV, cols)
    outs = call(
        functools.partial(backward_kernel, slots, together, width),
        [me],
        [norm_gain.reshape(1, cols), up, sums, hist_kv, slope, *got, *pack_slots],
        [((rows, cols), BF), (tile, F32), (tile, F32)] + [(tile, BF)] * (slots - 1),
        [(every, F32), (every, BF), (every, BF)],
    )
    attended, up_table = outs[:2]
    terms = scatter_slots(list(outs[2:]), "blk")

    end = (ITEMS_DEV, depth // wide)
    parts = call(
        functools.partial(weight_kernel, wide, len(terms)),
        [head_me],
        [weight, up_table, *terms],
        [(end, F32)] + [(end, BF)] * (wide - 1),
    )
    ends = scatter_slots(list(parts), "heads")
    item_grad = call(finish_kernel, [], ends, [(end, F32)])[0]
    return (attended, item_grad)


def solution(mesh):
    return jax.shard_map(
        whole_body,
        mesh=mesh,
        in_specs=(
            P(("groups", "blk"), None),
            P("groups"),
            P(None, None, "heads"),
            P("heads"),
            P(None, ("groups", "blk"), "heads"),
            P("groups"),
            P(("groups", "blk")),
            P(("groups", "blk"), "heads"),
            P(("groups", "blk"), None),
            P(("groups", "blk")),
        ),
        out_specs=(P(("groups", "blk"), "heads"), P(("groups", "blk"), "heads")),
        check_vma=False,
    )
```

time: 188 us -> 58.8 us (0.31)
  waiting for transfers between devices: 77.6 us -> 11.6 us
  matrix products: 38.4 us -> 0 us
  blocking collectives: 28.4 us -> 0 us
  starting transfers between devices: 0.16 us -> 23.4 us
  local copies, waits for them, and re-layouts: 24.2 us -> 6.7 us
  Pallas kernels: 0 us -> 16.1 us
  between operations: 14.1 us -> 0.78 us
  other arithmetic: 3.97 us -> 0 us
    reduce_scatter x4 -> x0, waiting for transfers between devices: 77.6 us -> none  [the longest x1 21.6 us: body(): lax.psum_scatter(table_terms, 'blk', scatter_dimension=0, tiled=True)]
    dot_general x17 -> x0, matrix products: 38.4 us -> none  [the longest x4 10.9 us: backward_advance(): jnp.einsum('hck,khd->chd', score_grad, key_block, preferred_element_type=...]
    all_gather x2 -> x0, blocking collectives: 28.4 us -> none  [the longest x1 15.1 us: body(): gathered_q = lax.all_gather(queries, 'blk', axis=0, tiled=True)]
    ppermute x0 -> x15, starting transfers between devices: none -> 23.4 us  [send(): lax.ppermute(x, axis, [(j, j ^ m) for j in range(lax.axis_size(axis))])]
    pallas_call x0 -> x8, Pallas kernels: none -> 16.1 us  [the longest x5 8.11 us: call(): pl.pallas_call(kernel, in_specs=[smem_spec()] * len(scalars) + [vmem_spec...]
    ppermute x0 -> x15, waiting for transfers between devices: none -> 11.6 us  [send(): lax.ppermute(x, axis, [(j, j ^ m) for j in range(lax.axis_size(axis))])]
    dynamic_slice x28 -> x0, local copies, waits for them, and re-layouts: 6.23 us -> none  [body(): lax.scan(forward_advance, start_sum, (key_blocks, value_blocks, key_user,...]
    another operation x2 -> x0, local copies, waits for them, and re-layouts: 5.09 us -> none  [the longest x1 2.54 us: body(): key_blocks = hist_kv[0].reshape(block_count, block_width, heads_here, HD)]
  transfers between devices with their start and end apart: 4 -> 15, of which waited for: 4 -> 5; matrix products, arithmetic and copies ran while one was open for 1% -> 1% of each run, Pallas kernels for 0% -> 15%
where the time goes in v3:
time: 58.8 us; the launch traced here: 58.6 us
  starting transfers between devices  23.4 us (40%)
  Pallas kernels  16.1 us (27%)
  waiting for transfers between devices  11.6 us (20%)
  local copies, waits for them, and re-layouts  6.7 us (11%)
  between operations  0.78 us (1%)
    ppermute x15, starting transfers between devices, send(): lax.ppermute(x, axis, [(j, j ^ m) for j in range(lax.axis_size(axis))])  23.4 us
    ppermute x15, waiting for transfers between devices, send(): lax.ppermute(x, axis, [(j, j ^ m) for j in range(lax.axis_size(axis))])  11.6 us
    pallas_call x5, Pallas kernels, call(): pl.pallas_call(kernel, in_specs=[smem_spec()] * len(scalars) + [vmem_spec...  8.11 us
    unnamed x18, local copies, waits for them, and re-layouts  6.7 us
    pallas_call x2, Pallas kernels, load(): pl.pallas_call(load_kernel, in_specs=[pl.BlockSpec(memory_space=HBM)], ou...  4.45 us
    pallas_call x1, Pallas kernels, whole_body(): pl.pallas_call(project_kernel, grid=(depth // kstep,), in_specs=[smem_spe...  3.57 us
  transfers between devices with their start and end apart: 15, of which 5 were waited for; matrix products, arithmetic and copies ran while one was open for 1% of the time, Pallas kernels for 15%

profile of v3, /device:TPU:0, one launch (start us, length us, event | category | flops | bytes accessed | tf_op | source)
XLA Modules:
  0.0 58.6 jit_solution(1569503469225161817)
XLA Ops:
  0.6 0.6 %copy-done.5 = s32[32,1]{0,1:T(1,128)S(1)} copy-done((s32[32,1]{0,1:T(1,128)S(1)}, s32[32,1]{0,1:T(1,128)}, u32[]{:S(2)}) %copy-start.5) | copy-done | bytes 152
  1.3 0.7 %copy-done.6 = s32[32]{0:T(128)S(1)} copy-done((s32[32]{0:T(128)S(1)}, s32[32]{0:T(128)}, u32[]{:S(2)}) %copy-start.6) | copy-done | bytes 152
  1.9 3.6 %project.1 = (bf16[32,512]{1,0:T(8,128)(2,1)S(1)}, bf16[32,1664]{1,0:T(8,128)(2,1)S(1)}, f32[32,512]{1,0:T(8,128)S(1)}) custom-call(s32[32]{0:T(128)S(1)} %bitcast.6, s32[32]{0:T(128)S(1)} %copy-done.6, bf16[32,2048]{1,0:T(8,128)(2,1)} %x_ref.1, bf16[2,2048,512]{2,1,0:T(8,128)(2,1)} %src_ref.3, bf16[32,512]{1,0:T(8,128)(2,1)} %cot_ref.1), custom_call_target="tpu_custom_call" | custom-call | tf_op jit(solution)/shard_map/project/pallas_call | solution.py:364
  5.5 5.1 %collective-permute-start.8 = (bf16[32,1664]{1,0:T(8,128)(2,1)S(1)}, bf16[32,1664]{1,0:T(8,128)(2,1)S(1)}, u32[]{:S(2)}, u32[]{:S(2)}) collective-permute-start(bf16[32,1664]{1,0:T(8,128)(2,1)S(1)} %get-tuple-element.23.refs_3_), channel_id=1, source_target_pairs={{0,12},{4,8},{8,4},{12,0},{1,13},{5,9},{9,5},{13,1},{2,14},{6,10},... | collective-permute-start | bytes 319496 | tf_op jit(solution)/shard_map/ppermute | solution.py:111
  10.7 0.9 %collective-permute-start.1 = (bf16[32,512]{1,0:T(8,128)(2,1)S(1)}, bf16[32,512]{1,0:T(8,128)(2,1)S(1)}, u32[]{:S(2)}, u32[]{:S(2)}) collective-permute-start(bf16[32,512]{1,0:T(8,128)(2,1)S(1)} %get-tuple-element.19.refs_0_), channel_id=1, source_target_pairs={{0,8},{4,12},{8,0},{12,4},{1,9},{5,13},{9,1},{13,5},{2,10},{6,14},... | collective-permute-start | bytes 98312 | tf_op jit(solution)/shard_map/ppermute | solution.py:111
  11.7 3.4 %collective-permute-start = (bf16[32,512]{1,0:T(8,128)(2,1)S(1)}, bf16[32,512]{1,0:T(8,128)(2,1)S(1)}, u32[]{:S(2)}, u32[]{:S(2)}) collective-permute-start(bf16[32,512]{1,0:T(8,128)(2,1)S(1)} %get-tuple-element.19.refs_0_), channel_id=1, source_target_pairs={{0,4},{4,0},{8,12},{12,8},{1,5},{5,1},{9,13},{13,9},{2,6},{6,2},{1... | collective-permute-start | bytes 98312 | tf_op jit(solution)/shard_map/ppermute | solution.py:111
  15.1 2.2 %shard_map.113.kv_ref = bf16[2,2048,512]{2,1,0:T(8,128)(2,1)S(1)} custom-call(bf16[2,2048,512]{2,1,0:T(8,128)(2,1)} %src_ref.2), custom_call_target="tpu_custom_call" | custom-call | tf_op jit(solution)/shard_map/pallas_call | solution.py:85
  17.9 2.1 %shard_map.114 = (f32[128,512]{1,0:T(8,128)S(1)}, bf16[128,512]{1,0:T(8,128)(2,1)S(1)}, bf16[128,512]{1,0:T(8,128)(2,1)S(1)}) custom-call(s32[1]{0:T(128)} %bitcast.me_ref, s32[2]{0:T(128)S(1)} %copy-done.3, s32[2]{0:T(128)S(1)} %copy-done.4, s32[1,2048]{1,0:T(1,128)S(1)} %bitcast.4, bf16[2,2048,512]{2,1,0:T(8,128)(2,1)S(1)} %shard_map.113.kv_ref, ...), custom_call_target="tpu_custom_call" | custom-call | tf_op jit(solution)/shard_map/pallas_call | solution.py:96
  20.0 2.5 %collective-permute-start.5 = (bf16[128,512]{1,0:T(8,128)(2,1)S(1)}, bf16[128,512]{1,0:T(8,128)(2,1)S(1)}, u32[]{:S(2)}, u32[]{:S(2)}) collective-permute-start(bf16[128,512]{1,0:T(8,128)(2,1)S(1)} %get-tuple-element.22), channel_id=1, source_target_pairs={{0,12},{4,8},{8,4},{12,0},{1,13},{5,9},{9,5},{13,1},{2,14},{6,10},... | collective-permute-start | bytes 393224 | tf_op jit(solution)/shard_map/ppermute | solution.py:111
  22.6 1.8 %collective-permute-start.3 = (bf16[128,512]{1,0:T(8,128)(2,1)S(1)}, bf16[128,512]{1,0:T(8,128)(2,1)S(1)}, u32[]{:S(2)}, u32[]{:S(2)}) collective-permute-start(bf16[128,512]{1,0:T(8,128)(2,1)S(1)} %get-tuple-element.22), channel_id=1, source_target_pairs={{0,4},{4,0},{8,12},{12,8},{1,5},{5,1},{9,13},{13,9},{2,6},{6,2},{1... | collective-permute-start | bytes 393224 | tf_op jit(solution)/shard_map/ppermute | solution.py:111
  24.5 1.0 %collective-permute-start.7 = (bf16[32,1664]{1,0:T(8,128)(2,1)S(1)}, bf16[32,1664]{1,0:T(8,128)(2,1)S(1)}, u32[]{:S(2)}, u32[]{:S(2)}) collective-permute-start(bf16[32,1664]{1,0:T(8,128)(2,1)S(1)} %get-tuple-element.23.refs_3_), channel_id=1, source_target_pairs={{0,8},{4,12},{8,0},{12,4},{1,9},{5,13},{9,1},{13,5},{2,10},{6,14},... | collective-permute-start | bytes 319496 | tf_op jit(solution)/shard_map/ppermute | solution.py:111
  25.5 2.0 %collective-permute-start.6 = (bf16[32,1664]{1,0:T(8,128)(2,1)S(1)}, bf16[32,1664]{1,0:T(8,128)(2,1)S(1)}, u32[]{:S(2)}, u32[]{:S(2)}) collective-permute-start(bf16[32,1664]{1,0:T(8,128)(2,1)S(1)} %get-tuple-element.23.refs_3_), channel_id=1, source_target_pairs={{0,4},{4,0},{8,12},{12,8},{1,5},{5,1},{9,13},{13,9},{2,6},{6,2},{1... | collective-permute-start | bytes 319496 | tf_op jit(solution)/shard_map/ppermute | solution.py:111
  27.5 2.4 %shard_map.115.slope_ref = bf16[512,2048]{1,0:T(8,128)(2,1)S(1)} custom-call(s32[1]{0:T(128)} %bitcast.me_ref, s32[2]{0:T(128)S(1)} %copy-done.3, s32[2]{0:T(128)S(1)} %copy-done.4, s32[1,2048]{1,0:T(1,128)S(1)} %bitcast.5, bf16[2,2048,512]{2,1,0:T(8,128)(2,1)S(1)} %shard_map.113.kv_ref, bf16[128,512]{1,0:T(8,128)(2,1)S(1)} %get-tuple-element.21.query_ref), custom_call_target="tpu_custom_call" | custom-call | tf_op jit(solution)/shard_map/pallas_call | solution.py:96
  29.9 7.9 %collective-permute-done.7.refs_5_ = bf16[32,1664]{1,0:T(8,128)(2,1)S(1)} collective-permute-done((bf16[32,1664]{1,0:T(8,128)(2,1)S(1)}, bf16[32,1664]{1,0:T(8,128)(2,1)S(1)}, u32[]{:S(2)}, u32[]{:S(2)}) %collective-permute-start.7) | collective-permute-done | bytes 106528 | tf_op jit(solution)/shard_map/ppermute | solution.py:111
  37.8 2.2 %shard_map.116 = (bf16[32,512]{1,0:T(8,128)(2,1)S(1)}, f32[48,512]{1,0:T(8,128)S(1)}, f32[48,512]{1,0:T(8,128)S(1)}, bf16[48,512]{1,0:T(8,128)(2,1)S(1)}, bf16[4...) custom-call(s32[1]{0:T(128)} %bitcast.me_ref, bf16[1,512]{1,0:T(2,128)(2,1)S(1)} %reshape.20.gain_ref, ...), custom_call_target="tpu_custom_call" | custom-call | tf_op jit(solution)/shard_map/pallas_call | solution.py:96
  40.1 3.0 %collective-permute-start.10 = (bf16[48,512]{1,0:T(8,128)(2,1)S(1)}, bf16[48,512]{1,0:T(8,128)(2,1)S(1)}, u32[]{:S(2)}, u32[]{:S(2)}) collective-permute-start(bf16[48,512]{1,0:T(8,128)(2,1)S(1)} %get-tuple-element.28), channel_id=1, source_target_pairs={{0,8},{4,12},{8,0},{12,4},{1,9},{5,13},{9,1},{13,5},{2,10},{6,14},... | collective-permute-start | bytes 147464 | tf_op jit(solution)/shard_map/ppermute | solution.py:111
  43.1 1.4 %collective-permute-start.11 = (bf16[48,512]{1,0:T(8,128)(2,1)S(1)}, bf16[48,512]{1,0:T(8,128)(2,1)S(1)}, u32[]{:S(2)}, u32[]{:S(2)}) collective-permute-start(bf16[48,512]{1,0:T(8,128)(2,1)S(1)} %get-tuple-element.29), channel_id=1, source_target_pairs={{0,12},{4,8},{8,4},{12,0},{1,13},{5,9},{9,5},{13,1},{2,14},{6,10},... | collective-permute-start | bytes 147464 | tf_op jit(solution)/shard_map/ppermute | solution.py:111
  44.4 2.2 %shard_map.117.w_ref = bf16[2,2048,512]{2,1,0:T(8,128)(2,1)S(1)} custom-call(bf16[2,2048,512]{2,1,0:T(8,128)(2,1)} %src_ref.3), custom_call_target="tpu_custom_call" | custom-call | tf_op jit(solution)/shard_map/pallas_call | solution.py:85
  46.7 1.9 %copy-done = bf16[2,2048,512]{2,1,0:T(8,128)(2,1)} copy-done((bf16[2,2048,512]{2,1,0:T(8,128)(2,1)}, bf16[2,2048,512]{2,1,0:T(8,128)(2,1)S(1)}, u32[]{:S(2)}) %copy-start) | copy-done | bytes 4194328
  48.9 2.2 %copy-done.1 = bf16[2,2048,512]{2,1,0:T(8,128)(2,1)S(1)} copy-done((bf16[2,2048,512]{2,1,0:T(8,128)(2,1)S(1)}, bf16[2,2048,512]{2,1,0:T(8,128)(2,1)}, u32[]{:S(2)}) %copy-start.1) | copy-done | bytes 4194328
  51.1 1.4 %shard_map.118 = (f32[48,512]{1,0:T(8,128)S(1)}, bf16[48,512]{1,0:T(8,128)(2,1)S(1)}, bf16[48,512]{1,0:T(8,128)(2,1)S(1)}, bf16[48,512]{1,0:T(8,128)(2,1)S(1)}) custom-call(s32[1]{0:T(128)} %bitcast.3.me_ref, bf16[2,2048,512]{2,1,0:T(8,128)(2,1)S(1)} %copy-done.1, f32[48,512]{1,0:T(8,128)S(1)} %get-tuple-element.25.upt_ref, ...), custom_call_target="tpu_custom_call" | custom-call | tf_op jit(solution)/shard_map/pallas_call | solution.py:96
  52.6 1.6 %collective-permute-start.13 = (bf16[48,512]{1,0:T(8,128)(2,1)S(1)}, bf16[48,512]{1,0:T(8,128)(2,1)S(1)}, u32[]{:S(2)}, u32[]{:S(2)}) collective-permute-start(bf16[48,512]{1,0:T(8,128)(2,1)S(1)} %get-tuple-element.32), channel_id=1, source_target_pairs={{0,2},{1,3},{2,0},{3,1},{4,6},{5,7},{6,4},{7,5},{8,10},{9,11},{10,... | collective-permute-start | bytes 147464 | tf_op jit(solution)/shard_map/ppermute | solution.py:111
  55.1 1.7 %collective-permute-done.13.refs_2_ = bf16[48,512]{1,0:T(8,128)(2,1)S(1)} collective-permute-done((bf16[48,512]{1,0:T(8,128)(2,1)S(1)}, bf16[48,512]{1,0:T(8,128)(2,1)S(1)}, u32[]{:S(2)}, u32[]{:S(2)}) %collective-permute-start.13) | collective-permute-done | bytes 49184 | tf_op jit(solution)/shard_map/ppermute | solution.py:111
  56.8 1.1 %collective-permute-done.14.refs_3_ = bf16[48,512]{1,0:T(8,128)(2,1)S(1)} collective-permute-done((bf16[48,512]{1,0:T(8,128)(2,1)S(1)}, bf16[48,512]{1,0:T(8,128)(2,1)S(1)}, u32[]{:S(2)}, u32[]{:S(2)}) %collective-permute-start.14) | collective-permute-done | bytes 49184 | tf_op jit(solution)/shard_map/ppermute | solution.py:111
  (33 shorter events, 2.8 us)
Async XLA Ops:
  0.6 0.7 %copy-start.5 = (s32[32,1]{0,1:T(1,128)S(1)}, s32[32,1]{0,1:T(1,128)}, u32[]{:S(2)}) copy-start(s32[32,1]{0,1:T(1,128)} %param.18) | copy-start | bytes 388
  1.3 0.7 %copy-start.6 = (s32[32]{0:T(128)S(1)}, s32[32]{0:T(128)}, u32[]{:S(2)}) copy-start(s32[32]{0:T(128)} %row_ref.1) | copy-start | bytes 388
  5.5 20.0 %collective-permute-start.8 = (bf16[32,1664]{1,0:T(8,128)(2,1)S(1)}, bf16[32,1664]{1,0:T(8,128)(2,1)S(1)}, u32[]{:S(2)}, u32[]{:S(2)}) collective-permute-start(bf16[32,1664]{1,0:T(8,128)(2,1)S(1)} %get-tuple-element.23.refs_3_), channel_id=1, source_target_pairs={{0,12},{4,8},{8,4},{12,0},{1,13},{5,9},{9,5},{13,1},{2,14},{6,10},... | collective-permute-start | bytes 319496 | tf_op jit(solution)/shard_map/ppermute | solution.py:111
  10.7 6.7 %collective-permute-start.2 = (bf16[32,512]{1,0:T(8,128)(2,1)S(1)}, bf16[32,512]{1,0:T(8,128)(2,1)S(1)}, u32[]{:S(2)}, u32[]{:S(2)}) collective-permute-start(bf16[32,512]{1,0:T(8,128)(2,1)S(1)} %get-tuple-element.19.refs_0_), channel_id=1, source_target_pairs={{0,12},{4,8},{8,4},{12,0},{1,13},{5,9},{9,5},{13,1},{2,14},{6,10},... | collective-permute-start | bytes 98312 | tf_op jit(solution)/shard_map/ppermute | solution.py:111
  10.7 7.1 %collective-permute-start.1 = (bf16[32,512]{1,0:T(8,128)(2,1)S(1)}, bf16[32,512]{1,0:T(8,128)(2,1)S(1)}, u32[]{:S(2)}, u32[]{:S(2)}) collective-permute-start(bf16[32,512]{1,0:T(8,128)(2,1)S(1)} %get-tuple-element.19.refs_0_), channel_id=1, source_target_pairs={{0,8},{4,12},{8,0},{12,4},{1,9},{5,13},{9,1},{13,5},{2,10},{6,14},... | collective-permute-start | bytes 98312 | tf_op jit(solution)/shard_map/ppermute | solution.py:111
  11.7 6.2 %collective-permute-start = (bf16[32,512]{1,0:T(8,128)(2,1)S(1)}, bf16[32,512]{1,0:T(8,128)(2,1)S(1)}, u32[]{:S(2)}, u32[]{:S(2)}) collective-permute-start(bf16[32,512]{1,0:T(8,128)(2,1)S(1)} %get-tuple-element.19.refs_0_), channel_id=1, source_target_pairs={{0,4},{4,0},{8,12},{12,8},{1,5},{5,1},{9,13},{13,9},{2,6},{6,2},{1... | collective-permute-start | bytes 98312 | tf_op jit(solution)/shard_map/ppermute | solution.py:111
  15.1 2.8 %copy-start.2 = (s32[2048]{0:T(1024)S(1)}, s32[2048]{0:T(1024)}, u32[]{:S(2)}) copy-start(s32[2048]{0:T(1024)} %param.16) | copy-start | bytes 24580
  15.1 2.8 %copy-start.3 = (s32[2]{0:T(128)S(1)}, s32[2]{0:T(128)}, u32[]{:S(2)}) copy-start(s32[2]{0:T(128)} %counts_ref.3) | copy-start | bytes 28
  15.1 2.8 %copy-start.4 = (s32[2]{0:T(128)S(1)}, s32[2]{0:T(128)}, u32[]{:S(2)}) copy-start(s32[2]{0:T(128)} %lens_ref.3) | copy-start | bytes 28
  17.3 10.2 %copy-start.7 = (bf16[512]{0:T(512)(128)(2,1)S(1)}, bf16[512]{0:T(512)(128)(2,1)}, u32[]{:S(2)}) copy-start(bf16[512]{0:T(512)(128)(2,1)} %param.13) | copy-start | bytes 3076
  20.0 17.7 %collective-permute-start.5 = (bf16[128,512]{1,0:T(8,128)(2,1)S(1)}, bf16[128,512]{1,0:T(8,128)(2,1)S(1)}, u32[]{:S(2)}, u32[]{:S(2)}) collective-permute-start(bf16[128,512]{1,0:T(8,128)(2,1)S(1)} %get-tuple-element.22), channel_id=1, source_target_pairs={{0,12},{4,8},{8,4},{12,0},{1,13},{5,9},{9,5},{13,1},{2,14},{6,10},... | collective-permute-start | bytes 393224 | tf_op jit(solution)/shard_map/ppermute | solution.py:111
  22.6 15.2 %collective-permute-start.4 = (bf16[128,512]{1,0:T(8,128)(2,1)S(1)}, bf16[128,512]{1,0:T(8,128)(2,1)S(1)}, u32[]{:S(2)}, u32[]{:S(2)}) collective-permute-start(bf16[128,512]{1,0:T(8,128)(2,1)S(1)} %get-tuple-element.22), channel_id=1, source_target_pairs={{0,8},{4,12},{8,0},{12,4},{1,9},{5,13},{9,1},{13,5},{2,10},{6,14},... | collective-permute-start | bytes 393224 | tf_op jit(solution)/shard_map/ppermute | solution.py:111
  22.6 15.1 %collective-permute-start.3 = (bf16[128,512]{1,0:T(8,128)(2,1)S(1)}, bf16[128,512]{1,0:T(8,128)(2,1)S(1)}, u32[]{:S(2)}, u32[]{:S(2)}) collective-permute-start(bf16[128,512]{1,0:T(8,128)(2,1)S(1)} %get-tuple-element.22), channel_id=1, source_target_pairs={{0,4},{4,0},{8,12},{12,8},{1,5},{5,1},{9,13},{13,9},{2,6},{6,2},{1... | collective-permute-start | bytes 393224 | tf_op jit(solution)/shard_map/ppermute | solution.py:111
  24.5 13.3 %collective-permute-start.7 = (bf16[32,1664]{1,0:T(8,128)(2,1)S(1)}, bf16[32,1664]{1,0:T(8,128)(2,1)S(1)}, u32[]{:S(2)}, u32[]{:S(2)}) collective-permute-start(bf16[32,1664]{1,0:T(8,128)(2,1)S(1)} %get-tuple-element.23.refs_3_), channel_id=1, source_target_pairs={{0,8},{4,12},{8,0},{12,4},{1,9},{5,13},{9,1},{13,5},{2,10},{6,14},... | collective-permute-start | bytes 319496 | tf_op jit(solution)/shard_map/ppermute | solution.py:111
  25.5 12.3 %collective-permute-start.6 = (bf16[32,1664]{1,0:T(8,128)(2,1)S(1)}, bf16[32,1664]{1,0:T(8,128)(2,1)S(1)}, u32[]{:S(2)}, u32[]{:S(2)}) collective-permute-start(bf16[32,1664]{1,0:T(8,128)(2,1)S(1)} %get-tuple-element.23.refs_3_), channel_id=1, source_target_pairs={{0,4},{4,0},{8,12},{12,8},{1,5},{5,1},{9,13},{13,9},{2,6},{6,2},{1... | collective-permute-start | bytes 319496 | tf_op jit(solution)/shard_map/ppermute | solution.py:111
  40.0 8.6 %collective-permute-start.9 = (bf16[48,512]{1,0:T(8,128)(2,1)S(1)}, bf16[48,512]{1,0:T(8,128)(2,1)S(1)}, u32[]{:S(2)}, u32[]{:S(2)}) collective-permute-start(bf16[48,512]{1,0:T(8,128)(2,1)S(1)} %get-tuple-element.27), channel_id=1, source_target_pairs={{0,4},{4,0},{8,12},{12,8},{1,5},{5,1},{9,13},{13,9},{2,6},{6,2},{1... | collective-permute-start | bytes 147464 | tf_op jit(solution)/shard_map/ppermute | solution.py:111
  40.1 8.5 %collective-permute-start.10 = (bf16[48,512]{1,0:T(8,128)(2,1)S(1)}, bf16[48,512]{1,0:T(8,128)(2,1)S(1)}, u32[]{:S(2)}, u32[]{:S(2)}) collective-permute-start(bf16[48,512]{1,0:T(8,128)(2,1)S(1)} %get-tuple-element.28), channel_id=1, source_target_pairs={{0,8},{4,12},{8,0},{12,4},{1,9},{5,13},{9,1},{13,5},{2,10},{6,14},... | collective-permute-start | bytes 147464 | tf_op jit(solution)/shard_map/ppermute | solution.py:111
  43.1 5.9 %collective-permute-start.11 = (bf16[48,512]{1,0:T(8,128)(2,1)S(1)}, bf16[48,512]{1,0:T(8,128)(2,1)S(1)}, u32[]{:S(2)}, u32[]{:S(2)}) collective-permute-start(bf16[48,512]{1,0:T(8,128)(2,1)S(1)} %get-tuple-element.29), channel_id=1, source_target_pairs={{0,12},{4,8},{8,4},{12,0},{1,13},{5,9},{9,5},{13,1},{2,14},{6,10},... | collective-permute-start | bytes 147464 | tf_op jit(solution)/shard_map/ppermute | solution.py:111
  46.7 1.9 %copy-start = (bf16[2,2048,512]{2,1,0:T(8,128)(2,1)}, bf16[2,2048,512]{2,1,0:T(8,128)(2,1)S(1)}, u32[]{:S(2)}) copy-start(bf16[2,2048,512]{2,1,0:T(8,128)(2,1)S(1)} %shard_map.117.w_ref) | copy-start | bytes 12582916
  48.9 2.2 %copy-start.1 = (bf16[2,2048,512]{2,1,0:T(8,128)(2,1)S(1)}, bf16[2,2048,512]{2,1,0:T(8,128)(2,1)}, u32[]{:S(2)}) copy-start(bf16[2,2048,512]{2,1,0:T(8,128)(2,1)} %copy-done) | copy-start | bytes 12582916
  52.5 2.5 %collective-permute-start.12 = (bf16[48,512]{1,0:T(8,128)(2,1)S(1)}, bf16[48,512]{1,0:T(8,128)(2,1)S(1)}, u32[]{:S(2)}, u32[]{:S(2)}) collective-permute-start(bf16[48,512]{1,0:T(8,128)(2,1)S(1)} %get-tuple-element.31), channel_id=1, source_target_pairs={{0,1},{1,0},{2,3},{3,2},{4,5},{5,4},{6,7},{7,6},{8,9},{9,8},{10,11... | collective-permute-start | bytes 147464 | tf_op jit(solution)/shard_map/ppermute | solution.py:111
  52.6 4.2 %collective-permute-start.13 = (bf16[48,512]{1,0:T(8,128)(2,1)S(1)}, bf16[48,512]{1,0:T(8,128)(2,1)S(1)}, u32[]{:S(2)}, u32[]{:S(2)}) collective-permute-start(bf16[48,512]{1,0:T(8,128)(2,1)S(1)} %get-tuple-element.32), channel_id=1, source_target_pairs={{0,2},{1,3},{2,0},{3,1},{4,6},{5,7},{6,4},{7,5},{8,10},{9,11},{10,... | collective-permute-start | bytes 147464 | tf_op jit(solution)/shard_map/ppermute | solution.py:111
  54.2 3.7 %collective-permute-start.14 = (bf16[48,512]{1,0:T(8,128)(2,1)S(1)}, bf16[48,512]{1,0:T(8,128)(2,1)S(1)}, u32[]{:S(2)}, u32[]{:S(2)}) collective-permute-start(bf16[48,512]{1,0:T(8,128)(2,1)S(1)} %get-tuple-element.33), channel_id=1, source_target_pairs={{0,3},{1,2},{2,1},{3,0},{4,7},{5,6},{6,5},{7,4},{8,11},{9,10},{10,... | collective-permute-start | bytes 147464 | tf_op jit(solution)/shard_map/ppermute | solution.py:111

commit v4 on v3

--- a/solution.py
+++ b/solution.py
@@ -63,6 +63,7 @@
 
 
 LOADS = 4
+PARTS = 4
 
 
 def load_kernel(src_ref, dst_ref, sems):
@@ -132,30 +133,56 @@
     return high, (v - high.astype(F32)).astype(BF)
 
 
-def project_kernel(owner_ref, row_ref, x_ref, w_ref, cot_ref, query_ref, pack_ref, up_ref, pre_ref):
-    k = pl.program_id(0)
+def column(line_ref):
+    n = line_ref.shape[1]
+    same = lax.broadcasted_iota(jnp.int32, (n, n), 0) == lax.broadcasted_iota(jnp.int32, (n, n), 1)
+    return jnp.sum(jnp.where(same, line_ref[...], 0).astype(F32), axis=1, keepdims=True)
+
+
+def project_kernel(
+    x_hbm, w_hbm, cot_hbm, owner_hbm, row_hbm, query_ref, pack_ref, both_ref, up_ref,
+    x_ref, w_ref, owner_ref, row_ref, sems,
+):
     rows, cols = up_ref.shape
-
-    @pl.when(k == 0)
-    def _():
-        pre_ref[...] = jnp.zeros_like(pre_ref)
-        up_ref[...] = jnp.zeros_like(up_ref)
-        lane = lax.broadcasted_iota(jnp.int32, (rows, IDX_LANES), 1)
-        line = lax.broadcasted_iota(jnp.int32, (rows, IDX_LANES), 0)
-        idx = jnp.zeros((rows, IDX_LANES), jnp.int32)
-        for r in range(rows):
-            idx = jnp.where(line == r, jnp.where(lane == 0, owner_ref[r], row_ref[r]), idx)
-        pack_ref[:, 3 * cols :] = idx.astype(F32).astype(BF)
-        pack_ref[:, :cols] = cot_ref[...]
-
-    pre_ref[...] += dot_nn(x_ref[...], w_ref[0])
-    up_ref[...] += dot_nn(x_ref[...], w_ref[1])
-
-    @pl.when(k == pl.num_programs(0) - 1)
-    def _():
-        query_ref[...] = silu(pre_ref[...]).astype(BF)
-        pack_ref[:, cols : 2 * cols] = up_ref[...].astype(BF)
-        pack_ref[:, 2 * cols : 3 * cols] = silu_grad(pre_ref[...]).astype(BF)
+    depth = x_ref.shape[1]
+    step = depth // PARTS
+    copies = []
+
+    def start(src, dst):
+        copies.append(pltpu.make_async_copy(src, dst, sems.at[len(copies)]))
+        copies[-1].start()
+
+    start(x_hbm, x_ref)
+    for j in range(2):
+        for i in range(PARTS):
+            at = pl.ds(i * step, step)
+            start(w_hbm.at[j, at], w_ref.at[j, at])
+    start(cot_hbm, pack_ref.at[:, pl.ds(0, cols)])
+    start(owner_hbm, owner_ref)
+    start(row_hbm, row_ref)
+    copies[0].wait()
+
+    def product(j):
+        total = jnp.zeros((rows, cols), F32)
+        for i in range(PARTS):
+            copies[1 + j * PARTS + i].wait()
+            at = slice(i * step, (i + 1) * step)
+            total = total + dot_nn(x_ref[:, at], w_ref[j, at, :])
+        return total
+
+    pre = product(0)
+    query_ref[...] = silu(pre).astype(BF)
+    pack_ref[:, 2 * cols : 3 * cols] = silu_grad(pre).astype(BF)
+    up = product(1)
+    up_ref[...] = up
+    pack_ref[:, cols : 2 * cols] = up.astype(BF)
+    for c in copies[1 + 2 * PARTS :]:
+        c.wait()
+    lane = lax.broadcasted_iota(jnp.int32, (rows, IDX_LANES), 1)
+    idx = jnp.where(lane == 0, column(owner_ref), column(row_ref))
+    pack_ref[:, 3 * cols :] = idx.astype(BF)
+    both_ref[:, :cols] = query_ref[...]
+    both_ref[:, cols:] = pack_ref[...]
 
 
 def user_of(pos, counts_ref):
@@ -209,7 +236,7 @@
     keys = kv_ref.shape[1]
     me = me_ref[0]
     for m in range(slots):
-        query_ref[m * rows : (m + 1) * rows, :] = got_refs[m][...]
+        query_ref[m * rows : (m + 1) * rows, :] = got_refs[m][:, :cols]
     for p in range(0, cols // HD, together):
         at = slice(p * HD, (p + together) * HD)
         query = diagonal(query_ref, p, together)
@@ -259,6 +286,7 @@
     cands = rows * slots
     keys = kv_ref.shape[1]
     me = me_ref[0]
+    packs = [r.at[:, pl.ds(r.shape[1] - 3 * cols - IDX_LANES, 3 * cols + IDX_LANES)] for r in pack_refs]
 
     for s in range(slots):
         block = slice(s * rows, (s + 1) * rows)
@@ -272,11 +300,11 @@
             inv = lax.rsqrt(jnp.mean(part * part, axis=-1, keepdims=True) + NORM_EPS)
             normed = part * inv
             gain = gain_ref[:, at].astype(F32)
-            cot = pack_refs[s][:, at].astype(F32)
+            cot = packs[s][:, at].astype(F32)
             if s == 0:
                 up = up_ref[:, at]
             else:
-                up = pack_refs[s][:, cols + h * HD : cols + (h + 1) * HD].astype(F32)
+                up = packs[s][:, cols + h * HD : cols + (h + 1) * HD].astype(F32)
             gate = silu(up)
             if s == 0:
                 att_ref[:, at] = (normed * gain * gate).astype(BF)
@@ -298,9 +326,9 @@
             hs = slice((p + h) * HD, (p + h + 1) * HD)
             acc_ref[:, hs] = total[h * cands : (h + 1) * cands, h * HD : (h + 1) * HD]
 
-    pre_slope = jnp.concatenate([r[:, 2 * cols : 3 * cols] for r in pack_refs], axis=0).astype(F32)
+    pre_slope = jnp.concatenate([r[:, 2 * cols : 3 * cols] for r in packs], axis=0).astype(F32)
     high, low = split(acc_ref[...] * (0.5 * SCALE) * pre_slope)
-    idx = jnp.concatenate([r[:, 3 * cols :] for r in pack_refs], axis=0).astype(F32)
+    idx = jnp.concatenate([r[:, 3 * cols :] for r in packs], axis=0).astype(F32)
     own, row = idx[:, :1], idx[:, 1:2]
     at_row = lax.broadcasted_iota(jnp.int32, (cands, ITEMS_DEV), 1).astype(F32)
     here = row == at_row
@@ -325,13 +353,6 @@
         at = pl.ds(pl.multiple_of((me_ref[0] ^ m) * height, height), height)
         part = dot_nt(table, w_ref[0, at, :]) + dot_nt(ups, w_ref[1, at, :])
         out_refs[m][...] = (part[:items, :] + part[items:, :]).astype(out_refs[m].dtype)
-
-
-def finish_kernel(*refs):
-    total = refs[0][...]
-    for r in refs[1:-1]:
-        total = total + r[...].astype(F32)
-    refs[-1][...] = total
 
 
 def whole_body(
@@ -356,33 +377,44 @@
     me = lax.axis_index("blk").astype(jnp.int32).reshape(1)
     head_me = lax.axis_index("heads").astype(jnp.int32).reshape(1)
     live = hist_mask.reshape(1, keys)
-    kstep = min(512, depth)
     width = min(512, keys)
 
     together = 2 if heads % 2 == 0 else 1
     pack_cols = 3 * cols + IDX_LANES
-    query, pack, up = pl.pallas_call(
+    query, pack, both, up = pl.pallas_call(
         project_kernel,
-        grid=(depth // kstep,),
-        in_specs=[
-            smem_spec(),
-            smem_spec(),
-            pl.BlockSpec((rows, kstep), lambda k: (0, k)),
-            pl.BlockSpec((2, kstep, cols), lambda k: (0, k, 0)),
-            pl.BlockSpec((rows, cols), lambda k: (0, 0)),
-        ],
-        out_specs=[vmem_spec()] * 3,
+        in_specs=[pl.BlockSpec(memory_space=HBM)] * 5,
+        out_specs=[vmem_spec()] * 4,
         out_shape=[
             pltpu.VMEM((rows, cols), BF),
             pltpu.VMEM((rows, pack_cols), BF),
+            pltpu.VMEM((rows, cols + pack_cols), BF),
             pltpu.VMEM((rows, cols), F32),
         ],
-        scratch_shapes=[pltpu.VMEM((rows, cols), F32)],
+        scratch_shapes=[
+            pltpu.VMEM((rows, depth), BF),
+            pltpu.VMEM((2, depth, cols), BF),
+            pltpu.VMEM((1, rows), jnp.int32),
+            pltpu.VMEM((1, rows), jnp.int32),
+            pltpu.SemaphoreType.DMA((2 * PARTS + 4,)),
+        ],
         compiler_params=pltpu.CompilerParams(vmem_limit_bytes=GRANT),
         name="project",
-    )(owner.reshape(rows), item_row, far(cand_feat), far(proj_weight), far(out_cot))
-    query_slots = gather_slots(query, "blk")
-    pack_slots = gather_slots(pack, "blk")
+    )(
+        far(cand_feat),
+        far(proj_weight),
+        far(out_cot),
+        far(owner.reshape(1, rows)),
+        far(item_row.reshape(1, rows)),
+    )
+    if slots == 4:
+        near_one = send(both, "blk", 1)
+        query_slots = [query, near_one] + [send(query, "blk", m) for m in (2, 3)]
+        second = send(pack, "blk", 2)
+        pack_slots = [pack, near_one, second, send(second, "blk", 1)]
+    else:
+        query_slots = gather_slots(query, "blk")
+        pack_slots = gather_slots(pack, "blk")
 
     hist_kv = load(hist_kv)
     weight = load(proj_weight)
@@ -428,7 +460,9 @@
         [(end, F32)] + [(end, BF)] * (wide - 1),
     )
     ends = scatter_slots(list(parts), "heads")
-    item_grad = call(finish_kernel, [], ends, [(end, F32)])[0]
+    item_grad = ends[0]
+    for e in ends[1:]:
+        item_grad = item_grad + e.astype(F32)
     return (attended, item_grad)
 
 

time: 58.8 us -> 53.4 us (0.908)
  starting transfers between devices: 23.4 us -> 18.5 us
  local copies, waits for them, and re-layouts: 6.7 us -> 4.75 us
  waiting for transfers between devices: 11.6 us -> 13.4 us
  Pallas kernels: 16.1 us -> 15.2 us
  other arithmetic: 0 us -> 0.66 us
    ppermute x15 -> x14, starting transfers between devices: 23.4 us -> 18.5 us  [send(): lax.ppermute(x, axis, [(j, j ^ m) for j in range(lax.axis_size(axis))])]
    unnamed x18 -> x13, local copies, waits for them, and re-layouts: 6.7 us -> 4.75 us
    ppermute x15 -> x14, waiting for transfers between devices: 11.6 us -> 13.4 us  [send(): lax.ppermute(x, axis, [(j, j ^ m) for j in range(lax.axis_size(axis))])]
    pallas_call x1, Pallas kernels: 3.57 us -> 2.63 us  [whole_body(): pl.pallas_call(project_kernel, in_specs=[pl.BlockSpec(memory_space=HBM)]...]
    add x0 -> x1, other arithmetic: none -> 0.66 us  [whole_body(): item_grad = item_grad + e.astype(F32)]
    pallas_call x5 -> x4, Pallas kernels: 8.11 us -> 8.09 us  [call(): pl.pallas_call(kernel, in_specs=[smem_spec()] * len(scalars) + [vmem_spec...]
  transfers between devices with their start and end apart: 15 -> 14, of which waited for: 5 -> 6; matrix products, arithmetic and copies ran while one was open for 1% -> 1% of each run, Pallas kernels for 15% -> 17%
where the time goes in v4:
time: 53.4 us; the launch traced here: 53.2 us
  starting transfers between devices  18.5 us (35%)
  Pallas kernels  15.2 us (28%)
  waiting for transfers between devices  13.4 us (25%)
  local copies, waits for them, and re-layouts  4.75 us (9%)
  between operations  0.74 us (1%)
  other arithmetic  0.66 us (1%)
    ppermute x14, starting transfers between devices, send(): lax.ppermute(x, axis, [(j, j ^ m) for j in range(lax.axis_size(axis))])  18.5 us
    ppermute x14, waiting for transfers between devices, send(): lax.ppermute(x, axis, [(j, j ^ m) for j in range(lax.axis_size(axis))])  13.4 us
    pallas_call x4, Pallas kernels, call(): pl.pallas_call(kernel, in_specs=[smem_spec()] * len(scalars) + [vmem_spec...  8.09 us
    unnamed x13, local copies, waits for them, and re-layouts  4.75 us
    pallas_call x2, Pallas kernels, load(): pl.pallas_call(load_kernel, in_specs=[pl.BlockSpec(memory_space=HBM)], ou...  4.45 us
    pallas_call x1, Pallas kernels, whole_body(): pl.pallas_call(project_kernel, in_specs=[pl.BlockSpec(memory_space=HBM)]...  2.63 us
  transfers between devices with their start and end apart: 14, of which 6 were waited for; matrix products, arithmetic and copies ran while one was open for 1% of the time, Pallas kernels for 17%

profile of v4, /device:TPU:0, one launch (start us, length us, event | category | flops | bytes accessed | tf_op | source)
XLA Modules:
  0.0 53.2 jit_solution(15070459529833817965)
XLA Ops:
  0.6 2.6 %project.1 = (bf16[32,512]{1,0:T(8,128)(2,1)S(1)}, bf16[32,1664]{1,0:T(8,128)(2,1)S(1)}, bf16[32,2176]{1,0:T(8,128)(2,1)S(1)}, f32[32,512]{1,0:T(8,128)S(1)}) custom-call(bf16[32,2048]{1,0:T(8,128)(2,1)} %x_hbm.1, bf16[2,2048,512]{2,1,0:T(8,128)(2,1)} %src_ref.3, bf16[32,512]{1,0:T(8,128)(2,1)} %cot_hbm.1, s32[1,32]{1,0:T(1,128)} %bitcast.7, s32[1,32]{1,0:T(1,128)} %bitcast.8), custom_call_target="tpu_custom_call" | custom-call | tf_op jit(solution)/shard_map/project/pallas_call | solution.py:384
  3.3 3.1 %collective-permute-start = (bf16[32,2176]{1,0:T(8,128)(2,1)S(1)}, bf16[32,2176]{1,0:T(8,128)(2,1)S(1)}, u32[]{:S(2)}, u32[]{:S(2)}) collective-permute-start(bf16[32,2176]{1,0:T(8,128)(2,1)S(1)} %get-tuple-element.21), channel_id=1, source_target_pairs={{0,4},{4,0},{8,12},{12,8},{1,5},{5,1},{9,13},{13,9},{2,6},{6,2},{1... | collective-permute-start | bytes 417800 | tf_op jit(solution)/shard_map/ppermute | solution.py:112
  6.4 2.6 %collective-permute-start.6 = (bf16[32,1664]{1,0:T(8,128)(2,1)S(1)}, bf16[32,1664]{1,0:T(8,128)(2,1)S(1)}, u32[]{:S(2)}, u32[]{:S(2)}) collective-permute-start(bf16[32,1664]{1,0:T(8,128)(2,1)S(1)} %get-tuple-element.25.refs_3_), channel_id=1, source_target_pairs={{0,8},{4,12},{8,0},{12,4},{1,9},{5,13},{9,1},{13,5},{2,10},{6,14},... | collective-permute-start | bytes 319496 | tf_op jit(solution)/shard_map/ppermute | solution.py:112
  9.0 1.9 %collective-permute-start.1 = (bf16[32,512]{1,0:T(8,128)(2,1)S(1)}, bf16[32,512]{1,0:T(8,128)(2,1)S(1)}, u32[]{:S(2)}, u32[]{:S(2)}) collective-permute-start(bf16[32,512]{1,0:T(8,128)(2,1)S(1)} %get-tuple-element.20.refs_0_), channel_id=1, source_target_pairs={{0,8},{4,12},{8,0},{12,4},{1,9},{5,13},{9,1},{13,5},{2,10},{6,14},... | collective-permute-start | bytes 98312 | tf_op jit(solution)/shard_map/ppermute | solution.py:112
  10.9 2.2 %shard_map.113.kv_ref = bf16[2,2048,512]{2,1,0:T(8,128)(2,1)S(1)} custom-call(bf16[2,2048,512]{2,1,0:T(8,128)(2,1)} %src_ref.2), custom_call_target="tpu_custom_call" | custom-call | tf_op jit(solution)/shard_map/pallas_call | solution.py:86
  13.2 2.5 %collective-permute-done.2.refs_3_ = bf16[32,512]{1,0:T(8,128)(2,1)S(1)} collective-permute-done((bf16[32,512]{1,0:T(8,128)(2,1)S(1)}, bf16[32,512]{1,0:T(8,128)(2,1)S(1)}, u32[]{:S(2)}, u32[]{:S(2)}) %collective-permute-start.2) | collective-permute-done | bytes 32800 | tf_op jit(solution)/shard_map/ppermute | solution.py:112
  15.7 1.3 %collective-permute-done.1.refs_2_ = bf16[32,512]{1,0:T(8,128)(2,1)S(1)} collective-permute-done((bf16[32,512]{1,0:T(8,128)(2,1)S(1)}, bf16[32,512]{1,0:T(8,128)(2,1)S(1)}, u32[]{:S(2)}, u32[]{:S(2)}) %collective-permute-start.1) | collective-permute-done | bytes 32800 | tf_op jit(solution)/shard_map/ppermute | solution.py:112
  17.0 2.1 %shard_map.114 = (f32[128,512]{1,0:T(8,128)S(1)}, bf16[128,512]{1,0:T(8,128)(2,1)S(1)}, bf16[128,512]{1,0:T(8,128)(2,1)S(1)}) custom-call(s32[1]{0:T(128)} %bitcast.me_ref, s32[2]{0:T(128)S(1)} %copy-done.3, s32[2]{0:T(128)S(1)} %copy-done.4, s32[1,2048]{1,0:T(1,128)S(1)} %bitcast.5, bf16[2,2048,512]{2,1,0:T(8,128)(2,1)S(1)} %shard_map.113.kv_ref, ...), custom_call_target="tpu_custom_call" | custom-call | tf_op jit(solution)/shard_map/pallas_call | solution.py:97
  19.1 2.4 %collective-permute-start.5 = (bf16[128,512]{1,0:T(8,128)(2,1)S(1)}, bf16[128,512]{1,0:T(8,128)(2,1)S(1)}, u32[]{:S(2)}, u32[]{:S(2)}) collective-permute-start(bf16[128,512]{1,0:T(8,128)(2,1)S(1)} %get-tuple-element.24), channel_id=1, source_target_pairs={{0,12},{4,8},{8,4},{12,0},{1,13},{5,9},{9,5},{13,1},{2,14},{6,10},... | collective-permute-start | bytes 393224 | tf_op jit(solution)/shard_map/ppermute | solution.py:112
  21.6 2.0 %collective-permute-start.3 = (bf16[128,512]{1,0:T(8,128)(2,1)S(1)}, bf16[128,512]{1,0:T(8,128)(2,1)S(1)}, u32[]{:S(2)}, u32[]{:S(2)}) collective-permute-start(bf16[128,512]{1,0:T(8,128)(2,1)S(1)} %get-tuple-element.24), channel_id=1, source_target_pairs={{0,4},{4,0},{8,12},{12,8},{1,5},{5,1},{9,13},{13,9},{2,6},{6,2},{1... | collective-permute-start | bytes 393224 | tf_op jit(solution)/shard_map/ppermute | solution.py:112
  23.6 2.4 %shard_map.115.slope_ref = bf16[512,2048]{1,0:T(8,128)(2,1)S(1)} custom-call(s32[1]{0:T(128)} %bitcast.me_ref, s32[2]{0:T(128)S(1)} %copy-done.3, s32[2]{0:T(128)S(1)} %copy-done.4, s32[1,2048]{1,0:T(1,128)S(1)} %bitcast.6, bf16[2,2048,512]{2,1,0:T(8,128)(2,1)S(1)} %shard_map.113.kv_ref, bf16[128,512]{1,0:T(8,128)(2,1)S(1)} %get-tuple-element.23.query_ref), custom_call_target="tpu_custom_call" | custom-call | tf_op jit(solution)/shard_map/pallas_call | solution.py:97
  26.0 6.1 %collective-permute-done.7.refs_6_ = bf16[32,1664]{1,0:T(8,128)(2,1)S(1)} collective-permute-done((bf16[32,1664]{1,0:T(8,128)(2,1)S(1)}, bf16[32,1664]{1,0:T(8,128)(2,1)S(1)}, u32[]{:S(2)}, u32[]{:S(2)}) %collective-permute-start.7) | collective-permute-done | bytes 106528 | tf_op jit(solution)/shard_map/ppermute | solution.py:112
  32.1 2.2 %shard_map.116 = (bf16[32,512]{1,0:T(8,128)(2,1)S(1)}, f32[48,512]{1,0:T(8,128)S(1)}, f32[48,512]{1,0:T(8,128)S(1)}, bf16[48,512]{1,0:T(8,128)(2,1)S(1)}, bf16[4...) custom-call(s32[1]{0:T(128)} %bitcast.me_ref, bf16[1,512]{1,0:T(2,128)(2,1)S(1)} %reshape.23.gain_ref, ...), custom_call_target="tpu_custom_call" | custom-call | tf_op jit(solution)/shard_map/pallas_call | solution.py:97
  34.4 1.8 %collective-permute-start.8 = (bf16[48,512]{1,0:T(8,128)(2,1)S(1)}, bf16[48,512]{1,0:T(8,128)(2,1)S(1)}, u32[]{:S(2)}, u32[]{:S(2)}) collective-permute-start(bf16[48,512]{1,0:T(8,128)(2,1)S(1)} %get-tuple-element.29), channel_id=1, source_target_pairs={{0,4},{4,0},{8,12},{12,8},{1,5},{5,1},{9,13},{13,9},{2,6},{6,2},{1... | collective-permute-start | bytes 147464 | tf_op jit(solution)/shard_map/ppermute | solution.py:112
  36.1 1.6 %collective-permute-start.9 = (bf16[48,512]{1,0:T(8,128)(2,1)S(1)}, bf16[48,512]{1,0:T(8,128)(2,1)S(1)}, u32[]{:S(2)}, u32[]{:S(2)}) collective-permute-start(bf16[48,512]{1,0:T(8,128)(2,1)S(1)} %get-tuple-element.30), channel_id=1, source_target_pairs={{0,8},{4,12},{8,0},{12,4},{1,9},{5,13},{9,1},{13,5},{2,10},{6,14},... | collective-permute-start | bytes 147464 | tf_op jit(solution)/shard_map/ppermute | solution.py:112
  37.8 1.1 %collective-permute-start.10 = (bf16[48,512]{1,0:T(8,128)(2,1)S(1)}, bf16[48,512]{1,0:T(8,128)(2,1)S(1)}, u32[]{:S(2)}, u32[]{:S(2)}) collective-permute-start(bf16[48,512]{1,0:T(8,128)(2,1)S(1)} %get-tuple-element.31), channel_id=1, source_target_pairs={{0,12},{4,8},{8,4},{12,0},{1,13},{5,9},{9,5},{13,1},{2,14},{6,10},... | collective-permute-start | bytes 147464 | tf_op jit(solution)/shard_map/ppermute | solution.py:112
  38.8 2.2 %shard_map.117.w_ref = bf16[2,2048,512]{2,1,0:T(8,128)(2,1)S(1)} custom-call(bf16[2,2048,512]{2,1,0:T(8,128)(2,1)} %src_ref.3), custom_call_target="tpu_custom_call" | custom-call | tf_op jit(solution)/shard_map/pallas_call | solution.py:86
  41.0 1.9 %copy-done = bf16[2,2048,512]{2,1,0:T(8,128)(2,1)} copy-done((bf16[2,2048,512]{2,1,0:T(8,128)(2,1)}, bf16[2,2048,512]{2,1,0:T(8,128)(2,1)S(1)}, u32[]{:S(2)}) %copy-start) | copy-done | bytes 4194328
  43.0 0.7 %collective-permute-done.10.refs_3_ = bf16[48,512]{1,0:T(8,128)(2,1)S(1)} collective-permute-done((bf16[48,512]{1,0:T(8,128)(2,1)S(1)}, bf16[48,512]{1,0:T(8,128)(2,1)S(1)}, u32[]{:S(2)}, u32[]{:S(2)}) %collective-permute-start.10) | collective-permute-done | bytes 49184 | tf_op jit(solution)/shard_map/ppermute | solution.py:112
  43.6 2.2 %copy-done.1 = bf16[2,2048,512]{2,1,0:T(8,128)(2,1)S(1)} copy-done((bf16[2,2048,512]{2,1,0:T(8,128)(2,1)S(1)}, bf16[2,2048,512]{2,1,0:T(8,128)(2,1)}, u32[]{:S(2)}) %copy-start.1) | copy-done | bytes 4194328
  45.8 1.4 %shard_map.118 = (f32[48,512]{1,0:T(8,128)S(1)}, bf16[48,512]{1,0:T(8,128)(2,1)S(1)}, bf16[48,512]{1,0:T(8,128)(2,1)S(1)}, bf16[48,512]{1,0:T(8,128)(2,1)S(1)}) custom-call(s32[1]{0:T(128)} %bitcast.4.me_ref, bf16[2,2048,512]{2,1,0:T(8,128)(2,1)S(1)} %copy-done.1, f32[48,512]{1,0:T(8,128)S(1)} %get-tuple-element.27.upt_ref, ...), custom_call_target="tpu_custom_call" | custom-call | tf_op jit(solution)/shard_map/pallas_call | solution.py:97
  47.3 1.5 %collective-permute-start.12 = (bf16[48,512]{1,0:T(8,128)(2,1)S(1)}, bf16[48,512]{1,0:T(8,128)(2,1)S(1)}, u32[]{:S(2)}, u32[]{:S(2)}) collective-permute-start(bf16[48,512]{1,0:T(8,128)(2,1)S(1)} %get-tuple-element.34), channel_id=1, source_target_pairs={{0,2},{1,3},{2,0},{3,1},{4,6},{5,7},{6,4},{7,5},{8,10},{9,11},{10,... | collective-permute-start | bytes 147464 | tf_op jit(solution)/shard_map/ppermute | solution.py:112
  49.8 1.7 %collective-permute-done.12 = bf16[48,512]{1,0:T(8,128)(2,1)S(1)} collective-permute-done((bf16[48,512]{1,0:T(8,128)(2,1)S(1)}, bf16[48,512]{1,0:T(8,128)(2,1)S(1)}, u32[]{:S(2)}, u32[]{:S(2)}) %collective-permute-start.12) | collective-permute-done | bytes 49184 | tf_op jit(solution)/shard_map/ppermute | solution.py:112
  51.5 1.1 %collective-permute-done.13 = bf16[48,512]{1,0:T(8,128)(2,1)S(1)} collective-permute-done((bf16[48,512]{1,0:T(8,128)(2,1)S(1)}, bf16[48,512]{1,0:T(8,128)(2,1)S(1)}, u32[]{:S(2)}, u32[]{:S(2)}) %collective-permute-start.13) | collective-permute-done | bytes 49184 | tf_op jit(solution)/shard_map/ppermute | solution.py:112
  (26 shorter events, 1.7 us)
Async XLA Ops:
  3.3 13.7 %collective-permute-start = (bf16[32,2176]{1,0:T(8,128)(2,1)S(1)}, bf16[32,2176]{1,0:T(8,128)(2,1)S(1)}, u32[]{:S(2)}, u32[]{:S(2)}) collective-permute-start(bf16[32,2176]{1,0:T(8,128)(2,1)S(1)} %get-tuple-element.21), channel_id=1, source_target_pairs={{0,4},{4,0},{8,12},{12,8},{1,5},{5,1},{9,13},{13,9},{2,6},{6,2},{1... | collective-permute-start | bytes 417800 | tf_op jit(solution)/shard_map/ppermute | solution.py:112
  6.4 17.2 %collective-permute-start.6 = (bf16[32,1664]{1,0:T(8,128)(2,1)S(1)}, bf16[32,1664]{1,0:T(8,128)(2,1)S(1)}, u32[]{:S(2)}, u32[]{:S(2)}) collective-permute-start(bf16[32,1664]{1,0:T(8,128)(2,1)S(1)} %get-tuple-element.25.refs_3_), channel_id=1, source_target_pairs={{0,8},{4,12},{8,0},{12,4},{1,9},{5,13},{9,1},{13,5},{2,10},{6,14},... | collective-permute-start | bytes 319496 | tf_op jit(solution)/shard_map/ppermute | solution.py:112
  9.0 6.7 %collective-permute-start.2 = (bf16[32,512]{1,0:T(8,128)(2,1)S(1)}, bf16[32,512]{1,0:T(8,128)(2,1)S(1)}, u32[]{:S(2)}, u32[]{:S(2)}) collective-permute-start(bf16[32,512]{1,0:T(8,128)(2,1)S(1)} %get-tuple-element.20.refs_0_), channel_id=1, source_target_pairs={{0,12},{4,8},{8,4},{12,0},{1,13},{5,9},{9,5},{13,1},{2,14},{6,10},... | collective-permute-start | bytes 98312 | tf_op jit(solution)/shard_map/ppermute | solution.py:112
  9.0 8.0 %collective-permute-start.1 = (bf16[32,512]{1,0:T(8,128)(2,1)S(1)}, bf16[32,512]{1,0:T(8,128)(2,1)S(1)}, u32[]{:S(2)}, u32[]{:S(2)}) collective-permute-start(bf16[32,512]{1,0:T(8,128)(2,1)S(1)} %get-tuple-element.20.refs_0_), channel_id=1, source_target_pairs={{0,8},{4,12},{8,0},{12,4},{1,9},{5,13},{9,1},{13,5},{2,10},{6,14},... | collective-permute-start | bytes 98312 | tf_op jit(solution)/shard_map/ppermute | solution.py:112
  10.9 6.1 %copy-start.2 = (s32[2048]{0:T(1024)S(1)}, s32[2048]{0:T(1024)}, u32[]{:S(2)}) copy-start(s32[2048]{0:T(1024)} %param.16) | copy-start | bytes 24580
  10.9 6.1 %copy-start.3 = (s32[2]{0:T(128)S(1)}, s32[2]{0:T(128)}, u32[]{:S(2)}) copy-start(s32[2]{0:T(128)} %counts_ref.3) | copy-start | bytes 28
  10.9 6.1 %copy-start.4 = (s32[2]{0:T(128)S(1)}, s32[2]{0:T(128)}, u32[]{:S(2)}) copy-start(s32[2]{0:T(128)} %lens_ref.3) | copy-start | bytes 28
  13.1 10.5 %copy-start.5 = (bf16[512]{0:T(512)(128)(2,1)S(1)}, bf16[512]{0:T(512)(128)(2,1)}, u32[]{:S(2)}) copy-start(bf16[512]{0:T(512)(128)(2,1)} %param.13) | copy-start | bytes 3076
  19.1 13.0 %collective-permute-start.5 = (bf16[128,512]{1,0:T(8,128)(2,1)S(1)}, bf16[128,512]{1,0:T(8,128)(2,1)S(1)}, u32[]{:S(2)}, u32[]{:S(2)}) collective-permute-start(bf16[128,512]{1,0:T(8,128)(2,1)S(1)} %get-tuple-element.24), channel_id=1, source_target_pairs={{0,12},{4,8},{8,4},{12,0},{1,13},{5,9},{9,5},{13,1},{2,14},{6,10},... | collective-permute-start | bytes 393224 | tf_op jit(solution)/shard_map/ppermute | solution.py:112
  21.5 10.6 %collective-permute-start.4 = (bf16[128,512]{1,0:T(8,128)(2,1)S(1)}, bf16[128,512]{1,0:T(8,128)(2,1)S(1)}, u32[]{:S(2)}, u32[]{:S(2)}) collective-permute-start(bf16[128,512]{1,0:T(8,128)(2,1)S(1)} %get-tuple-element.24), channel_id=1, source_target_pairs={{0,8},{4,12},{8,0},{12,4},{1,9},{5,13},{9,1},{13,5},{2,10},{6,14},... | collective-permute-start | bytes 393224 | tf_op jit(solution)/shard_map/ppermute | solution.py:112
  21.6 10.6 %collective-permute-start.3 = (bf16[128,512]{1,0:T(8,128)(2,1)S(1)}, bf16[128,512]{1,0:T(8,128)(2,1)S(1)}, u32[]{:S(2)}, u32[]{:S(2)}) collective-permute-start(bf16[128,512]{1,0:T(8,128)(2,1)S(1)} %get-tuple-element.24), channel_id=1, source_target_pairs={{0,4},{4,0},{8,12},{12,8},{1,5},{5,1},{9,13},{13,9},{2,6},{6,2},{1... | collective-permute-start | bytes 393224 | tf_op jit(solution)/shard_map/ppermute | solution.py:112
  23.6 8.5 %collective-permute-start.7 = (bf16[32,1664]{1,0:T(8,128)(2,1)S(1)}, bf16[32,1664]{1,0:T(8,128)(2,1)S(1)}, u32[]{:S(2)}, u32[]{:S(2)}) collective-permute-start(bf16[32,1664]{1,0:T(8,128)(2,1)S(1)} %collective-permute-done.6.refs_5_), channel_id=1, source_target_pairs={{0,4},{4,0},{8,12},{12,8},{1,5},{5,1},{9,13},{13,9},{2,6},{6,2},{1... | collective-permute-start | bytes 319496 | tf_op jit(solution)/shard_map/ppermute | solution.py:112
  34.4 8.6 %collective-permute-start.8 = (bf16[48,512]{1,0:T(8,128)(2,1)S(1)}, bf16[48,512]{1,0:T(8,128)(2,1)S(1)}, u32[]{:S(2)}, u32[]{:S(2)}) collective-permute-start(bf16[48,512]{1,0:T(8,128)(2,1)S(1)} %get-tuple-element.29), channel_id=1, source_target_pairs={{0,4},{4,0},{8,12},{12,8},{1,5},{5,1},{9,13},{13,9},{2,6},{6,2},{1... | collective-permute-start | bytes 147464 | tf_op jit(solution)/shard_map/ppermute | solution.py:112
  36.1 6.8 %collective-permute-start.9 = (bf16[48,512]{1,0:T(8,128)(2,1)S(1)}, bf16[48,512]{1,0:T(8,128)(2,1)S(1)}, u32[]{:S(2)}, u32[]{:S(2)}) collective-permute-start(bf16[48,512]{1,0:T(8,128)(2,1)S(1)} %get-tuple-element.30), channel_id=1, source_target_pairs={{0,8},{4,12},{8,0},{12,4},{1,9},{5,13},{9,1},{13,5},{2,10},{6,14},... | collective-permute-start | bytes 147464 | tf_op jit(solution)/shard_map/ppermute | solution.py:112
  37.8 5.9 %collective-permute-start.10 = (bf16[48,512]{1,0:T(8,128)(2,1)S(1)}, bf16[48,512]{1,0:T(8,128)(2,1)S(1)}, u32[]{:S(2)}, u32[]{:S(2)}) collective-permute-start(bf16[48,512]{1,0:T(8,128)(2,1)S(1)} %get-tuple-element.31), channel_id=1, source_target_pairs={{0,12},{4,8},{8,4},{12,0},{1,13},{5,9},{9,5},{13,1},{2,14},{6,10},... | collective-permute-start | bytes 147464 | tf_op jit(solution)/shard_map/ppermute | solution.py:112
  41.0 1.9 %copy-start = (bf16[2,2048,512]{2,1,0:T(8,128)(2,1)}, bf16[2,2048,512]{2,1,0:T(8,128)(2,1)S(1)}, u32[]{:S(2)}) copy-start(bf16[2,2048,512]{2,1,0:T(8,128)(2,1)S(1)} %shard_map.117.w_ref) | copy-start | bytes 12582916
  43.6 2.2 %copy-start.1 = (bf16[2,2048,512]{2,1,0:T(8,128)(2,1)S(1)}, bf16[2,2048,512]{2,1,0:T(8,128)(2,1)}, u32[]{:S(2)}) copy-start(bf16[2,2048,512]{2,1,0:T(8,128)(2,1)} %copy-done) | copy-start | bytes 12582916
  47.2 2.5 %collective-permute-start.11 = (bf16[48,512]{1,0:T(8,128)(2,1)S(1)}, bf16[48,512]{1,0:T(8,128)(2,1)S(1)}, u32[]{:S(2)}, u32[]{:S(2)}) collective-permute-start(bf16[48,512]{1,0:T(8,128)(2,1)S(1)} %get-tuple-element.33), channel_id=1, source_target_pairs={{0,1},{1,0},{2,3},{3,2},{4,5},{5,4},{6,7},{7,6},{8,9},{9,8},{10,11... | collective-permute-start | bytes 147464 | tf_op jit(solution)/shard_map/ppermute | solution.py:112
  47.3 4.2 %collective-permute-start.12 = (bf16[48,512]{1,0:T(8,128)(2,1)S(1)}, bf16[48,512]{1,0:T(8,128)(2,1)S(1)}, u32[]{:S(2)}, u32[]{:S(2)}) collective-permute-start(bf16[48,512]{1,0:T(8,128)(2,1)S(1)} %get-tuple-element.34), channel_id=1, source_target_pairs={{0,2},{1,3},{2,0},{3,1},{4,6},{5,7},{6,4},{7,5},{8,10},{9,11},{10,... | collective-permute-start | bytes 147464 | tf_op jit(solution)/shard_map/ppermute | solution.py:112
  48.8 3.7 %collective-permute-start.13 = (bf16[48,512]{1,0:T(8,128)(2,1)S(1)}, bf16[48,512]{1,0:T(8,128)(2,1)S(1)}, u32[]{:S(2)}, u32[]{:S(2)}) collective-permute-start(bf16[48,512]{1,0:T(8,128)(2,1)S(1)} %get-tuple-element.35), channel_id=1, source_target_pairs={{0,3},{1,2},{2,1},{3,0},{4,7},{5,6},{6,5},{7,4},{8,11},{9,10},{10,... | collective-permute-start | bytes 147464 | tf_op jit(solution)/shard_map/ppermute | solution.py:112

commit v5 on v4

--- a/solution.py
+++ b/solution.py
@@ -140,7 +140,7 @@
 
 
 def project_kernel(
-    x_hbm, w_hbm, cot_hbm, owner_hbm, row_hbm, query_ref, pack_ref, both_ref, up_ref,
+    x_hbm, w_hbm, cot_hbm, owner_hbm, row_hbm, query_ref, pack_ref, up_ref,
     x_ref, w_ref, owner_ref, row_ref, sems,
 ):
     rows, cols = up_ref.shape
@@ -181,8 +181,6 @@
     lane = lax.broadcasted_iota(jnp.int32, (rows, IDX_LANES), 1)
     idx = jnp.where(lane == 0, column(owner_ref), column(row_ref))
     pack_ref[:, 3 * cols :] = idx.astype(BF)
-    both_ref[:, :cols] = query_ref[...]
-    both_ref[:, cols:] = pack_ref[...]
 
 
 def user_of(pos, counts_ref):
@@ -230,13 +228,14 @@
     slots, together, width, me_ref, counts_ref, lens_ref, live_ref, kv_ref, *refs
 ):
     got_refs = refs[:slots]
-    sum_ref, low_ref, query_ref = refs[slots:]
+    sum_ref, low_ref, query_ref = refs[slots : slots + 3]
+    half_refs = refs[slots + 3 :]
     cands, cols = sum_ref.shape
     rows = cands // slots
     keys = kv_ref.shape[1]
     me = me_ref[0]
     for m in range(slots):
-        query_ref[m * rows : (m + 1) * rows, :] = got_refs[m][:, :cols]
+        query_ref[m * rows : (m + 1) * rows, :] = got_refs[m][...]
     for p in range(0, cols // HD, together):
         at = slice(p * HD, (p + together) * HD)
         query = diagonal(query_ref, p, together)
@@ -254,6 +253,9 @@
             hs = slice((p + h) * HD, (p + h + 1) * HD)
             sum_ref[:, hs] = part
             low_ref[:, hs] = part.astype(BF)
+            for i, ref in enumerate(half_refs):
+                size = ref.shape[0]
+                ref[:, hs] = part[i * size : (i + 1) * size, :].astype(BF)
 
 
 def slope_kernel(
@@ -276,7 +278,7 @@
             out_ref[p * cands : (p + together) * cands, ks] = jnp.where(keep, slope, 0.0).astype(BF)
 
 
-def backward_kernel(slots, together, width, me_ref, gain_ref, up_ref, sum_ref, kv_ref, slope_ref, *refs):
+def backward_kernel(pieces, slots, together, width, me_ref, gain_ref, up_ref, sum_ref, kv_ref, slope_ref, *refs):
     got, pack_refs = refs[: len(refs) - 2 * slots - 5], refs[len(refs) - 2 * slots - 5 :][:slots]
     refs = refs[len(refs) - slots - 5 :]
     att_ref, upt_ref = refs[:2]
@@ -291,9 +293,11 @@
     for s in range(slots):
         block = slice(s * rows, (s + 1) * rows)
         total = sum_ref[block, :]
-        for m in range(1, len(got) + 1):
+        for m in range(1, len(pieces) + 1):
             other = s ^ m
-            total = total + got[m - 1][other * rows : (other + 1) * rows, :].astype(F32)
+            ref = got[sum(pieces[: m - 1]) + other * pieces[m - 1] // slots]
+            start = other * rows % ref.shape[0]
+            total = total + ref[start : start + rows, :].astype(F32)
         for h in range(cols // HD):
             at = slice(h * HD, (h + 1) * HD)
             part = total[:, at]
@@ -381,14 +385,13 @@
 
     together = 2 if heads % 2 == 0 else 1
     pack_cols = 3 * cols + IDX_LANES
-    query, pack, both, up = pl.pallas_call(
+    query, pack, up = pl.pallas_call(
         project_kernel,
         in_specs=[pl.BlockSpec(memory_space=HBM)] * 5,
-        out_specs=[vmem_spec()] * 4,
+        out_specs=[vmem_spec()] * 3,
         out_shape=[
             pltpu.VMEM((rows, cols), BF),
             pltpu.VMEM((rows, pack_cols), BF),
-            pltpu.VMEM((rows, cols + pack_cols), BF),
             pltpu.VMEM((rows, cols), F32),
         ],
         scratch_shapes=[
@@ -408,10 +411,10 @@
         far(item_row.reshape(1, rows)),
     )
     if slots == 4:
-        near_one = send(both, "blk", 1)
-        query_slots = [query, near_one] + [send(query, "blk", m) for m in (2, 3)]
+        query_slots = gather_slots(query, "blk")
         second = send(pack, "blk", 2)
-        pack_slots = [pack, near_one, second, send(second, "blk", 1)]
+        pack_slots = [pack, send(pack, "blk", 1), second]
+        pack_slots.append(send(second, "blk", 1))
     else:
         query_slots = gather_slots(query, "blk")
         pack_slots = gather_slots(pack, "blk")
@@ -421,14 +424,20 @@
 
     every = (cands, cols)
     ranges = [me, cand_counts, hist_lens]
-    sums, low, queries = call(
+    outs = call(
         functools.partial(forward_kernel, slots, together, width),
         ranges,
         [live, hist_kv, *query_slots],
-        [(every, F32), (every, BF), (every, BF)],
-    )
-    if slots <= DIRECT:
-        got = [send(low, "blk", m) for m in range(1, slots)]
+        [(every, F32), (every, BF), (every, BF)] + [((cands // 2, cols), BF)] * (2 * (slots == 4)),
+    )
+    sums, low, queries = outs[:3]
+    if slots == 4:
+        ahead, behind = outs[3:]
+        second = [send(ahead, "blk", 2), send(behind, "blk", 2)]
+        third = [send(ahead, "blk", 3), send(second[1], "blk", 1)]
+        got = [[send(low, "blk", 1)], second, third]
+    elif slots <= DIRECT:
+        got = [[send(low, "blk", m)] for m in range(1, slots)]
     else:
         order = slot_order("blk")
         whole = lax.psum(sums.reshape(slots, rows, cols)[order], "blk")
@@ -443,9 +452,9 @@
 
     tile = (ITEMS_DEV, cols)
     outs = call(
-        functools.partial(backward_kernel, slots, together, width),
+        functools.partial(backward_kernel, [len(g) for g in got], slots, together, width),
         [me],
-        [norm_gain.reshape(1, cols), up, sums, hist_kv, slope, *got, *pack_slots],
+        [norm_gain.reshape(1, cols), up, sums, hist_kv, slope, *sum(got, []), *pack_slots],
         [((rows, cols), BF), (tile, F32), (tile, F32)] + [(tile, BF)] * (slots - 1),
         [(every, F32), (every, BF), (every, BF)],
     )

time: 53.4 us -> 56.6 us (1.060)
  starting transfers between devices: 18.5 us -> 24 us
  waiting for transfers between devices: 13.4 us -> 11.1 us
    ppermute x14 -> x17, starting transfers between devices: 18.5 us -> 24 us  [send(): lax.ppermute(x, axis, [(j, j ^ m) for j in range(lax.axis_size(axis))])]
    ppermute x14 -> x17, waiting for transfers between devices: 13.4 us -> 11.1 us  [send(): lax.ppermute(x, axis, [(j, j ^ m) for j in range(lax.axis_size(axis))])]
  transfers between devices with their start and end apart: 14 -> 17, of which waited for: 6 -> 8; matrix products, arithmetic and copies ran while one was open for 1% -> 1% of each run, Pallas kernels for 17% -> 16%
where the time goes in v5:
time: 56.6 us; the launch traced here: 56.5 us
  starting transfers between devices  24 us (42%)
  Pallas kernels  15.1 us (27%)
  waiting for transfers between devices  11.1 us (20%)
  local copies, waits for them, and re-layouts  4.75 us (8%)
  between operations  0.76 us (1%)
  other arithmetic  0.67 us (1%)
    ppermute x17, starting transfers between devices, send(): lax.ppermute(x, axis, [(j, j ^ m) for j in range(lax.axis_size(axis))])  24 us
    ppermute x17, waiting for transfers between devices, send(): lax.ppermute(x, axis, [(j, j ^ m) for j in range(lax.axis_size(axis))])  11.1 us
    pallas_call x4, Pallas kernels, call(): pl.pallas_call(kernel, in_specs=[smem_spec()] * len(scalars) + [vmem_spec...  8.08 us
    unnamed x13, local copies, waits for them, and re-layouts  4.75 us
    pallas_call x2, Pallas kernels, load(): pl.pallas_call(load_kernel, in_specs=[pl.BlockSpec(memory_space=HBM)], ou...  4.45 us
    pallas_call x1, Pallas kernels, whole_body(): pl.pallas_call(project_kernel, in_specs=[pl.BlockSpec(memory_space=HBM)]...  2.62 us
  transfers between devices with their start and end apart: 17, of which 8 were waited for; matrix products, arithmetic and copies ran while one was open for 1% of the time, Pallas kernels for 16%

profile of v5, /device:TPU:0, one launch (start us, length us, event | category | flops | bytes accessed | tf_op | source)
XLA Modules:
  0.0 56.5 jit_solution(7013208349737840324)
XLA Ops:
  0.6 2.6 %project.1 = (bf16[32,512]{1,0:T(8,128)(2,1)S(1)}, bf16[32,1664]{1,0:T(8,128)(2,1)S(1)}, f32[32,512]{1,0:T(8,128)S(1)}) custom-call(bf16[32,2048]{1,0:T(8,128)(2,1)} %x_hbm.1, bf16[2,2048,512]{2,1,0:T(8,128)(2,1)} %src_ref.3, bf16[32,512]{1,0:T(8,128)(2,1)} %cot_hbm.1, s32[1,32]{1,0:T(1,128)} %bitcast.7, s32[1,32]{1,0:T(1,128)} %bitcast.8), custom_call_target="tpu_custom_call" | custom-call | tf_op jit(solution)/shard_map/project/pallas_call | solution.py:388
  3.3 4.1 %collective-permute-start.9 = (bf16[32,1664]{1,0:T(8,128)(2,1)S(1)}, bf16[32,1664]{1,0:T(8,128)(2,1)S(1)}, u32[]{:S(2)}, u32[]{:S(2)}) collective-permute-start(bf16[32,1664]{1,0:T(8,128)(2,1)S(1)} %get-tuple-element.27.refs_5_), channel_id=1, source_target_pairs={{0,8},{4,12},{8,0},{12,4},{1,9},{5,13},{9,1},{13,5},{2,10},{6,14},... | collective-permute-start | bytes 319496 | tf_op jit(solution)/shard_map/ppermute | solution.py:112
  7.4 1.3 %collective-permute-start.2 = (bf16[32,512]{1,0:T(8,128)(2,1)S(1)}, bf16[32,512]{1,0:T(8,128)(2,1)S(1)}, u32[]{:S(2)}, u32[]{:S(2)}) collective-permute-start(bf16[32,512]{1,0:T(8,128)(2,1)S(1)} %get-tuple-element.21.refs_0_), channel_id=1, source_target_pairs={{0,12},{4,8},{8,4},{12,0},{1,13},{5,9},{9,5},{13,1},{2,14},{6,10},... | collective-permute-start | bytes 98312 | tf_op jit(solution)/shard_map/ppermute | solution.py:112
  8.7 1.7 %collective-permute-start.1 = (bf16[32,512]{1,0:T(8,128)(2,1)S(1)}, bf16[32,512]{1,0:T(8,128)(2,1)S(1)}, u32[]{:S(2)}, u32[]{:S(2)}) collective-permute-start(bf16[32,512]{1,0:T(8,128)(2,1)S(1)} %get-tuple-element.21.refs_0_), channel_id=1, source_target_pairs={{0,8},{4,12},{8,0},{12,4},{1,9},{5,13},{9,1},{13,5},{2,10},{6,14},... | collective-permute-start | bytes 98312 | tf_op jit(solution)/shard_map/ppermute | solution.py:112
  10.4 1.3 %collective-permute-start = (bf16[32,512]{1,0:T(8,128)(2,1)S(1)}, bf16[32,512]{1,0:T(8,128)(2,1)S(1)}, u32[]{:S(2)}, u32[]{:S(2)}) collective-permute-start(bf16[32,512]{1,0:T(8,128)(2,1)S(1)} %get-tuple-element.21.refs_0_), channel_id=1, source_target_pairs={{0,4},{4,0},{8,12},{12,8},{1,5},{5,1},{9,13},{13,9},{2,6},{6,2},{1... | collective-permute-start | bytes 98312 | tf_op jit(solution)/shard_map/ppermute | solution.py:112
  11.8 2.2 %shard_map.113.kv_ref = bf16[2,2048,512]{2,1,0:T(8,128)(2,1)S(1)} custom-call(bf16[2,2048,512]{2,1,0:T(8,128)(2,1)} %src_ref.2), custom_call_target="tpu_custom_call" | custom-call | tf_op jit(solution)/shard_map/pallas_call | solution.py:86
  14.1 1.4 %collective-permute-done.1.refs_2_ = bf16[32,512]{1,0:T(8,128)(2,1)S(1)} collective-permute-done((bf16[32,512]{1,0:T(8,128)(2,1)S(1)}, bf16[32,512]{1,0:T(8,128)(2,1)S(1)}, u32[]{:S(2)}, u32[]{:S(2)}) %collective-permute-start.1) | collective-permute-done | bytes 32800 | tf_op jit(solution)/shard_map/ppermute | solution.py:112
  15.5 2.1 %shard_map.114 = (f32[128,512]{1,0:T(8,128)S(1)}, bf16[128,512]{1,0:T(8,128)(2,1)S(1)}, bf16[128,512]{1,0:T(8,128)(2,1)S(1)}, bf16[64,512]{1,0:T(8,128)(2,1)S(1)}, bf16[64,512]{1,0:T(8,128)(2,1)S(1)}) custom-call(s32[1]{0:T(128)} %bitcast.me_ref, s32[2]{0:T(128)S(1)} %copy-done.3, s32[2]{0:T(128)S(1)} %copy-done.4, s32[1,2048]{1,0:T(1,128)S(1)} %bitcast.5, ...), custom_call_target="tpu_custom_call" | custom-call | tf_op jit(solution)/shard_map/pallas_call | solution.py:97
  17.6 2.1 %collective-permute-start.5 = (bf16[64,512]{1,0:T(8,128)(2,1)S(1)}, bf16[64,512]{1,0:T(8,128)(2,1)S(1)}, u32[]{:S(2)}, u32[]{:S(2)}) collective-permute-start(bf16[64,512]{1,0:T(8,128)(2,1)S(1)} %get-tuple-element.26), channel_id=1, source_target_pairs={{0,8},{4,12},{8,0},{12,4},{1,9},{5,13},{9,1},{13,5},{2,10},{6,14},... | collective-permute-start | bytes 196616 | tf_op jit(solution)/shard_map/ppermute | solution.py:112
  19.7 1.6 %collective-permute-start.6 = (bf16[64,512]{1,0:T(8,128)(2,1)S(1)}, bf16[64,512]{1,0:T(8,128)(2,1)S(1)}, u32[]{:S(2)}, u32[]{:S(2)}) collective-permute-start(bf16[64,512]{1,0:T(8,128)(2,1)S(1)} %get-tuple-element.25), channel_id=1, source_target_pairs={{0,12},{4,8},{8,4},{12,0},{1,13},{5,9},{9,5},{13,1},{2,14},{6,10},... | collective-permute-start | bytes 196616 | tf_op jit(solution)/shard_map/ppermute | solution.py:112
  21.8 1.5 %collective-permute-start.8 = (bf16[32,1664]{1,0:T(8,128)(2,1)S(1)}, bf16[32,1664]{1,0:T(8,128)(2,1)S(1)}, u32[]{:S(2)}, u32[]{:S(2)}) collective-permute-start(bf16[32,1664]{1,0:T(8,128)(2,1)S(1)} %get-tuple-element.27.refs_5_), channel_id=1, source_target_pairs={{0,4},{4,0},{8,12},{12,8},{1,5},{5,1},{9,13},{13,9},{2,6},{6,2},{1... | collective-permute-start | bytes 319496 | tf_op jit(solution)/shard_map/ppermute | solution.py:112
  23.8 2.1 %collective-permute-done.5.refs_2_ = bf16[64,512]{1,0:T(8,128)(2,1)S(1)} collective-permute-done((bf16[64,512]{1,0:T(8,128)(2,1)S(1)}, bf16[64,512]{1,0:T(8,128)(2,1)S(1)}, u32[]{:S(2)}, u32[]{:S(2)}) %collective-permute-start.5) | collective-permute-done | bytes 65568 | tf_op jit(solution)/shard_map/ppermute | solution.py:112
  26.5 2.7 %collective-permute-start.7 = (bf16[64,512]{1,0:T(8,128)(2,1)S(1)}, bf16[64,512]{1,0:T(8,128)(2,1)S(1)}, u32[]{:S(2)}, u32[]{:S(2)}) collective-permute-start(bf16[64,512]{1,0:T(8,128)(2,1)S(1)} %collective-permute-done.5.refs_2_), channel_id=1, source_target_pairs={{0,4},{4,0},{8,12},{12,8},{1,5},{5,1},{9,13},{13,9},{2,6},{6,2},{1... | collective-permute-start | bytes 196616 | tf_op jit(solution)/shard_map/ppermute | solution.py:112
  29.2 2.4 %shard_map.115.slope_ref = bf16[512,2048]{1,0:T(8,128)(2,1)S(1)} custom-call(s32[1]{0:T(128)} %bitcast.me_ref, s32[2]{0:T(128)S(1)} %copy-done.3, s32[2]{0:T(128)S(1)} %copy-done.4, s32[1,2048]{1,0:T(1,128)S(1)} %bitcast.6, bf16[2,2048,512]{2,1,0:T(8,128)(2,1)S(1)} %shard_map.113.kv_ref, bf16[128,512]{1,0:T(8,128)(2,1)S(1)} %get-tuple-element.23.query_ref), custom_call_target="tpu_custom_call" | custom-call | tf_op jit(solution)/shard_map/pallas_call | solution.py:97
  32.4 3.4 %collective-permute-done.7.refs_4_ = bf16[64,512]{1,0:T(8,128)(2,1)S(1)} collective-permute-done((bf16[64,512]{1,0:T(8,128)(2,1)S(1)}, bf16[64,512]{1,0:T(8,128)(2,1)S(1)}, u32[]{:S(2)}, u32[]{:S(2)}) %collective-permute-start.7) | collective-permute-done | bytes 65568 | tf_op jit(solution)/shard_map/ppermute | solution.py:112
  35.8 2.2 %shard_map.116 = (bf16[32,512]{1,0:T(8,128)(2,1)S(1)}, f32[48,512]{1,0:T(8,128)S(1)}, f32[48,512]{1,0:T(8,128)S(1)}, bf16[48,512]{1,0:T(8,128)(2,1)S(1)}, bf16[4...) custom-call(s32[1]{0:T(128)} %bitcast.me_ref, bf16[1,512]{1,0:T(2,128)(2,1)S(1)} %reshape.23.gain_ref, ...), custom_call_target="tpu_custom_call" | custom-call | tf_op jit(solution)/shard_map/pallas_call | solution.py:97
  38.1 2.9 %collective-permute-start.12 = (bf16[48,512]{1,0:T(8,128)(2,1)S(1)}, bf16[48,512]{1,0:T(8,128)(2,1)S(1)}, u32[]{:S(2)}, u32[]{:S(2)}) collective-permute-start(bf16[48,512]{1,0:T(8,128)(2,1)S(1)} %get-tuple-element.32), channel_id=1, source_target_pairs={{0,8},{4,12},{8,0},{12,4},{1,9},{5,13},{9,1},{13,5},{2,10},{6,14},... | collective-permute-start | bytes 147464 | tf_op jit(solution)/shard_map/ppermute | solution.py:112
  41.0 1.5 %collective-permute-start.13 = (bf16[48,512]{1,0:T(8,128)(2,1)S(1)}, bf16[48,512]{1,0:T(8,128)(2,1)S(1)}, u32[]{:S(2)}, u32[]{:S(2)}) collective-permute-start(bf16[48,512]{1,0:T(8,128)(2,1)S(1)} %get-tuple-element.33), channel_id=1, source_target_pairs={{0,12},{4,8},{8,4},{12,0},{1,13},{5,9},{9,5},{13,1},{2,14},{6,10},... | collective-permute-start | bytes 147464 | tf_op jit(solution)/shard_map/ppermute | solution.py:112
  42.5 2.2 %shard_map.117.w_ref = bf16[2,2048,512]{2,1,0:T(8,128)(2,1)S(1)} custom-call(bf16[2,2048,512]{2,1,0:T(8,128)(2,1)} %src_ref.3), custom_call_target="tpu_custom_call" | custom-call | tf_op jit(solution)/shard_map/pallas_call | solution.py:86
  44.7 1.9 %copy-done = bf16[2,2048,512]{2,1,0:T(8,128)(2,1)} copy-done((bf16[2,2048,512]{2,1,0:T(8,128)(2,1)}, bf16[2,2048,512]{2,1,0:T(8,128)(2,1)S(1)}, u32[]{:S(2)}) %copy-start) | copy-done | bytes 4194328
  46.9 2.2 %copy-done.1 = bf16[2,2048,512]{2,1,0:T(8,128)(2,1)S(1)} copy-done((bf16[2,2048,512]{2,1,0:T(8,128)(2,1)S(1)}, bf16[2,2048,512]{2,1,0:T(8,128)(2,1)}, u32[]{:S(2)}) %copy-start.1) | copy-done | bytes 4194328
  49.1 1.4 %shard_map.118 = (f32[48,512]{1,0:T(8,128)S(1)}, bf16[48,512]{1,0:T(8,128)(2,1)S(1)}, bf16[48,512]{1,0:T(8,128)(2,1)S(1)}, bf16[48,512]{1,0:T(8,128)(2,1)S(1)}) custom-call(s32[1]{0:T(128)} %bitcast.4.me_ref, bf16[2,2048,512]{2,1,0:T(8,128)(2,1)S(1)} %copy-done.1, f32[48,512]{1,0:T(8,128)S(1)} %get-tuple-element.29.upt_ref, ...), custom_call_target="tpu_custom_call" | custom-call | tf_op jit(solution)/shard_map/pallas_call | solution.py:97
  50.5 1.6 %collective-permute-start.15 = (bf16[48,512]{1,0:T(8,128)(2,1)S(1)}, bf16[48,512]{1,0:T(8,128)(2,1)S(1)}, u32[]{:S(2)}, u32[]{:S(2)}) collective-permute-start(bf16[48,512]{1,0:T(8,128)(2,1)S(1)} %get-tuple-element.36), channel_id=1, source_target_pairs={{0,2},{1,3},{2,0},{3,1},{4,6},{5,7},{6,4},{7,5},{8,10},{9,11},{10,... | collective-permute-start | bytes 147464 | tf_op jit(solution)/shard_map/ppermute | solution.py:112
  53.0 1.7 %collective-permute-done.15 = bf16[48,512]{1,0:T(8,128)(2,1)S(1)} collective-permute-done((bf16[48,512]{1,0:T(8,128)(2,1)S(1)}, bf16[48,512]{1,0:T(8,128)(2,1)S(1)}, u32[]{:S(2)}, u32[]{:S(2)}) %collective-permute-start.15) | collective-permute-done | bytes 49184 | tf_op jit(solution)/shard_map/ppermute | solution.py:112
  (32 shorter events, 5.5 us)
Async XLA Ops:
  3.3 20.1 %collective-permute-start.9 = (bf16[32,1664]{1,0:T(8,128)(2,1)S(1)}, bf16[32,1664]{1,0:T(8,128)(2,1)S(1)}, u32[]{:S(2)}, u32[]{:S(2)}) collective-permute-start(bf16[32,1664]{1,0:T(8,128)(2,1)S(1)} %get-tuple-element.27.refs_5_), channel_id=1, source_target_pairs={{0,8},{4,12},{8,0},{12,4},{1,9},{5,13},{9,1},{13,5},{2,10},{6,14},... | collective-permute-start | bytes 319496 | tf_op jit(solution)/shard_map/ppermute | solution.py:112
  7.4 6.7 %collective-permute-start.2 = (bf16[32,512]{1,0:T(8,128)(2,1)S(1)}, bf16[32,512]{1,0:T(8,128)(2,1)S(1)}, u32[]{:S(2)}, u32[]{:S(2)}) collective-permute-start(bf16[32,512]{1,0:T(8,128)(2,1)S(1)} %get-tuple-element.21.refs_0_), channel_id=1, source_target_pairs={{0,12},{4,8},{8,4},{12,0},{1,13},{5,9},{9,5},{13,1},{2,14},{6,10},... | collective-permute-start | bytes 98312 | tf_op jit(solution)/shard_map/ppermute | solution.py:112
  8.7 6.7 %collective-permute-start.1 = (bf16[32,512]{1,0:T(8,128)(2,1)S(1)}, bf16[32,512]{1,0:T(8,128)(2,1)S(1)}, u32[]{:S(2)}, u32[]{:S(2)}) collective-permute-start(bf16[32,512]{1,0:T(8,128)(2,1)S(1)} %get-tuple-element.21.refs_0_), channel_id=1, source_target_pairs={{0,8},{4,12},{8,0},{12,4},{1,9},{5,13},{9,1},{13,5},{2,10},{6,14},... | collective-permute-start | bytes 98312 | tf_op jit(solution)/shard_map/ppermute | solution.py:112
  10.4 5.0 %collective-permute-start = (bf16[32,512]{1,0:T(8,128)(2,1)S(1)}, bf16[32,512]{1,0:T(8,128)(2,1)S(1)}, u32[]{:S(2)}, u32[]{:S(2)}) collective-permute-start(bf16[32,512]{1,0:T(8,128)(2,1)S(1)} %get-tuple-element.21.refs_0_), channel_id=1, source_target_pairs={{0,4},{4,0},{8,12},{12,8},{1,5},{5,1},{9,13},{13,9},{2,6},{6,2},{1... | collective-permute-start | bytes 98312 | tf_op jit(solution)/shard_map/ppermute | solution.py:112
  11.8 3.7 %copy-start.2 = (s32[2048]{0:T(1024)S(1)}, s32[2048]{0:T(1024)}, u32[]{:S(2)}) copy-start(s32[2048]{0:T(1024)} %param.16) | copy-start | bytes 24580
  11.8 3.7 %copy-start.3 = (s32[2]{0:T(128)S(1)}, s32[2]{0:T(128)}, u32[]{:S(2)}) copy-start(s32[2]{0:T(128)} %counts_ref.3) | copy-start | bytes 28
  11.8 3.7 %copy-start.4 = (s32[2]{0:T(128)S(1)}, s32[2]{0:T(128)}, u32[]{:S(2)}) copy-start(s32[2]{0:T(128)} %lens_ref.3) | copy-start | bytes 28
  14.0 15.2 %copy-start.5 = (bf16[512]{0:T(512)(128)(2,1)S(1)}, bf16[512]{0:T(512)(128)(2,1)}, u32[]{:S(2)}) copy-start(bf16[512]{0:T(512)(128)(2,1)} %param.13) | copy-start | bytes 3076
  17.6 8.3 %collective-permute-start.5 = (bf16[64,512]{1,0:T(8,128)(2,1)S(1)}, bf16[64,512]{1,0:T(8,128)(2,1)S(1)}, u32[]{:S(2)}, u32[]{:S(2)}) collective-permute-start(bf16[64,512]{1,0:T(8,128)(2,1)S(1)} %get-tuple-element.26), channel_id=1, source_target_pairs={{0,8},{4,12},{8,0},{12,4},{1,9},{5,13},{9,1},{13,5},{2,10},{6,14},... | collective-permute-start | bytes 196616 | tf_op jit(solution)/shard_map/ppermute | solution.py:112
  19.7 6.8 %collective-permute-start.6 = (bf16[64,512]{1,0:T(8,128)(2,1)S(1)}, bf16[64,512]{1,0:T(8,128)(2,1)S(1)}, u32[]{:S(2)}, u32[]{:S(2)}) collective-permute-start(bf16[64,512]{1,0:T(8,128)(2,1)S(1)} %get-tuple-element.25), channel_id=1, source_target_pairs={{0,12},{4,8},{8,4},{12,0},{1,13},{5,9},{9,5},{13,1},{2,14},{6,10},... | collective-permute-start | bytes 196616 | tf_op jit(solution)/shard_map/ppermute | solution.py:112
  21.3 14.5 %collective-permute-start.3 = (bf16[128,512]{1,0:T(8,128)(2,1)S(1)}, bf16[128,512]{1,0:T(8,128)(2,1)S(1)}, u32[]{:S(2)}, u32[]{:S(2)}) collective-permute-start(bf16[128,512]{1,0:T(8,128)(2,1)S(1)} %get-tuple-element.24), channel_id=1, source_target_pairs={{0,4},{4,0},{8,12},{12,8},{1,5},{5,1},{9,13},{13,9},{2,6},{6,2},{1... | collective-permute-start | bytes 393224 | tf_op jit(solution)/shard_map/ppermute | solution.py:112
  21.8 10.6 %collective-permute-start.8 = (bf16[32,1664]{1,0:T(8,128)(2,1)S(1)}, bf16[32,1664]{1,0:T(8,128)(2,1)S(1)}, u32[]{:S(2)}, u32[]{:S(2)}) collective-permute-start(bf16[32,1664]{1,0:T(8,128)(2,1)S(1)} %get-tuple-element.27.refs_5_), channel_id=1, source_target_pairs={{0,4},{4,0},{8,12},{12,8},{1,5},{5,1},{9,13},{13,9},{2,6},{6,2},{1... | collective-permute-start | bytes 319496 | tf_op jit(solution)/shard_map/ppermute | solution.py:112
  23.3 12.5 %collective-permute-start.10 = (bf16[32,1664]{1,0:T(8,128)(2,1)S(1)}, bf16[32,1664]{1,0:T(8,128)(2,1)S(1)}, u32[]{:S(2)}, u32[]{:S(2)}) collective-permute-start(bf16[32,1664]{1,0:T(8,128)(2,1)S(1)} %collective-permute-done.9.refs_7_), channel_id=1, source_target_pairs={{0,4},{4,0},{8,12},{12,8},{1,5},{5,1},{9,13},{13,9},{2,6},{6,2},{1... | collective-permute-start | bytes 319496 | tf_op jit(solution)/shard_map/ppermute | solution.py:112
  25.9 6.5 %collective-permute-start.4 = (bf16[64,512]{1,0:T(8,128)(2,1)S(1)}, bf16[64,512]{1,0:T(8,128)(2,1)S(1)}, u32[]{:S(2)}, u32[]{:S(2)}) collective-permute-start(bf16[64,512]{1,0:T(8,128)(2,1)S(1)} %get-tuple-element.25), channel_id=1, source_target_pairs={{0,8},{4,12},{8,0},{12,4},{1,9},{5,13},{9,1},{13,5},{2,10},{6,14},... | collective-permute-start | bytes 196616 | tf_op jit(solution)/shard_map/ppermute | solution.py:112
  26.5 9.3 %collective-permute-start.7 = (bf16[64,512]{1,0:T(8,128)(2,1)S(1)}, bf16[64,512]{1,0:T(8,128)(2,1)S(1)}, u32[]{:S(2)}, u32[]{:S(2)}) collective-permute-start(bf16[64,512]{1,0:T(8,128)(2,1)S(1)} %collective-permute-done.5.refs_2_), channel_id=1, source_target_pairs={{0,4},{4,0},{8,12},{12,8},{1,5},{5,1},{9,13},{13,9},{2,6},{6,2},{1... | collective-permute-start | bytes 196616 | tf_op jit(solution)/shard_map/ppermute | solution.py:112
  38.0 8.6 %collective-permute-start.11 = (bf16[48,512]{1,0:T(8,128)(2,1)S(1)}, bf16[48,512]{1,0:T(8,128)(2,1)S(1)}, u32[]{:S(2)}, u32[]{:S(2)}) collective-permute-start(bf16[48,512]{1,0:T(8,128)(2,1)S(1)} %get-tuple-element.31), channel_id=1, source_target_pairs={{0,4},{4,0},{8,12},{12,8},{1,5},{5,1},{9,13},{13,9},{2,6},{6,2},{1... | collective-permute-start | bytes 147464 | tf_op jit(solution)/shard_map/ppermute | solution.py:112
  38.1 8.5 %collective-permute-start.12 = (bf16[48,512]{1,0:T(8,128)(2,1)S(1)}, bf16[48,512]{1,0:T(8,128)(2,1)S(1)}, u32[]{:S(2)}, u32[]{:S(2)}) collective-permute-start(bf16[48,512]{1,0:T(8,128)(2,1)S(1)} %get-tuple-element.32), channel_id=1, source_target_pairs={{0,8},{4,12},{8,0},{12,4},{1,9},{5,13},{9,1},{13,5},{2,10},{6,14},... | collective-permute-start | bytes 147464 | tf_op jit(solution)/shard_map/ppermute | solution.py:112
  41.0 5.9 %collective-permute-start.13 = (bf16[48,512]{1,0:T(8,128)(2,1)S(1)}, bf16[48,512]{1,0:T(8,128)(2,1)S(1)}, u32[]{:S(2)}, u32[]{:S(2)}) collective-permute-start(bf16[48,512]{1,0:T(8,128)(2,1)S(1)} %get-tuple-element.33), channel_id=1, source_target_pairs={{0,12},{4,8},{8,4},{12,0},{1,13},{5,9},{9,5},{13,1},{2,14},{6,10},... | collective-permute-start | bytes 147464 | tf_op jit(solution)/shard_map/ppermute | solution.py:112
  44.7 1.9 %copy-start = (bf16[2,2048,512]{2,1,0:T(8,128)(2,1)}, bf16[2,2048,512]{2,1,0:T(8,128)(2,1)S(1)}, u32[]{:S(2)}) copy-start(bf16[2,2048,512]{2,1,0:T(8,128)(2,1)S(1)} %shard_map.117.w_ref) | copy-start | bytes 12582916
  46.9 2.2 %copy-start.1 = (bf16[2,2048,512]{2,1,0:T(8,128)(2,1)S(1)}, bf16[2,2048,512]{2,1,0:T(8,128)(2,1)}, u32[]{:S(2)}) copy-start(bf16[2,2048,512]{2,1,0:T(8,128)(2,1)} %copy-done) | copy-start | bytes 12582916
  50.5 2.5 %collective-permute-start.14 = (bf16[48,512]{1,0:T(8,128)(2,1)S(1)}, bf16[48,512]{1,0:T(8,128)(2,1)S(1)}, u32[]{:S(2)}, u32[]{:S(2)}) collective-permute-start(bf16[48,512]{1,0:T(8,128)(2,1)S(1)} %get-tuple-element.35), channel_id=1, source_target_pairs={{0,1},{1,0},{2,3},{3,2},{4,5},{5,4},{6,7},{7,6},{8,9},{9,8},{10,11... | collective-permute-start | bytes 147464 | tf_op jit(solution)/shard_map/ppermute | solution.py:112
  50.5 4.2 %collective-permute-start.15 = (bf16[48,512]{1,0:T(8,128)(2,1)S(1)}, bf16[48,512]{1,0:T(8,128)(2,1)S(1)}, u32[]{:S(2)}, u32[]{:S(2)}) collective-permute-start(bf16[48,512]{1,0:T(8,128)(2,1)S(1)} %get-tuple-element.36), channel_id=1, source_target_pairs={{0,2},{1,3},{2,0},{3,1},{4,6},{5,7},{6,4},{7,5},{8,10},{9,11},{10,... | collective-permute-start | bytes 147464 | tf_op jit(solution)/shard_map/ppermute | solution.py:112
  52.1 3.7 %collective-permute-start.16 = (bf16[48,512]{1,0:T(8,128)(2,1)S(1)}, bf16[48,512]{1,0:T(8,128)(2,1)S(1)}, u32[]{:S(2)}, u32[]{:S(2)}) collective-permute-start(bf16[48,512]{1,0:T(8,128)(2,1)S(1)} %get-tuple-element.37), channel_id=1, source_target_pairs={{0,3},{1,2},{2,1},{3,0},{4,7},{5,6},{6,5},{7,4},{8,11},{9,10},{10,... | collective-permute-start | bytes 147464 | tf_op jit(solution)/shard_map/ppermute | solution.py:112
